TPU v7x, 256 devices: a whole 4x4x8 slice. The times are simulated.
256 devices in a mesh: dp: 16 (over z_hi, y), ctx: 16 (over x, z_lo, core).
Axes of the slice: x: 4, y: 4, z: 8 (z_hi: 4, z_lo: 2; z = z_hi * 2 + z_lo), core: 2. Of those that a mesh axis runs over, the one named last changes fastest.
Arguments:
- layer_input: bfloat16 [16, 2048, 4096], P('dp', 'ctx'), may hold values from -6 to 6
- query_states: bfloat16 [16, 2048, 512], P('dp', 'ctx'), may hold values from -9 to 9
- key_states: bfloat16 [16, 2048, 128], P('dp', 'ctx'), may hold values from -9 to 9
- value_states: bfloat16 [16, 2048, 128], P('dp', 'ctx'), may hold values from -6 to 6
- output_grad: bfloat16 [16, 2048, 512], P('dp', 'ctx'), may hold values from -6 to 6
- doc_lengths: int32 [16, 8], P('dp'), may hold values from 1 to 1024, 2048 in all within a row
Outputs:
- query_grad: bfloat16 [16, 2048, 512], P('dp', 'ctx')
- key_grad: bfloat16 [16, 2048, 128], P('dp', 'ctx')
- value_grad: bfloat16 [16, 2048, 128], P('dp', 'ctx')
- kv_weight_grad: float32 [4096, 256], P(('dp', 'ctx'))
All inputs are finite; a program needn't handle non-finite values.
Results may differ from a plain program's by a relative error of at most 0.014.
Values may be sent and summed in bfloat16 or wider, within the bound.
No kernel may reach another device: no remote copies, remote signals or barrier semaphores. Data moves between devices by JAX's collectives and lax.ppermute only.
A program may use at most 64 MiB of HBM per device.

v0:
```python
import math

import jax
import jax.numpy as jnp
from jax import lax
from jax.experimental import pallas as pl
from jax.experimental.pallas import tpu as pltpu
from jax.sharding import PartitionSpec as P


ROPE_BASE = 500000.0
NEG = -1e30
MIB = 1024 * 1024
B = 128
HEADS = 4
HALF = HEADS * 2 * B
NT = (((1,), (1,)), ((), ()))
TN = (((0,), (0,)), ((), ()))
NN = (((1,), (0,)), ((), ()))
SCALE = B**-0.5


VMEM = pl.BlockSpec(memory_space=pltpu.VMEM)
SMEM = pl.BlockSpec(memory_space=pltpu.SMEM)
HBM = pl.BlockSpec(memory_space=pltpu.HBM)


def dot(a, b, dims):
    return lax.dot_general(a, b, dims, preferred_element_type=jnp.float32)


def shape(dims, dtype):
    return jax.ShapeDtypeStruct(dims, dtype)


def rope_table(first):
    half = B // 2
    index = lax.broadcasted_iota(jnp.int32, (1, half), 1).astype(jnp.float32)
    frequency = jnp.exp(index * (-2.0 * math.log(ROPE_BASE) / B))
    position = first + lax.broadcasted_iota(jnp.int32, (B, 1), 0)
    angles = position.astype(jnp.float32) * frequency
    return jnp.concatenate([jnp.cos(angles), jnp.sin(angles)], 1)


def split_table(table):
    lane = lax.broadcasted_iota(jnp.int32, table.shape, 1)
    swapped = pltpu.roll(table, B // 2, 1)
    low = lane < B // 2
    return jnp.where(low, table, swapped), jnp.where(low, -swapped, table)


def rotated(u, cosine, sine):
    return u * cosine + pltpu.roll(u, B // 2, 1) * sine


def rows(index, size=B):
    return pl.ds(pl.multiple_of(index * size, size), size)


def prepare_kernel(
    where_ref, key_ref, value_ref, query_ref, grad_ref, x_ref, len_ref,
    kv_ref, qg_ref, x_out, len_out,
    key_s, query_s, sem,
):
    copies = [
        pltpu.make_async_copy(key_ref, key_s, sem.at[0]),
        pltpu.make_async_copy(query_ref, query_s, sem.at[1]),
        pltpu.make_async_copy(value_ref, kv_ref.at[:, B:], sem.at[2]),
        pltpu.make_async_copy(grad_ref, qg_ref.at[:, HEADS * B :], sem.at[3]),
        pltpu.make_async_copy(len_ref, len_out, sem.at[4]),
        pltpu.make_async_copy(x_ref, x_out, sem.at[5]),
    ]
    for copy in copies:
        copy.start()
    cosine, sine = split_table(rope_table(where_ref[0] * B))
    copies[0].wait()
    kv_ref[:, :B] = rotated(key_s[...].astype(jnp.float32), cosine, sine).astype(jnp.bfloat16)
    copies[1].wait()
    for h in range(HEADS):
        part = slice(h * B, (h + 1) * B)
        u = query_s[:, part].astype(jnp.float32)
        qg_ref[:, part] = rotated(u, cosine, sine).astype(jnp.bfloat16)
    for copy in copies[2:]:
        copy.wait()


def prepare(rank, keys, values, queries, grads, x, lengths):
    hbm = [pltpu.with_memory_space_constraint(a, pltpu.HBM) for a in (keys, values, queries, grads, x, lengths)]
    keys, values, queries, grads, x, lengths = hbm
    return pl.pallas_call(
        prepare_kernel,
        out_shape=(
            shape((B, 2 * B), jnp.bfloat16),
            shape((B, 2 * HEADS * B), jnp.bfloat16),
            shape((B, 4096), jnp.bfloat16),
            shape((1, 8), jnp.int32),
        ),
        in_specs=[SMEM] + [HBM] * 6,
        out_specs=(VMEM,) * 4,
        scratch_shapes=[
            pltpu.VMEM((B, B), jnp.bfloat16),
            pltpu.VMEM((B, HEADS * B), jnp.bfloat16),
            pltpu.SemaphoreType.DMA((6,)),
        ],
        compiler_params=pltpu.CompilerParams(vmem_limit_bytes=4 * MIB),
        name="prepare",
    )(rank, keys, values, queries, grads, x, lengths)


def slices_kernel(where_ref, x_ref, o0, o1, o2, o3, turned):
    slab = where_ref[0] // 4
    for i in range(32):
        turned[i * B : (i + 1) * B, :] = x_ref[:, i * B : (i + 1) * B].T
    for k, out in enumerate((o0, o1, o2, o3)):
        target = (slab + k) % 4
        for dp in range(16):
            out[dp * 64 : (dp + 1) * 64, :] = turned[rows(dp * 4 + target, 64), :]


def slices(rank, x):
    return pl.pallas_call(
        slices_kernel,
        out_shape=[shape((1024, B), jnp.bfloat16)] * 4,
        in_specs=[SMEM, VMEM],
        out_specs=[VMEM] * 4,
        scratch_shapes=[pltpu.VMEM((4096, B), jnp.bfloat16)],
        compiler_params=pltpu.CompilerParams(vmem_limit_bytes=8 * MIB),
        cost_estimate=pl.CostEstimate(flops=0, bytes_accessed=2_000_000, transcendentals=0),
        name="slices",
    )(rank, x)


def tables_kernel(where_ref, tab_ref):
    rank = where_ref[0]
    for k in range(4):
        tab_ref[k * B : (k + 1) * B, :] = rope_table(((rank // 4 - k + 4) % 4 * 4 + rank % 4) * B)


def tables(rank):
    return pl.pallas_call(
        tables_kernel,
        out_shape=shape((4 * B, B), jnp.float32),
        in_specs=[SMEM],
        out_specs=VMEM,
        compiler_params=pltpu.CompilerParams(vmem_limit_bytes=4 * MIB),
        cost_estimate=pl.CostEstimate(flops=2_000_000, bytes_accessed=260_000, transcendentals=64_000),
        name="tables",
    )(rank)


def document_start(len_ref, position):
    start = position * 0
    end = jnp.int32(0)
    for d in range(8):
        end = end + len_ref[0, d]
        start = jnp.where(position >= end, end, start)
    return start


def unit_needed(rank, b, half, lows):
    key_first = (rank - 4 * b) * B
    query_first = (rank // 4 * 4 + 2 * half) * B
    low = jnp.where(half == 0, lows[0], lows[1])
    return (key_first <= query_first + 2 * B - 1) & (key_first + B > low)


def half_lows(len_ref, rank):
    return [document_start(len_ref, (rank // 4 * 4 + 2 * half) * B) for half in range(2)]


def scores_kernel(
    where_ref, len_ref, kv0, kv1, kv2, qg0, qg1, qg2, qg3,
    p_ref, d_ref, q_ref, g_ref, stat_ref,
    k_s, v_s, m_s, l_s, w_s, start_s,
):
    rank = where_ref[0]
    slab, col = rank // 4, rank % 4
    lows = half_lows(len_ref, rank)
    for b, ref in enumerate((kv0, kv1, kv2)):
        k_s[b * B : (b + 1) * B, :] = ref[:, :B]
        v_s[b * B : (b + 1) * B, :] = ref[:, B:]
    for source, ref in enumerate((qg0, qg1, qg2, qg3)):
        column = col ^ source
        for h in range(HEADS):
            at = rows(column // 2 * 8 + h * 2 + column % 2)
            q_ref[at, :] = ref[:, h * B : (h + 1) * B]
            g_ref[at, :] = ref[:, (HEADS + h) * B : (HEADS + h + 1) * B]
    m_s[...] = jnp.full(m_s.shape, NEG, jnp.float32)
    l_s[...] = jnp.zeros(l_s.shape, jnp.float32)
    w_s[...] = jnp.zeros(w_s.shape, jnp.float32)
    start_s[...] = document_start(
        len_ref, slab * 4 * B + lax.broadcasted_iota(jnp.int32, (1, 4 * B), 1)
    )

    def first_pass(unit, carry):
        b, half = unit // 2, unit % 2

        @pl.when(unit_needed(rank, b, half, lows))
        def _():
            keys, queries = rows(b), rows(half, HALF)
            s = dot(k_s[keys, :], q_ref[queries, :], NT) * SCALE
            d_ref[keys, queries] = dot(v_s[keys, :], g_ref[queries, :], NT)
            key_pos = (rank - 4 * b) * B + lax.broadcasted_iota(jnp.int32, (B, 2 * B), 0)
            query_pos = (slab * 4 + 2 * half) * B + lax.broadcasted_iota(jnp.int32, (1, 2 * B), 1)
            allowed = (key_pos <= query_pos) & (key_pos >= start_s[:, rows(half, 2 * B)])
            for h in range(HEADS):
                lanes = rows(half * HEADS + h, 2 * B)
                part = jnp.where(allowed, s[:, h * 2 * B : (h + 1) * 2 * B], NEG)
                p_ref[keys, lanes] = part
                m_s[:, lanes] = jnp.maximum(m_s[:, lanes], jnp.max(part.reshape(16, 8, 2 * B), axis=0))

        return carry

    lax.fori_loop(0, 6, first_pass, 0)
    top = jnp.max(m_s[...], axis=0, keepdims=True)
    stat_ref[0:1, :] = top

    def second_pass(unit, carry):
        b, half = unit // 2, unit % 2

        @pl.when(unit_needed(rank, b, half, lows))
        def _():
            keys, queries = rows(b), rows(half, HALF)
            p = jnp.exp(p_ref[keys, queries] - stat_ref[0:1, queries])
            p_ref[keys, queries] = p
            l_s[:, queries] += jnp.sum(p.reshape(16, 8, HALF), axis=0)
            w_s[:, queries] += jnp.sum((p * d_ref[keys, queries]).reshape(16, 8, HALF), axis=0)

        return carry

    lax.fori_loop(0, 6, second_pass, 0)
    stat_ref[1:2, :] = jnp.sum(l_s[...], axis=0, keepdims=True)
    stat_ref[2:3, :] = jnp.sum(w_s[...], axis=0, keepdims=True)
    stat_ref[3:4, :] = jnp.zeros((1, 2 * HALF), jnp.float32)


def scores(rank, lengths, kvs, qgs):
    wide = (3 * B, 2 * HALF)
    return pl.pallas_call(
        scores_kernel,
        out_shape=(
            shape(wide, jnp.float32),
            shape(wide, jnp.float32),
            shape((2 * HALF, B), jnp.bfloat16),
            shape((2 * HALF, B), jnp.bfloat16),
            shape((4, 2 * HALF), jnp.float32),
        ),
        in_specs=[SMEM, SMEM] + [VMEM] * 7,
        out_specs=(VMEM,) * 5,
        scratch_shapes=[
            pltpu.VMEM((3 * B, B), jnp.bfloat16),
            pltpu.VMEM((3 * B, B), jnp.bfloat16),
            pltpu.VMEM((8, 2 * HALF), jnp.float32),
            pltpu.VMEM((8, 2 * HALF), jnp.float32),
            pltpu.VMEM((8, 2 * HALF), jnp.float32),
            pltpu.VMEM((1, 4 * B), jnp.int32),
        ],
        compiler_params=pltpu.CompilerParams(vmem_limit_bytes=20 * MIB),
        cost_estimate=pl.CostEstimate(flops=400_000_000, bytes_accessed=8_000_000, transcendentals=790_000),
        name="scores",
    )(rank, lengths, *kvs, *qgs)


def gradients_kernel(
    where_ref, len_ref, kv0, kv1, kv2, p_ref, d_ref, q_ref, g_ref, st0, st1, st2, st3,
    keep_ref, send_ref, dq_keep_ref, dq_send_ref,
    k_s, dq_s, f_s, delta_s,
):
    rank = where_ref[0]
    lows = half_lows(len_ref, rank)
    for b, ref in enumerate((kv0, kv1, kv2)):
        k_s[b * B : (b + 1) * B, :] = ref[:, :B]
    tops = [st[0:1, :] for st in (st0, st1, st2, st3)]
    top = jnp.maximum(jnp.maximum(tops[0], tops[1]), jnp.maximum(tops[2], tops[3]))
    factors = [jnp.exp(t - top) for t in tops]
    total = sum(st[1:2, :] * f for st, f in zip((st0, st1, st2, st3), factors))
    weighted = sum(st[2:3, :] * f for st, f in zip((st0, st1, st2, st3), factors))
    inverse = 1.0 / total
    f_s[...] = factors[0] * inverse
    delta_s[...] = weighted * inverse
    keep_ref[...] = jnp.zeros(keep_ref.shape, jnp.float32)
    dq_s[...] = jnp.zeros(dq_s.shape, jnp.float32)

    def one_pass(unit, carry):
        b, half = unit // 2, unit % 2

        @pl.when(unit_needed(rank, b, half, lows))
        def _():
            keys, queries = rows(b), rows(half, HALF)
            p = p_ref[keys, queries] * f_s[:, queries]
            ds = (p * (d_ref[keys, queries] - delta_s[:, queries])).astype(jnp.bfloat16)
            keep_ref[keys, B:] += dot(p.astype(jnp.bfloat16), g_ref[queries, :], NN)
            keep_ref[keys, :B] += dot(ds, q_ref[queries, :], NN) * SCALE
            dq_s[:, queries] += dot(k_s[keys, :], ds, TN)

        return carry

    lax.fori_loop(0, 6, one_pass, 0)
    send_ref[...] = keep_ref[...].astype(jnp.bfloat16)
    z = rank % 4 // 2
    dq_keep_ref[...] = dq_s[:, rows(z, HALF)]
    dq_send_ref[...] = dq_s[:, rows(1 - z, HALF)].astype(jnp.bfloat16)


def gradients(rank, lengths, kvs, p, d, q, g, stats):
    return pl.pallas_call(
        gradients_kernel,
        out_shape=(
            shape((3 * B, 2 * B), jnp.float32),
            shape((3 * B, 2 * B), jnp.bfloat16),
            shape((B, HALF), jnp.float32),
            shape((B, HALF), jnp.bfloat16),
        ),
        in_specs=[SMEM, SMEM] + [VMEM] * 11,
        out_specs=(VMEM,) * 4,
        scratch_shapes=[
            pltpu.VMEM((3 * B, B), jnp.bfloat16),
            pltpu.VMEM((B, 2 * HALF), jnp.float32),
            pltpu.VMEM((1, 2 * HALF), jnp.float32),
            pltpu.VMEM((1, 2 * HALF), jnp.float32),
        ],
        compiler_params=pltpu.CompilerParams(vmem_limit_bytes=20 * MIB),
        cost_estimate=pl.CostEstimate(flops=600_000_000, bytes_accessed=8_000_000, transcendentals=8_000),
        name="gradients",
    )(rank, lengths, *kvs, p, d, q, g, *stats)


def query_fold_kernel(where_ref, keep_ref, arrived_ref, mine_ref, send_ref):
    core = where_ref[0] % 2
    for h in range(HEADS):
        part = slice(h * B, (h + 1) * B)
        mine, other = rows(h * 2 + core), rows(h * 2 + 1 - core)
        mine_ref[:, part] = keep_ref[:, mine] + arrived_ref[:, mine].astype(jnp.float32)
        both = keep_ref[:, other] + arrived_ref[:, other].astype(jnp.float32)
        send_ref[:, part] = both.astype(jnp.bfloat16)


def query_fold(rank, keep, arrived):
    return pl.pallas_call(
        query_fold_kernel,
        out_shape=(shape((B, HEADS * B), jnp.float32), shape((B, HEADS * B), jnp.bfloat16)),
        in_specs=[SMEM, VMEM, VMEM],
        out_specs=(VMEM, VMEM),
        compiler_params=pltpu.CompilerParams(vmem_limit_bytes=4 * MIB),
        cost_estimate=pl.CostEstimate(flops=300_000, bytes_accessed=1_200_000, transcendentals=0),
        name="query_fold",
    )(rank, keep, arrived)


def query_end_kernel(mine_ref, arrived_ref, tab_ref, out_ref):
    cosine, sine = split_table(tab_ref[:B, :])
    for h in range(HEADS):
        part = slice(h * B, (h + 1) * B)
        u = (mine_ref[:, part] + arrived_ref[:, part].astype(jnp.float32)).T * SCALE
        out_ref[:, part] = rotated(u, cosine, -sine).astype(jnp.bfloat16)


def query_end(mine, arrived, table):
    return pl.pallas_call(
        query_end_kernel,
        out_shape=shape((B, HEADS * B), jnp.bfloat16),
        in_specs=[VMEM, VMEM, VMEM],
        out_specs=VMEM,
        compiler_params=pltpu.CompilerParams(vmem_limit_bytes=4 * MIB),
        cost_estimate=pl.CostEstimate(flops=300_000, bytes_accessed=700_000, transcendentals=0),
        name="query_end",
    )(mine, arrived, table)


def weight_kernel(
    where_ref, keep_ref, r1, r2, r3, tab_ref, x0, x1, x2, x3,
    key_ref, value_ref, own_ref, send_ref, acc,
):
    core = where_ref[0] % 2
    parts = (keep_ref, r1, r2, r3)
    total = None
    for k, x in enumerate((x0, x1, x2, x3)):
        grad = None
        for b in range(3):
            part = parts[(k - b) % 4][b * B : (b + 1) * B, :].astype(jnp.float32)
            grad = part if grad is None else grad + part
        cosine, sine = split_table(tab_ref[k * B : (k + 1) * B, :])
        key = rotated(grad[:, :B], cosine, -sine).astype(jnp.bfloat16)
        value = grad[:, B:].astype(jnp.bfloat16)
        if k == 0:
            key_ref[...] = key
            value_ref[...] = value
        term = dot(x[...], jnp.concatenate([key, value], 1), NN)
        total = term if total is None else total + term
    acc[...] = total
    for i in range(32):
        part = slice(i * 16, (i + 1) * 16)
        own_ref[part, :] = acc[rows(i * 2 + core, 16), :]
        send_ref[part, :] = acc[rows(i * 2 + 1 - core, 16), :].astype(jnp.bfloat16)


def weight_part(rank, keep, arrived, table, xs):
    return pl.pallas_call(
        weight_kernel,
        out_shape=(
            shape((B, B), jnp.bfloat16),
            shape((B, B), jnp.bfloat16),
            shape((512, 256), jnp.float32),
            shape((512, 256), jnp.bfloat16),
        ),
        in_specs=[SMEM] + [VMEM] * 9,
        out_specs=(VMEM,) * 4,
        scratch_shapes=[pltpu.VMEM((1024, 256), jnp.float32)],
        compiler_params=pltpu.CompilerParams(vmem_limit_bytes=12 * MIB),
        cost_estimate=pl.CostEstimate(flops=268_000_000, bytes_accessed=3_000_000, transcendentals=0),
        name="weight",
    )(rank, keep, *arrived, table, *xs)


def compute(layer_input, query_states, key_states, value_states, output_grad, doc_lengths):
    where = lax.axis_index("ctx").astype(jnp.int32)[None]

    def permute(array, pairs):
        return lax.ppermute(array, "ctx", pairs)

    def around(array, slabs):
        return permute(array, [(i, (i + 4 * slabs) % 16) for i in range(16)])

    def swap(array, bits):
        return permute(array, [(i, i ^ bits) for i in range(16)])

    kv, qg, x, lengths = prepare(
        where,
        key_states[0],
        value_states[0],
        query_states[0],
        output_grad[0],
        layer_input[0],
        doc_lengths,
    )
    qg_z = swap(qg, 2)
    kvs = [kv, around(kv, 1), around(kv, 2)]
    qg_c = swap(qg, 1)
    qg_cz = swap(qg_z, 1)

    xs = slices(where, x)
    xs = [xs[0]] + [around(xs[k], k) for k in (1, 2, 3)]

    p, d, q, g, stat = scores(where, lengths, kvs, (qg, qg_c, qg_z, qg_cz))
    stats = [stat] + [swap(stat, bits) for bits in (1, 2, 3)]
    table = tables(where)
    keep, send, dq_keep, dq_send = gradients(where, lengths, kvs, p, d, q, g, stats)

    arrived = [around(send, k) for k in (1, 2, 3)]
    dq_z = swap(dq_send, 2)
    dq_mine, dq_send = query_fold(where, dq_keep, dq_z)
    dq_c = swap(dq_send, 1)
    query_grad = query_end(dq_mine, dq_c, table)

    key_grad, value_grad, own, send = weight_part(where, keep, arrived, table, xs)
    own = own + swap(send, 1).astype(jnp.float32)
    blocks = own.astype(jnp.bfloat16).reshape(32, 16, 256)
    groups = [
        [dp * 16 + slab * 4 + z * 2 + core for dp in range(16) for z in range(2)]
        for slab in range(4)
        for core in range(2)
    ]
    blocks = lax.all_to_all(
        blocks, ("dp", "ctx"), split_axis=0, concat_axis=0, tiled=True, axis_index_groups=groups
    )
    weight_grad = jnp.sum(blocks.astype(jnp.float32), axis=0)
    return query_grad[None], key_grad[None], value_grad[None], weight_grad


def solution(mesh):
    split = P("dp", "ctx", None)
    return jax.shard_map(
        compute,
        mesh=mesh,
        in_specs=(split,) * 5 + (P("dp", None),),
        out_specs=(split, split, split, P(("dp", "ctx"), None)),
        check_vma=False,
    )
```

profile of v0, /device:TPU:1, one launch (start us, length us, event | category | flops | bytes accessed | tf_op | source)
XLA Modules:
  0.0 82.5 jit_solution(34637182749788890)
XLA Ops:
  0.6 1.5 %prepare.1 = (bf16[128,256]{1,0:T(8,128)(2,1)S(1)}, bf16[128,1024]{1,0:T(8,128)(2,1)S(1)}, bf16[128,4096]{1,0:T(8,128)(2,1)S(1)}, s32[1,8]{1,0:T(1,128)S(1)}) custom-call(s32[1]{0:T(128)} %bitcast.where_ref, bf16[128,128]{1,0:T(8,128)(2,1)} %bitcast.14, bf16[128,128]{1,0:T(8,128)(2,1)} %bitcast.15, bf16[128,512]{1,0:T(8,128)(2,1)} %bitcast.11, ...), custom_call_target="tpu_custom_call" | custom-call | tf_op jit(solution)/shard_map/prepare/pallas_call | solution.py:90
  2.1 2.5 %collective-permute-start.3 = (bf16[128,1024]{1,0:T(8,128)(2,1)S(1)}, bf16[128,1024]{1,0:T(8,128)(2,1)S(1)}, u32[]{:S(2)}, u32[]{:S(2)}) collective-permute-start(bf16[128,1024]{1,0:T(8,128)(2,1)S(1)} %get-tuple-element.29.qg0), channel_id=1, source_target_pairs={{0,2},{1,3},{2,0},{3,1},{4,6},{5,7},{6,4},{7,5},{8,10},{9,11},{10,... | collective-permute-start | bytes 786440 | tf_op jit(solution)/shard_map/ppermute | solution.py:419
  4.7 1.0 %collective-permute-start.2 = (bf16[128,1024]{1,0:T(8,128)(2,1)S(1)}, bf16[128,1024]{1,0:T(8,128)(2,1)S(1)}, u32[]{:S(2)}, u32[]{:S(2)}) collective-permute-start(bf16[128,1024]{1,0:T(8,128)(2,1)S(1)} %get-tuple-element.29.qg0), channel_id=1, source_target_pairs={{0,1},{1,0},{2,3},{3,2},{4,5},{5,4},{6,7},{7,6},{8,9},{9,8},{10,11... | collective-permute-start | bytes 786440 | tf_op jit(solution)/shard_map/ppermute | solution.py:419
  5.6 4.0 %collective-permute-done.3.qg2 = bf16[128,1024]{1,0:T(8,128)(2,1)S(1)} collective-permute-done((bf16[128,1024]{1,0:T(8,128)(2,1)S(1)}, bf16[128,1024]{1,0:T(8,128)(2,1)S(1)}, u32[]{:S(2)}, u32[]{:S(2)}) %collective-permute-start.3) | collective-permute-done | bytes 262176 | tf_op jit(solution)/shard_map/ppermute | solution.py:419
  9.7 2.3 %collective-permute-start.4 = (bf16[128,1024]{1,0:T(8,128)(2,1)S(1)}, bf16[128,1024]{1,0:T(8,128)(2,1)S(1)}, u32[]{:S(2)}, u32[]{:S(2)}) collective-permute-start(bf16[128,1024]{1,0:T(8,128)(2,1)S(1)} %collective-permute-done.3.qg2), channel_id=1, source_target_pairs={{0,1},{1,0},{2,3},{3,2},{4,5},{5,4},{6,7},{7,6},{8,9},{9,8},{10,11... | collective-permute-start | bytes 786440 | tf_op jit(solution)/shard_map/ppermute | solution.py:419
  11.9 0.4 slices.1
  12.3 1.3 %collective-permute-start.13 = (bf16[1024,128]{1,0:T(8,128)(2,1)S(1)}, bf16[1024,128]{1,0:T(8,128)(2,1)S(1)}, u32[]{:S(2)}, u32[]{:S(2)}) collective-permute-start(bf16[1024,128]{1,0:T(8,128)(2,1)S(1)} %get-tuple-element.43), channel_id=1, source_target_pairs={{0,4},{1,5},{2,6},{3,7},{4,8},{5,9},{6,10},{7,11},{8,12},{9,13},{1... | collective-permute-start | bytes 786440 | tf_op jit(solution)/shard_map/ppermute | solution.py:419
  13.6 1.2 %collective-permute-start = (bf16[128,256]{1,0:T(8,128)(2,1)S(1)}, bf16[128,256]{1,0:T(8,128)(2,1)S(1)}, u32[]{:S(2)}, u32[]{:S(2)}) collective-permute-start(bf16[128,256]{1,0:T(8,128)(2,1)S(1)} %get-tuple-element.28.kv0), channel_id=1, source_target_pairs={{0,4},{1,5},{2,6},{3,7},{4,8},{5,9},{6,10},{7,11},{8,12},{9,13},{1... | collective-permute-start | bytes 196616 | tf_op jit(solution)/shard_map/ppermute | solution.py:419
  14.8 1.4 %collective-permute-start.1 = (bf16[128,256]{1,0:T(8,128)(2,1)S(1)}, bf16[128,256]{1,0:T(8,128)(2,1)S(1)}, u32[]{:S(2)}, u32[]{:S(2)}) collective-permute-start(bf16[128,256]{1,0:T(8,128)(2,1)S(1)} %get-tuple-element.28.kv0), channel_id=1, source_target_pairs={{0,8},{1,9},{2,10},{3,11},{4,12},{5,13},{6,14},{7,15},{8,0},{9,1},... | collective-permute-start | bytes 196616 | tf_op jit(solution)/shard_map/ppermute | solution.py:419
  16.3 6.6 %collective-permute-done.kv1 = bf16[128,256]{1,0:T(8,128)(2,1)S(1)} collective-permute-done((bf16[128,256]{1,0:T(8,128)(2,1)S(1)}, bf16[128,256]{1,0:T(8,128)(2,1)S(1)}, u32[]{:S(2)}, u32[]{:S(2)}) %collective-permute-start) | collective-permute-done | bytes 65568 | tf_op jit(solution)/shard_map/ppermute | solution.py:419
  22.9 2.4 %collective-permute-done.1.kv2 = bf16[128,256]{1,0:T(8,128)(2,1)S(1)} collective-permute-done((bf16[128,256]{1,0:T(8,128)(2,1)S(1)}, bf16[128,256]{1,0:T(8,128)(2,1)S(1)}, u32[]{:S(2)}, u32[]{:S(2)}) %collective-permute-start.1) | collective-permute-done | bytes 65568 | tf_op jit(solution)/shard_map/ppermute | solution.py:419
  25.3 0.0 collective-permute-done.2.qg1
  25.3 0.0 collective-permute-done.4.qg3
  25.3 1.9 %scores.1 = (f32[384,2048]{1,0:T(8,128)S(1)}, f32[384,2048]{1,0:T(8,128)S(1)}, bf16[2048,128]{1,0:T(8,128)(2,1)S(1)}, bf16[2048,128]{1,0:T(8,128)(2,1)S(1)}, f32[4,2048]{1,0:T(4,128)S(1)}) custom-call(s32[1]{0:T(128)} %bitcast.where_ref, s32[1,8]{1,0:T(1,128)S(1)} %get-tuple-element.27.len_ref, bf16[128,256]{1,0:T(8,128)(2,1)S(1)} %get-tuple-element.28.kv0, ...), custom_call_target="tpu_custom_call" | custom-call | flops 400000000 | bytes 8000000 | tf_op jit(solution)/shard_map/scores/pallas_call | solution.py:239
  27.2 0.5 collective-permute-start.5
  27.7 1.5 %collective-permute-start.6 = (f32[4,2048]{1,0:T(4,128)S(1)}, f32[4,2048]{1,0:T(4,128)S(1)}, u32[]{:S(2)}, u32[]{:S(2)}) collective-permute-start(f32[4,2048]{1,0:T(4,128)S(1)} %get-tuple-element.34.st0), channel_id=1, source_target_pairs={{0,2},{1,3},{2,0},{3,1},{4,6},{5,7},{6,4},{7,5},{8,10},{9,11},{10,... | collective-permute-start | bytes 98312 | tf_op jit(solution)/shard_map/ppermute | solution.py:419
  29.2 0.3 collective-permute-start.7
  29.5 1.4 %collective-permute-start.14 = (bf16[1024,128]{1,0:T(8,128)(2,1)S(1)}, bf16[1024,128]{1,0:T(8,128)(2,1)S(1)}, u32[]{:S(2)}, u32[]{:S(2)}) collective-permute-start(bf16[1024,128]{1,0:T(8,128)(2,1)S(1)} %get-tuple-element.44), channel_id=1, source_target_pairs={{0,8},{1,9},{2,10},{3,11},{4,12},{5,13},{6,14},{7,15},{8,0},{9,1},... | collective-permute-start | bytes 786440 | tf_op jit(solution)/shard_map/ppermute | solution.py:419
  30.8 0.0 collective-permute-done.5.st1
  30.8 0.0 collective-permute-start.15
  30.8 0.0 collective-permute-done.6.st2
  30.9 1.7 %collective-permute-done.7.st3 = f32[4,2048]{1,0:T(4,128)S(1)} collective-permute-done((f32[4,2048]{1,0:T(4,128)S(1)}, f32[4,2048]{1,0:T(4,128)S(1)}, u32[]{:S(2)}, u32[]{:S(2)}) %collective-permute-start.7) | collective-permute-done | bytes 32800 | tf_op jit(solution)/shard_map/ppermute | solution.py:419
  32.6 1.6 %gradients.1 = (f32[384,256]{1,0:T(8,128)S(1)}, bf16[384,256]{1,0:T(8,128)(2,1)S(1)}, f32[128,1024]{1,0:T(8,128)S(1)}, bf16[128,1024]{1,0:T(8,128)(2,1)S(1)}) custom-call(s32[1]{0:T(128)} %bitcast.where_ref, s32[1,8]{1,0:T(1,128)S(1)} %get-tuple-element.27.len_ref, bf16[128,256]{1,0:T(8,128)(2,1)S(1)} %get-tuple-element.28.kv0, ...), custom_call_target="tpu_custom_call" | custom-call | flops 600000000 | bytes 8000000 | tf_op jit(solution)/shard_map/gradients/pallas_call | solution.py:306
  34.2 0.6 collective-permute-start.10
  34.7 1.8 %collective-permute-start.11 = (bf16[384,256]{1,0:T(8,128)(2,1)S(1)}, bf16[384,256]{1,0:T(8,128)(2,1)S(1)}, u32[]{:S(2)}, u32[]{:S(2)}) collective-permute-start(bf16[384,256]{1,0:T(8,128)(2,1)S(1)} %get-tuple-element.40), channel_id=1, source_target_pairs={{0,8},{1,9},{2,10},{3,11},{4,12},{5,13},{6,14},{7,15},{8,0},{9,1},... | collective-permute-start | bytes 589832 | tf_op jit(solution)/shard_map/ppermute | solution.py:419
  36.5 0.0 collective-permute-done.13.x1
  36.5 2.0 %collective-permute-start.12 = (bf16[384,256]{1,0:T(8,128)(2,1)S(1)}, bf16[384,256]{1,0:T(8,128)(2,1)S(1)}, u32[]{:S(2)}, u32[]{:S(2)}) collective-permute-start(bf16[384,256]{1,0:T(8,128)(2,1)S(1)} %get-tuple-element.40), channel_id=1, source_target_pairs={{0,12},{1,13},{2,14},{3,15},{4,0},{5,1},{6,2},{7,3},{8,4},{9,5},{1... | collective-permute-start | bytes 589832 | tf_op jit(solution)/shard_map/ppermute | solution.py:419
  38.5 1.0 %tables.1.tab_ref = f32[512,128]{1,0:T(8,128)S(1)} custom-call(s32[1]{0:T(128)} %bitcast.where_ref), custom_call_target="tpu_custom_call" | custom-call | flops 2000000 | bytes 260000 | tf_op jit(solution)/shard_map/tables/pallas_call | solution.py:140
  39.5 0.0 collective-permute-done.14.x2
  39.5 1.9 %collective-permute-done.15.x3 = bf16[1024,128]{1,0:T(8,128)(2,1)S(1)} collective-permute-done((bf16[1024,128]{1,0:T(8,128)(2,1)S(1)}, bf16[1024,128]{1,0:T(8,128)(2,1)S(1)}, u32[]{:S(2)}, u32[]{:S(2)}) %collective-permute-start.15) | collective-permute-done | bytes 262176 | tf_op jit(solution)/shard_map/ppermute | solution.py:419
  41.4 2.6 %collective-permute-done.10.r1 = bf16[384,256]{1,0:T(8,128)(2,1)S(1)} collective-permute-done((bf16[384,256]{1,0:T(8,128)(2,1)S(1)}, bf16[384,256]{1,0:T(8,128)(2,1)S(1)}, u32[]{:S(2)}, u32[]{:S(2)}) %collective-permute-start.10) | collective-permute-done | bytes 196640 | tf_op jit(solution)/shard_map/ppermute | solution.py:419
  44.0 3.1 %collective-permute-done.11.r2 = bf16[384,256]{1,0:T(8,128)(2,1)S(1)} collective-permute-done((bf16[384,256]{1,0:T(8,128)(2,1)S(1)}, bf16[384,256]{1,0:T(8,128)(2,1)S(1)}, u32[]{:S(2)}, u32[]{:S(2)}) %collective-permute-start.11) | collective-permute-done | bytes 196640 | tf_op jit(solution)/shard_map/ppermute | solution.py:419
  47.1 2.7 %collective-permute-done.12.r3 = bf16[384,256]{1,0:T(8,128)(2,1)S(1)} collective-permute-done((bf16[384,256]{1,0:T(8,128)(2,1)S(1)}, bf16[384,256]{1,0:T(8,128)(2,1)S(1)}, u32[]{:S(2)}, u32[]{:S(2)}) %collective-permute-start.12) | collective-permute-done | bytes 196640 | tf_op jit(solution)/shard_map/ppermute | solution.py:419
  49.9 1.5 %weight.1 = (bf16[128,128]{1,0:T(8,128)(2,1)}, bf16[128,128]{1,0:T(8,128)(2,1)}, f32[512,256]{1,0:T(8,128)S(1)}, bf16[512,256]{1,0:T(8,128)(2,1)S(1)}) custom-call(s32[1]{0:T(128)} %bitcast.where_ref, f32[384,256]{1,0:T(8,128)S(1)} %get-tuple-element.39.keep_ref, bf16[384,256]{1,0:T(8,128)(2,1)S(1)} %collective-permute-done.10.r1, ...), custom_call_target="tpu_custom_call" | custom-call | flops 268000000 | bytes 3000000 | tf_op jit(solution)/shard_map/weight/pallas_call | solution.py:398
  51.4 1.2 %collective-permute-start.16 = (bf16[512,256]{1,0:T(8,128)(2,1)S(1)}, bf16[512,256]{1,0:T(8,128)(2,1)S(1)}, u32[]{:S(2)}, u32[]{:S(2)}) collective-permute-start(bf16[512,256]{1,0:T(8,128)(2,1)S(1)} %get-tuple-element.49), channel_id=1, source_target_pairs={{0,1},{1,0},{2,3},{3,2},{4,5},{5,4},{6,7},{7,6},{8,9},{9,8},{10,11... | collective-permute-start | bytes 786440 | tf_op jit(solution)/shard_map/ppermute | solution.py:419
  52.6 1.2 %collective-permute-done.16 = bf16[512,256]{1,0:T(8,128)(2,1)S(1)} collective-permute-done((bf16[512,256]{1,0:T(8,128)(2,1)S(1)}, bf16[512,256]{1,0:T(8,128)(2,1)S(1)}, u32[]{:S(2)}, u32[]{:S(2)}) %collective-permute-start.16) | collective-permute-done | bytes 262176 | tf_op jit(solution)/shard_map/ppermute | solution.py:419
  53.7 0.8 add_convert_fusion
  54.5 11.0 %all-to-all-start = ((bf16[32,16,256]{2,1,0:T(8,128)(2,1)}), bf16[32,16,256]{2,1,0:T(8,128)(2,1)S(1)}, u32[]{:S(2)}, u32[]{:S(2)}) async-start(bf16[32,16,256]{2,1,0:T(8,128)(2,1)} %bitcast.9), calls=%async_computation | async-start | bytes 524288 | tf_op jit(solution)/shard_map/all_to_all | solution.py:463
  65.5 1.3 %collective-permute-start.8 = (bf16[128,1024]{1,0:T(8,128)(2,1)S(1)}, bf16[128,1024]{1,0:T(8,128)(2,1)S(1)}, u32[]{:S(2)}, u32[]{:S(2)}) collective-permute-start(bf16[128,1024]{1,0:T(8,128)(2,1)S(1)} %get-tuple-element.36), channel_id=1, source_target_pairs={{0,2},{1,3},{2,0},{3,1},{4,6},{5,7},{6,4},{7,5},{8,10},{9,11},{10,... | collective-permute-start | bytes 786440 | tf_op jit(solution)/shard_map/ppermute | solution.py:419
  66.9 11.4 %collective-permute-done.8.arrived_ref = bf16[128,1024]{1,0:T(8,128)(2,1)S(1)} collective-permute-done((bf16[128,1024]{1,0:T(8,128)(2,1)S(1)}, bf16[128,1024]{1,0:T(8,128)(2,1)S(1)}, u32[]{:S(2)}, u32[]{:S(2)}) %collective-permute-start.8) | collective-permute-done | bytes 262176 | tf_op jit(solution)/shard_map/ppermute | solution.py:419
  78.3 0.1 query_fold.1
  78.4 1.6 %collective-permute-start.9 = (bf16[128,512]{1,0:T(8,128)(2,1)S(1)}, bf16[128,512]{1,0:T(8,128)(2,1)S(1)}, u32[]{:S(2)}, u32[]{:S(2)}) collective-permute-start(bf16[128,512]{1,0:T(8,128)(2,1)S(1)} %get-tuple-element.38), channel_id=1, source_target_pairs={{0,1},{1,0},{2,3},{3,2},{4,5},{5,4},{6,7},{7,6},{8,9},{9,8},{10,11... | collective-permute-start | bytes 393224 | tf_op jit(solution)/shard_map/ppermute | solution.py:419
  80.0 1.0 %collective-permute-done.9.arrived_ref = bf16[128,512]{1,0:T(8,128)(2,1)S(1)} collective-permute-done((bf16[128,512]{1,0:T(8,128)(2,1)S(1)}, bf16[128,512]{1,0:T(8,128)(2,1)S(1)}, u32[]{:S(2)}, u32[]{:S(2)}) %collective-permute-start.9) | collective-permute-done | bytes 131104 | tf_op jit(solution)/shard_map/ppermute | solution.py:419
  81.0 0.9 %query_end.1 = bf16[128,512]{1,0:T(8,128)(2,1)} custom-call(f32[128,512]{1,0:T(8,128)S(1)} %get-tuple-element.37.mine_ref, bf16[128,512]{1,0:T(8,128)(2,1)S(1)} %collective-permute-done.9.arrived_ref, f32[512,128]{1,0:T(8,128)S(1)} %tables.1.tab_ref), custom_call_target="tpu_custom_call" | custom-call | flops 300000 | bytes 700000 | tf_op jit(solution)/shard_map/query_end/pallas_call | solution.py:359
  81.9 0.0 all-to-all-done
  81.9 0.7 convert_reduce_fusion
Async XLA Ops:
  2.1 7.5 %collective-permute-start.3 = (bf16[128,1024]{1,0:T(8,128)(2,1)S(1)}, bf16[128,1024]{1,0:T(8,128)(2,1)S(1)}, u32[]{:S(2)}, u32[]{:S(2)}) collective-permute-start(bf16[128,1024]{1,0:T(8,128)(2,1)S(1)} %get-tuple-element.29.qg0), channel_id=1, source_target_pairs={{0,2},{1,3},{2,0},{3,1},{4,6},{5,7},{6,4},{7,5},{8,10},{9,11},{10,... | collective-permute-start | bytes 786440 | tf_op jit(solution)/shard_map/ppermute | solution.py:419
  4.7 20.6 %collective-permute-start.2 = (bf16[128,1024]{1,0:T(8,128)(2,1)S(1)}, bf16[128,1024]{1,0:T(8,128)(2,1)S(1)}, u32[]{:S(2)}, u32[]{:S(2)}) collective-permute-start(bf16[128,1024]{1,0:T(8,128)(2,1)S(1)} %get-tuple-element.29.qg0), channel_id=1, source_target_pairs={{0,1},{1,0},{2,3},{3,2},{4,5},{5,4},{6,7},{7,6},{8,9},{9,8},{10,11... | collective-permute-start | bytes 786440 | tf_op jit(solution)/shard_map/ppermute | solution.py:419
  9.7 15.6 %collective-permute-start.4 = (bf16[128,1024]{1,0:T(8,128)(2,1)S(1)}, bf16[128,1024]{1,0:T(8,128)(2,1)S(1)}, u32[]{:S(2)}, u32[]{:S(2)}) collective-permute-start(bf16[128,1024]{1,0:T(8,128)(2,1)S(1)} %collective-permute-done.3.qg2), channel_id=1, source_target_pairs={{0,1},{1,0},{2,3},{3,2},{4,5},{5,4},{6,7},{7,6},{8,9},{9,8},{10,11... | collective-permute-start | bytes 786440 | tf_op jit(solution)/shard_map/ppermute | solution.py:419
  12.3 24.2 %collective-permute-start.13 = (bf16[1024,128]{1,0:T(8,128)(2,1)S(1)}, bf16[1024,128]{1,0:T(8,128)(2,1)S(1)}, u32[]{:S(2)}, u32[]{:S(2)}) collective-permute-start(bf16[1024,128]{1,0:T(8,128)(2,1)S(1)} %get-tuple-element.43), channel_id=1, source_target_pairs={{0,4},{1,5},{2,6},{3,7},{4,8},{5,9},{6,10},{7,11},{8,12},{9,13},{1... | collective-permute-start | bytes 786440 | tf_op jit(solution)/shard_map/ppermute | solution.py:419
  13.6 9.3 %collective-permute-start = (bf16[128,256]{1,0:T(8,128)(2,1)S(1)}, bf16[128,256]{1,0:T(8,128)(2,1)S(1)}, u32[]{:S(2)}, u32[]{:S(2)}) collective-permute-start(bf16[128,256]{1,0:T(8,128)(2,1)S(1)} %get-tuple-element.28.kv0), channel_id=1, source_target_pairs={{0,4},{1,5},{2,6},{3,7},{4,8},{5,9},{6,10},{7,11},{8,12},{9,13},{1... | collective-permute-start | bytes 196616 | tf_op jit(solution)/shard_map/ppermute | solution.py:419
  14.8 10.4 %collective-permute-start.1 = (bf16[128,256]{1,0:T(8,128)(2,1)S(1)}, bf16[128,256]{1,0:T(8,128)(2,1)S(1)}, u32[]{:S(2)}, u32[]{:S(2)}) collective-permute-start(bf16[128,256]{1,0:T(8,128)(2,1)S(1)} %get-tuple-element.28.kv0), channel_id=1, source_target_pairs={{0,8},{1,9},{2,10},{3,11},{4,12},{5,13},{6,14},{7,15},{8,0},{9,1},... | collective-permute-start | bytes 196616 | tf_op jit(solution)/shard_map/ppermute | solution.py:419
  27.2 3.6 %collective-permute-start.5 = (f32[4,2048]{1,0:T(4,128)S(1)}, f32[4,2048]{1,0:T(4,128)S(1)}, u32[]{:S(2)}, u32[]{:S(2)}) collective-permute-start(f32[4,2048]{1,0:T(4,128)S(1)} %get-tuple-element.34.st0), channel_id=1, source_target_pairs={{0,1},{1,0},{2,3},{3,2},{4,5},{5,4},{6,7},{7,6},{8,9},{9,8},{10,11... | collective-permute-start | bytes 98312 | tf_op jit(solution)/shard_map/ppermute | solution.py:419
  27.7 3.1 %collective-permute-start.6 = (f32[4,2048]{1,0:T(4,128)S(1)}, f32[4,2048]{1,0:T(4,128)S(1)}, u32[]{:S(2)}, u32[]{:S(2)}) collective-permute-start(f32[4,2048]{1,0:T(4,128)S(1)} %get-tuple-element.34.st0), channel_id=1, source_target_pairs={{0,2},{1,3},{2,0},{3,1},{4,6},{5,7},{6,4},{7,5},{8,10},{9,11},{10,... | collective-permute-start | bytes 98312 | tf_op jit(solution)/shard_map/ppermute | solution.py:419
  29.2 3.4 %collective-permute-start.7 = (f32[4,2048]{1,0:T(4,128)S(1)}, f32[4,2048]{1,0:T(4,128)S(1)}, u32[]{:S(2)}, u32[]{:S(2)}) collective-permute-start(f32[4,2048]{1,0:T(4,128)S(1)} %get-tuple-element.34.st0), channel_id=1, source_target_pairs={{0,3},{1,2},{2,1},{3,0},{4,7},{5,6},{6,5},{7,4},{8,11},{9,10},{10,... | collective-permute-start | bytes 98312 | tf_op jit(solution)/shard_map/ppermute | solution.py:419
  29.5 10.1 %collective-permute-start.14 = (bf16[1024,128]{1,0:T(8,128)(2,1)S(1)}, bf16[1024,128]{1,0:T(8,128)(2,1)S(1)}, u32[]{:S(2)}, u32[]{:S(2)}) collective-permute-start(bf16[1024,128]{1,0:T(8,128)(2,1)S(1)} %get-tuple-element.44), channel_id=1, source_target_pairs={{0,8},{1,9},{2,10},{3,11},{4,12},{5,13},{6,14},{7,15},{8,0},{9,1},... | collective-permute-start | bytes 786440 | tf_op jit(solution)/shard_map/ppermute | solution.py:419
  30.8 10.6 %collective-permute-start.15 = (bf16[1024,128]{1,0:T(8,128)(2,1)S(1)}, bf16[1024,128]{1,0:T(8,128)(2,1)S(1)}, u32[]{:S(2)}, u32[]{:S(2)}) collective-permute-start(bf16[1024,128]{1,0:T(8,128)(2,1)S(1)} %get-tuple-element.45), channel_id=1, source_target_pairs={{0,12},{1,13},{2,14},{3,15},{4,0},{5,1},{6,2},{7,3},{8,4},{9,5},{1... | collective-permute-start | bytes 786440 | tf_op jit(solution)/shard_map/ppermute | solution.py:419
  34.2 9.8 %collective-permute-start.10 = (bf16[384,256]{1,0:T(8,128)(2,1)S(1)}, bf16[384,256]{1,0:T(8,128)(2,1)S(1)}, u32[]{:S(2)}, u32[]{:S(2)}) collective-permute-start(bf16[384,256]{1,0:T(8,128)(2,1)S(1)} %get-tuple-element.40), channel_id=1, source_target_pairs={{0,4},{1,5},{2,6},{3,7},{4,8},{5,9},{6,10},{7,11},{8,12},{9,13},{1... | collective-permute-start | bytes 589832 | tf_op jit(solution)/shard_map/ppermute | solution.py:419
  34.7 12.4 %collective-permute-start.11 = (bf16[384,256]{1,0:T(8,128)(2,1)S(1)}, bf16[384,256]{1,0:T(8,128)(2,1)S(1)}, u32[]{:S(2)}, u32[]{:S(2)}) collective-permute-start(bf16[384,256]{1,0:T(8,128)(2,1)S(1)} %get-tuple-element.40), channel_id=1, source_target_pairs={{0,8},{1,9},{2,10},{3,11},{4,12},{5,13},{6,14},{7,15},{8,0},{9,1},... | collective-permute-start | bytes 589832 | tf_op jit(solution)/shard_map/ppermute | solution.py:419
  36.5 13.3 %collective-permute-start.12 = (bf16[384,256]{1,0:T(8,128)(2,1)S(1)}, bf16[384,256]{1,0:T(8,128)(2,1)S(1)}, u32[]{:S(2)}, u32[]{:S(2)}) collective-permute-start(bf16[384,256]{1,0:T(8,128)(2,1)S(1)} %get-tuple-element.40), channel_id=1, source_target_pairs={{0,12},{1,13},{2,14},{3,15},{4,0},{5,1},{6,2},{7,3},{8,4},{9,5},{1... | collective-permute-start | bytes 589832 | tf_op jit(solution)/shard_map/ppermute | solution.py:419
  51.4 2.3 %collective-permute-start.16 = (bf16[512,256]{1,0:T(8,128)(2,1)S(1)}, bf16[512,256]{1,0:T(8,128)(2,1)S(1)}, u32[]{:S(2)}, u32[]{:S(2)}) collective-permute-start(bf16[512,256]{1,0:T(8,128)(2,1)S(1)} %get-tuple-element.49), channel_id=1, source_target_pairs={{0,1},{1,0},{2,3},{3,2},{4,5},{5,4},{6,7},{7,6},{8,9},{9,8},{10,11... | collective-permute-start | bytes 786440 | tf_op jit(solution)/shard_map/ppermute | solution.py:419
  54.5 27.4 %all-to-all-start = ((bf16[32,16,256]{2,1,0:T(8,128)(2,1)}), bf16[32,16,256]{2,1,0:T(8,128)(2,1)S(1)}, u32[]{:S(2)}, u32[]{:S(2)}) async-start(bf16[32,16,256]{2,1,0:T(8,128)(2,1)} %bitcast.9), calls=%async_computation | async-start | bytes 524288 | tf_op jit(solution)/shard_map/all_to_all | solution.py:463
  65.5 12.7 %collective-permute-start.8 = (bf16[128,1024]{1,0:T(8,128)(2,1)S(1)}, bf16[128,1024]{1,0:T(8,128)(2,1)S(1)}, u32[]{:S(2)}, u32[]{:S(2)}) collective-permute-start(bf16[128,1024]{1,0:T(8,128)(2,1)S(1)} %get-tuple-element.36), channel_id=1, source_target_pairs={{0,2},{1,3},{2,0},{3,1},{4,6},{5,7},{6,4},{7,5},{8,10},{9,11},{10,... | collective-permute-start | bytes 786440 | tf_op jit(solution)/shard_map/ppermute | solution.py:419
  78.4 2.6 %collective-permute-start.9 = (bf16[128,512]{1,0:T(8,128)(2,1)S(1)}, bf16[128,512]{1,0:T(8,128)(2,1)S(1)}, u32[]{:S(2)}, u32[]{:S(2)}) collective-permute-start(bf16[128,512]{1,0:T(8,128)(2,1)S(1)} %get-tuple-element.38), channel_id=1, source_target_pairs={{0,1},{1,0},{2,3},{3,2},{4,5},{5,4},{6,7},{7,6},{8,9},{9,8},{10,11... | collective-permute-start | bytes 393224 | tf_op jit(solution)/shard_map/ppermute | solution.py:419
where the time goes:
time: 82.7 us; the launch traced here: 82.5 us
  waiting for transfers between devices  38.7 us (47%)
  starting transfers between devices  32.7 us (40%)
  Pallas kernels  9.03 us (11%)
  other arithmetic  1.41 us (2%)
    ppermute x17, waiting for transfers between devices, permute(): return lax.ppermute(array, 'ctx', pairs)  38.7 us
    ppermute x17, starting transfers between devices, permute(): return lax.ppermute(array, 'ctx', pairs)  21.7 us
    all_to_all x1, starting transfers between devices, compute(): lax.all_to_all(blocks, ('dp', 'ctx'), split_axis=0, concat_axis=0, tiled=...  11 us
    pallas_call x1, Pallas kernels, scores(): pl.pallas_call(scores_kernel, out_shape=(shape(wide, jnp.float32), shape(...  1.95 us
  transfers between devices with their start and end apart: 18, of which 11 were waited for; matrix products, arithmetic and copies ran while one was open for 0% of the time, Pallas kernels for 7%

commit v1 on v0

--- a/solution.py
+++ b/solution.py
@@ -368,25 +368,32 @@
 
 
 def weight_kernel(
-    where_ref, keep_ref, r1, r2, r3, tab_ref, x0, x1, x2, x3,
+    where_ref, keep_ref, r1, r2k, r2v, r3, tab_ref, x0, x1, x2, x3,
     key_ref, value_ref, own_ref, send_ref, acc,
 ):
     core = where_ref[0] % 2
-    parts = (keep_ref, r1, r2, r3)
-    total = None
-    for k, x in enumerate((x0, x1, x2, x3)):
-        grad = None
-        for b in range(3):
-            part = parts[(k - b) % 4][b * B : (b + 1) * B, :].astype(jnp.float32)
-            grad = part if grad is None else grad + part
+
+    def part(source, b, lanes):
+        at = slice(b * B, (b + 1) * B)
+        if source == 2:
+            return (r2k, r2v)[lanes][at, :].astype(jnp.float32)
+        ref = (keep_ref, r1, None, r3)[source]
+        return ref[at, lanes * B : (lanes + 1) * B].astype(jnp.float32)
+
+    grads = []
+    for k in range(4):
+        key, value = (
+            part(k, 0, lanes) + part((k - 1) % 4, 1, lanes) + part((k - 2) % 4, 2, lanes) for lanes in (0, 1)
+        )
         cosine, sine = split_table(tab_ref[k * B : (k + 1) * B, :])
-        key = rotated(grad[:, :B], cosine, -sine).astype(jnp.bfloat16)
-        value = grad[:, B:].astype(jnp.bfloat16)
+        key = rotated(key, cosine, -sine).astype(jnp.bfloat16)
+        value = value.astype(jnp.bfloat16)
         if k == 0:
             key_ref[...] = key
             value_ref[...] = value
-        term = dot(x[...], jnp.concatenate([key, value], 1), NN)
-        total = term if total is None else total + term
+        grads.append(jnp.concatenate([key, value], 1))
+    total = dot(jnp.concatenate([x0[...], x1[...]], 1), jnp.concatenate(grads[:2], 0), NN)
+    total = total + dot(jnp.concatenate([x2[...], x3[...]], 1), jnp.concatenate(grads[2:], 0), NN)
     acc[...] = total
     for i in range(32):
         part = slice(i * 16, (i + 1) * 16)
@@ -403,13 +410,29 @@
             shape((512, 256), jnp.float32),
             shape((512, 256), jnp.bfloat16),
         ),
-        in_specs=[SMEM] + [VMEM] * 9,
+        in_specs=[SMEM] + [VMEM] * 10,
         out_specs=(VMEM,) * 4,
         scratch_shapes=[pltpu.VMEM((1024, 256), jnp.float32)],
         compiler_params=pltpu.CompilerParams(vmem_limit_bytes=12 * MIB),
         cost_estimate=pl.CostEstimate(flops=268_000_000, bytes_accessed=3_000_000, transcendentals=0),
         name="weight",
     )(rank, keep, *arrived, table, *xs)
+
+
+def weight_fold_kernel(own_ref, arrived_ref, out_ref):
+    out_ref[...] = (own_ref[...] + arrived_ref[...].astype(jnp.float32)).astype(jnp.bfloat16)
+
+
+def weight_fold(own, arrived):
+    return pl.pallas_call(
+        weight_fold_kernel,
+        out_shape=pltpu.VMEM((512, 256), jnp.bfloat16),
+        in_specs=[VMEM, VMEM],
+        out_specs=VMEM,
+        compiler_params=pltpu.CompilerParams(vmem_limit_bytes=4 * MIB),
+        cost_estimate=pl.CostEstimate(flops=131_072, bytes_accessed=1_000_000, transcendentals=0),
+        name="weight_fold",
+    )(own, arrived)
 
 
 def compute(layer_input, query_states, key_states, value_states, output_grad, doc_lengths):
@@ -446,15 +469,16 @@
     table = tables(where)
     keep, send, dq_keep, dq_send = gradients(where, lengths, kvs, p, d, q, g, stats)
 
-    arrived = [around(send, k) for k in (1, 2, 3)]
+    one, three = around(send, 1), around(send, 3)
+    arrived = [one, around(one[:, :B], 1), around(three[:, B:], 3), three]
     dq_z = swap(dq_send, 2)
     dq_mine, dq_send = query_fold(where, dq_keep, dq_z)
     dq_c = swap(dq_send, 1)
     query_grad = query_end(dq_mine, dq_c, table)
 
     key_grad, value_grad, own, send = weight_part(where, keep, arrived, table, xs)
-    own = own + swap(send, 1).astype(jnp.float32)
-    blocks = own.astype(jnp.bfloat16).reshape(32, 16, 256)
+    arrived = swap(send, 1)
+    blocks = weight_fold(own, arrived).reshape(32, 16, 256)
     groups = [
         [dp * 16 + slab * 4 + z * 2 + core for dp in range(16) for z in range(2)]
         for slab in range(4)

time: 82.7 us -> 81.9 us (level)
  waiting for transfers between devices: 38.7 us -> 34.9 us
  starting transfers between devices: 32.7 us -> 35.9 us
    ppermute x17 -> x18, waiting for transfers between devices: 38.7 us -> 34.9 us  [permute(): return lax.ppermute(array, 'ctx', pairs)]
    ppermute x17 -> x18, starting transfers between devices: 21.7 us -> 25.3 us  [permute(): return lax.ppermute(array, 'ctx', pairs)]
  transfers between devices with their start and end apart: 18 -> 19, of which waited for: 11 -> 14; matrix products, arithmetic and copies ran while one was open for 0% -> 0% of each run, Pallas kernels for 7% -> 3%
where the time goes in v1:
time: 81.9 us; the launch traced here: 81.7 us
  starting transfers between devices  35.9 us (44%)
  waiting for transfers between devices  34.9 us (43%)
  Pallas kernels  9.57 us (12%)
    ppermute x18, waiting for transfers between devices, permute(): return lax.ppermute(array, 'ctx', pairs)  34.9 us
    ppermute x18, starting transfers between devices, permute(): return lax.ppermute(array, 'ctx', pairs)  25.3 us
    all_to_all x1, starting transfers between devices, compute(): lax.all_to_all(blocks, ('dp', 'ctx'), split_axis=0, concat_axis=0, tiled=...  10.6 us
    pallas_call x1, Pallas kernels, scores(): pl.pallas_call(scores_kernel, out_shape=(shape(wide, jnp.float32), shape(...  1.95 us
  transfers between devices with their start and end apart: 19, of which 14 were waited for; matrix products, arithmetic and copies ran while one was open for 0% of the time, Pallas kernels for 3%

profile of v1, /device:TPU:1, one launch (start us, length us, event | category | flops | bytes accessed | tf_op | source)
XLA Modules:
  0.0 81.7 jit_solution(10357903602974724746)
XLA Ops:
  0.6 1.5 %prepare.1 = (bf16[128,256]{1,0:T(8,128)(2,1)S(1)}, bf16[128,1024]{1,0:T(8,128)(2,1)S(1)}, bf16[128,4096]{1,0:T(8,128)(2,1)S(1)}, s32[1,8]{1,0:T(1,128)S(1)}) custom-call(s32[1]{0:T(128)} %bitcast.where_ref, bf16[128,128]{1,0:T(8,128)(2,1)} %bitcast.14, bf16[128,128]{1,0:T(8,128)(2,1)} %bitcast.15, bf16[128,512]{1,0:T(8,128)(2,1)} %bitcast.11, ...), custom_call_target="tpu_custom_call" | custom-call | tf_op jit(solution)/shard_map/prepare/pallas_call | solution.py:90
  2.1 2.5 %collective-permute-start.3 = (bf16[128,1024]{1,0:T(8,128)(2,1)S(1)}, bf16[128,1024]{1,0:T(8,128)(2,1)S(1)}, u32[]{:S(2)}, u32[]{:S(2)}) collective-permute-start(bf16[128,1024]{1,0:T(8,128)(2,1)S(1)} %get-tuple-element.29.qg0), channel_id=1, source_target_pairs={{0,2},{1,3},{2,0},{3,1},{4,6},{5,7},{6,4},{7,5},{8,10},{9,11},{10,... | collective-permute-start | bytes 786440 | tf_op jit(solution)/shard_map/ppermute | solution.py:442
  4.7 1.0 %collective-permute-start.2 = (bf16[128,1024]{1,0:T(8,128)(2,1)S(1)}, bf16[128,1024]{1,0:T(8,128)(2,1)S(1)}, u32[]{:S(2)}, u32[]{:S(2)}) collective-permute-start(bf16[128,1024]{1,0:T(8,128)(2,1)S(1)} %get-tuple-element.29.qg0), channel_id=1, source_target_pairs={{0,1},{1,0},{2,3},{3,2},{4,5},{5,4},{6,7},{7,6},{8,9},{9,8},{10,11... | collective-permute-start | bytes 786440 | tf_op jit(solution)/shard_map/ppermute | solution.py:442
  5.6 4.0 %collective-permute-done.3.qg2 = bf16[128,1024]{1,0:T(8,128)(2,1)S(1)} collective-permute-done((bf16[128,1024]{1,0:T(8,128)(2,1)S(1)}, bf16[128,1024]{1,0:T(8,128)(2,1)S(1)}, u32[]{:S(2)}, u32[]{:S(2)}) %collective-permute-start.3) | collective-permute-done | bytes 262176 | tf_op jit(solution)/shard_map/ppermute | solution.py:442
  9.7 2.3 %collective-permute-start.4 = (bf16[128,1024]{1,0:T(8,128)(2,1)S(1)}, bf16[128,1024]{1,0:T(8,128)(2,1)S(1)}, u32[]{:S(2)}, u32[]{:S(2)}) collective-permute-start(bf16[128,1024]{1,0:T(8,128)(2,1)S(1)} %collective-permute-done.3.qg2), channel_id=1, source_target_pairs={{0,1},{1,0},{2,3},{3,2},{4,5},{5,4},{6,7},{7,6},{8,9},{9,8},{10,11... | collective-permute-start | bytes 786440 | tf_op jit(solution)/shard_map/ppermute | solution.py:442
  11.9 1.2 %collective-permute-start = (bf16[128,256]{1,0:T(8,128)(2,1)S(1)}, bf16[128,256]{1,0:T(8,128)(2,1)S(1)}, u32[]{:S(2)}, u32[]{:S(2)}) collective-permute-start(bf16[128,256]{1,0:T(8,128)(2,1)S(1)} %get-tuple-element.28.kv0), channel_id=1, source_target_pairs={{0,4},{1,5},{2,6},{3,7},{4,8},{5,9},{6,10},{7,11},{8,12},{9,13},{1... | collective-permute-start | bytes 196616 | tf_op jit(solution)/shard_map/ppermute | solution.py:442
  13.1 2.5 %collective-permute-start.1 = (bf16[128,256]{1,0:T(8,128)(2,1)S(1)}, bf16[128,256]{1,0:T(8,128)(2,1)S(1)}, u32[]{:S(2)}, u32[]{:S(2)}) collective-permute-start(bf16[128,256]{1,0:T(8,128)(2,1)S(1)} %get-tuple-element.28.kv0), channel_id=1, source_target_pairs={{0,8},{1,9},{2,10},{3,11},{4,12},{5,13},{6,14},{7,15},{8,0},{9,1},... | collective-permute-start | bytes 196616 | tf_op jit(solution)/shard_map/ppermute | solution.py:442
  15.6 1.2 %collective-permute-done.kv1 = bf16[128,256]{1,0:T(8,128)(2,1)S(1)} collective-permute-done((bf16[128,256]{1,0:T(8,128)(2,1)S(1)}, bf16[128,256]{1,0:T(8,128)(2,1)S(1)}, u32[]{:S(2)}, u32[]{:S(2)}) %collective-permute-start) | collective-permute-done | bytes 65568 | tf_op jit(solution)/shard_map/ppermute | solution.py:442
  16.8 2.4 %collective-permute-done.1.kv2 = bf16[128,256]{1,0:T(8,128)(2,1)S(1)} collective-permute-done((bf16[128,256]{1,0:T(8,128)(2,1)S(1)}, bf16[128,256]{1,0:T(8,128)(2,1)S(1)}, u32[]{:S(2)}, u32[]{:S(2)}) %collective-permute-start.1) | collective-permute-done | bytes 65568 | tf_op jit(solution)/shard_map/ppermute | solution.py:442
  19.2 0.0 collective-permute-done.2.qg1
  19.2 0.0 collective-permute-done.4.qg3
  19.2 1.9 %scores.1 = (f32[384,2048]{1,0:T(8,128)S(1)}, f32[384,2048]{1,0:T(8,128)S(1)}, bf16[2048,128]{1,0:T(8,128)(2,1)S(1)}, bf16[2048,128]{1,0:T(8,128)(2,1)S(1)}, f32[4,2048]{1,0:T(4,128)S(1)}) custom-call(s32[1]{0:T(128)} %bitcast.where_ref, s32[1,8]{1,0:T(1,128)S(1)} %get-tuple-element.27.len_ref, bf16[128,256]{1,0:T(8,128)(2,1)S(1)} %get-tuple-element.28.kv0, ...), custom_call_target="tpu_custom_call" | custom-call | flops 400000000 | bytes 8000000 | tf_op jit(solution)/shard_map/scores/pallas_call | solution.py:239
  21.1 0.5 collective-permute-start.5
  21.6 1.5 %collective-permute-start.6 = (f32[4,2048]{1,0:T(4,128)S(1)}, f32[4,2048]{1,0:T(4,128)S(1)}, u32[]{:S(2)}, u32[]{:S(2)}) collective-permute-start(f32[4,2048]{1,0:T(4,128)S(1)} %get-tuple-element.34.st0), channel_id=1, source_target_pairs={{0,2},{1,3},{2,0},{3,1},{4,6},{5,7},{6,4},{7,5},{8,10},{9,11},{10,... | collective-permute-start | bytes 98312 | tf_op jit(solution)/shard_map/ppermute | solution.py:442
  23.1 0.3 collective-permute-start.7
  23.4 0.0 collective-permute-done.5.st1
  23.4 1.0 %collective-permute-done.6.st2 = f32[4,2048]{1,0:T(4,128)S(1)} collective-permute-done((f32[4,2048]{1,0:T(4,128)S(1)}, f32[4,2048]{1,0:T(4,128)S(1)}, u32[]{:S(2)}, u32[]{:S(2)}) %collective-permute-start.6) | collective-permute-done | bytes 32800 | tf_op jit(solution)/shard_map/ppermute | solution.py:442
  24.4 2.1 %collective-permute-done.7.st3 = f32[4,2048]{1,0:T(4,128)S(1)} collective-permute-done((f32[4,2048]{1,0:T(4,128)S(1)}, f32[4,2048]{1,0:T(4,128)S(1)}, u32[]{:S(2)}, u32[]{:S(2)}) %collective-permute-start.7) | collective-permute-done | bytes 32800 | tf_op jit(solution)/shard_map/ppermute | solution.py:442
  26.5 1.6 %gradients.1 = (f32[384,256]{1,0:T(8,128)S(1)}, bf16[384,256]{1,0:T(8,128)(2,1)S(1)}, f32[128,1024]{1,0:T(8,128)S(1)}, bf16[128,1024]{1,0:T(8,128)(2,1)S(1)}) custom-call(s32[1]{0:T(128)} %bitcast.where_ref, s32[1,8]{1,0:T(1,128)S(1)} %get-tuple-element.27.len_ref, bf16[128,256]{1,0:T(8,128)(2,1)S(1)} %get-tuple-element.28.kv0, ...), custom_call_target="tpu_custom_call" | custom-call | flops 600000000 | bytes 8000000 | tf_op jit(solution)/shard_map/gradients/pallas_call | solution.py:306
  28.1 2.1 %collective-permute-start.10 = (bf16[384,256]{1,0:T(8,128)(2,1)S(1)}, bf16[384,256]{1,0:T(8,128)(2,1)S(1)}, u32[]{:S(2)}, u32[]{:S(2)}) collective-permute-start(bf16[384,256]{1,0:T(8,128)(2,1)S(1)} %get-tuple-element.40), channel_id=1, source_target_pairs={{0,4},{1,5},{2,6},{3,7},{4,8},{5,9},{6,10},{7,11},{8,12},{9,13},{1... | collective-permute-start | bytes 589832 | tf_op jit(solution)/shard_map/ppermute | solution.py:442
  30.2 0.7 collective-permute-start.12
  30.8 0.4 slices.1
  31.2 0.9 %collective-permute-start.14 = (bf16[1024,128]{1,0:T(8,128)(2,1)S(1)}, bf16[1024,128]{1,0:T(8,128)(2,1)S(1)}, u32[]{:S(2)}, u32[]{:S(2)}) collective-permute-start(bf16[1024,128]{1,0:T(8,128)(2,1)S(1)} %get-tuple-element.43), channel_id=1, source_target_pairs={{0,4},{1,5},{2,6},{3,7},{4,8},{5,9},{6,10},{7,11},{8,12},{9,13},{1... | collective-permute-start | bytes 786440 | tf_op jit(solution)/shard_map/ppermute | solution.py:442
  32.1 1.3 %collective-permute-start.15 = (bf16[1024,128]{1,0:T(8,128)(2,1)S(1)}, bf16[1024,128]{1,0:T(8,128)(2,1)S(1)}, u32[]{:S(2)}, u32[]{:S(2)}) collective-permute-start(bf16[1024,128]{1,0:T(8,128)(2,1)S(1)} %get-tuple-element.44), channel_id=1, source_target_pairs={{0,8},{1,9},{2,10},{3,11},{4,12},{5,13},{6,14},{7,15},{8,0},{9,1},... | collective-permute-start | bytes 786440 | tf_op jit(solution)/shard_map/ppermute | solution.py:442
  33.4 2.0 %collective-permute-start.16 = (bf16[1024,128]{1,0:T(8,128)(2,1)S(1)}, bf16[1024,128]{1,0:T(8,128)(2,1)S(1)}, u32[]{:S(2)}, u32[]{:S(2)}) collective-permute-start(bf16[1024,128]{1,0:T(8,128)(2,1)S(1)} %get-tuple-element.45), channel_id=1, source_target_pairs={{0,12},{1,13},{2,14},{3,15},{4,0},{5,1},{6,2},{7,3},{8,4},{9,5},{1... | collective-permute-start | bytes 786440 | tf_op jit(solution)/shard_map/ppermute | solution.py:442
  35.4 0.4 collective-permute-done.10.r1
  35.8 1.2 %collective-permute-start.11 = (bf16[384,128]{1,0:T(8,128)(2,1)S(1)}, bf16[384,128]{1,0:T(8,128)(2,1)S(1)}, u32[]{:S(2)}, u32[]{:S(2)}) collective-permute-start(bf16[384,128]{1,0:T(8,128)(2,1)S(1)} %slice.8), channel_id=1, source_target_pairs={{0,4},{1,5},{2,6},{3,7},{4,8},{5,9},{6,10},{7,11},{8,12},{9,13},{1... | collective-permute-start | bytes 294920 | tf_op jit(solution)/shard_map/ppermute | solution.py:442
  37.1 0.0 collective-permute-done.12.r3
  37.1 1.8 %collective-permute-start.13 = (bf16[384,128]{1,0:T(8,128)(2,1)S(1)}, bf16[384,128]{1,0:T(8,128)(2,1)S(1)}, u32[]{:S(2)}, u32[]{:S(2)}) collective-permute-start(bf16[384,128]{1,0:T(8,128)(2,1)S(1)} %slice.9), channel_id=1, source_target_pairs={{0,12},{1,13},{2,14},{3,15},{4,0},{5,1},{6,2},{7,3},{8,4},{9,5},{1... | collective-permute-start | bytes 294920 | tf_op jit(solution)/shard_map/ppermute | solution.py:442
  38.9 1.0 %tables.1.tab_ref = f32[512,128]{1,0:T(8,128)S(1)} custom-call(s32[1]{0:T(128)} %bitcast.where_ref), custom_call_target="tpu_custom_call" | custom-call | flops 2000000 | bytes 260000 | tf_op jit(solution)/shard_map/tables/pallas_call | solution.py:140
  39.9 1.5 %collective-permute-done.14.x1 = bf16[1024,128]{1,0:T(8,128)(2,1)S(1)} collective-permute-done((bf16[1024,128]{1,0:T(8,128)(2,1)S(1)}, bf16[1024,128]{1,0:T(8,128)(2,1)S(1)}, u32[]{:S(2)}, u32[]{:S(2)}) %collective-permute-start.14) | collective-permute-done | bytes 262176 | tf_op jit(solution)/shard_map/ppermute | solution.py:442
  41.5 6.4 %collective-permute-done.15.x2 = bf16[1024,128]{1,0:T(8,128)(2,1)S(1)} collective-permute-done((bf16[1024,128]{1,0:T(8,128)(2,1)S(1)}, bf16[1024,128]{1,0:T(8,128)(2,1)S(1)}, u32[]{:S(2)}, u32[]{:S(2)}) %collective-permute-start.15) | collective-permute-done | bytes 262176 | tf_op jit(solution)/shard_map/ppermute | solution.py:442
  47.8 0.1 collective-permute-done.16.x3
  48.0 1.2 %collective-permute-done.11.r2k = bf16[384,128]{1,0:T(8,128)(2,1)S(1)} collective-permute-done((bf16[384,128]{1,0:T(8,128)(2,1)S(1)}, bf16[384,128]{1,0:T(8,128)(2,1)S(1)}, u32[]{:S(2)}, u32[]{:S(2)}) %collective-permute-start.11) | collective-permute-done | bytes 98336 | tf_op jit(solution)/shard_map/ppermute | solution.py:442
  49.2 0.9 %collective-permute-done.13.r2v = bf16[384,128]{1,0:T(8,128)(2,1)S(1)} collective-permute-done((bf16[384,128]{1,0:T(8,128)(2,1)S(1)}, bf16[384,128]{1,0:T(8,128)(2,1)S(1)}, u32[]{:S(2)}, u32[]{:S(2)}) %collective-permute-start.13) | collective-permute-done | bytes 98336 | tf_op jit(solution)/shard_map/ppermute | solution.py:442
  50.1 1.3 %weight.1 = (bf16[128,128]{1,0:T(8,128)(2,1)}, bf16[128,128]{1,0:T(8,128)(2,1)}, f32[512,256]{1,0:T(8,128)S(1)}, bf16[512,256]{1,0:T(8,128)(2,1)S(1)}) custom-call(s32[1]{0:T(128)} %bitcast.where_ref, f32[384,256]{1,0:T(8,128)S(1)} %get-tuple-element.39.keep_ref, bf16[384,256]{1,0:T(8,128)(2,1)S(1)} %collective-permute-done.10.r1, ...), custom_call_target="tpu_custom_call" | custom-call | flops 268000000 | bytes 3000000 | tf_op jit(solution)/shard_map/weight/pallas_call | solution.py:405
  51.4 0.8 collective-permute-start.17
  52.2 1.2 %collective-permute-done.17.arrived_ref = bf16[512,256]{1,0:T(8,128)(2,1)S(1)} collective-permute-done((bf16[512,256]{1,0:T(8,128)(2,1)S(1)}, bf16[512,256]{1,0:T(8,128)(2,1)S(1)}, u32[]{:S(2)}, u32[]{:S(2)}) %collective-permute-start.17) | collective-permute-done | bytes 262176 | tf_op jit(solution)/shard_map/ppermute | solution.py:442
  53.3 0.8 weight_fold.1
  54.1 10.6 %all-to-all-start = ((bf16[32,16,256]{2,1,0:T(8,128)(2,1)}), bf16[32,16,256]{2,1,0:T(8,128)(2,1)S(1)}, u32[]{:S(2)}, u32[]{:S(2)}) async-start(bf16[32,16,256]{2,1,0:T(8,128)(2,1)} %bitcast.9), calls=%async_computation | async-start | bytes 524288 | tf_op jit(solution)/shard_map/all_to_all | solution.py:487
  64.8 1.3 %collective-permute-start.8 = (bf16[128,1024]{1,0:T(8,128)(2,1)S(1)}, bf16[128,1024]{1,0:T(8,128)(2,1)S(1)}, u32[]{:S(2)}, u32[]{:S(2)}) collective-permute-start(bf16[128,1024]{1,0:T(8,128)(2,1)S(1)} %get-tuple-element.36), channel_id=1, source_target_pairs={{0,2},{1,3},{2,0},{3,1},{4,6},{5,7},{6,4},{7,5},{8,10},{9,11},{10,... | collective-permute-start | bytes 786440 | tf_op jit(solution)/shard_map/ppermute | solution.py:442
  66.1 11.4 %collective-permute-done.8.arrived_ref = bf16[128,1024]{1,0:T(8,128)(2,1)S(1)} collective-permute-done((bf16[128,1024]{1,0:T(8,128)(2,1)S(1)}, bf16[128,1024]{1,0:T(8,128)(2,1)S(1)}, u32[]{:S(2)}, u32[]{:S(2)}) %collective-permute-start.8) | collective-permute-done | bytes 262176 | tf_op jit(solution)/shard_map/ppermute | solution.py:442
  77.5 0.1 query_fold.1
  77.6 1.6 %collective-permute-start.9 = (bf16[128,512]{1,0:T(8,128)(2,1)S(1)}, bf16[128,512]{1,0:T(8,128)(2,1)S(1)}, u32[]{:S(2)}, u32[]{:S(2)}) collective-permute-start(bf16[128,512]{1,0:T(8,128)(2,1)S(1)} %get-tuple-element.38), channel_id=1, source_target_pairs={{0,1},{1,0},{2,3},{3,2},{4,5},{5,4},{6,7},{7,6},{8,9},{9,8},{10,11... | collective-permute-start | bytes 393224 | tf_op jit(solution)/shard_map/ppermute | solution.py:442
  79.2 1.0 %collective-permute-done.9.arrived_ref = bf16[128,512]{1,0:T(8,128)(2,1)S(1)} collective-permute-done((bf16[128,512]{1,0:T(8,128)(2,1)S(1)}, bf16[128,512]{1,0:T(8,128)(2,1)S(1)}, u32[]{:S(2)}, u32[]{:S(2)}) %collective-permute-start.9) | collective-permute-done | bytes 131104 | tf_op jit(solution)/shard_map/ppermute | solution.py:442
  80.2 0.9 %query_end.1 = bf16[128,512]{1,0:T(8,128)(2,1)} custom-call(f32[128,512]{1,0:T(8,128)S(1)} %get-tuple-element.37.mine_ref, bf16[128,512]{1,0:T(8,128)(2,1)S(1)} %collective-permute-done.9.arrived_ref, f32[512,128]{1,0:T(8,128)S(1)} %tables.1.tab_ref), custom_call_target="tpu_custom_call" | custom-call | flops 300000 | bytes 700000 | tf_op jit(solution)/shard_map/query_end/pallas_call | solution.py:359
  81.1 0.0 all-to-all-done
  81.1 0.7 convert_reduce_fusion
  (2 shorter events, 0.0 us)
Async XLA Ops:
  2.1 7.5 %collective-permute-start.3 = (bf16[128,1024]{1,0:T(8,128)(2,1)S(1)}, bf16[128,1024]{1,0:T(8,128)(2,1)S(1)}, u32[]{:S(2)}, u32[]{:S(2)}) collective-permute-start(bf16[128,1024]{1,0:T(8,128)(2,1)S(1)} %get-tuple-element.29.qg0), channel_id=1, source_target_pairs={{0,2},{1,3},{2,0},{3,1},{4,6},{5,7},{6,4},{7,5},{8,10},{9,11},{10,... | collective-permute-start | bytes 786440 | tf_op jit(solution)/shard_map/ppermute | solution.py:442
  4.7 14.5 %collective-permute-start.2 = (bf16[128,1024]{1,0:T(8,128)(2,1)S(1)}, bf16[128,1024]{1,0:T(8,128)(2,1)S(1)}, u32[]{:S(2)}, u32[]{:S(2)}) collective-permute-start(bf16[128,1024]{1,0:T(8,128)(2,1)S(1)} %get-tuple-element.29.qg0), channel_id=1, source_target_pairs={{0,1},{1,0},{2,3},{3,2},{4,5},{5,4},{6,7},{7,6},{8,9},{9,8},{10,11... | collective-permute-start | bytes 786440 | tf_op jit(solution)/shard_map/ppermute | solution.py:442
  9.7 9.5 %collective-permute-start.4 = (bf16[128,1024]{1,0:T(8,128)(2,1)S(1)}, bf16[128,1024]{1,0:T(8,128)(2,1)S(1)}, u32[]{:S(2)}, u32[]{:S(2)}) collective-permute-start(bf16[128,1024]{1,0:T(8,128)(2,1)S(1)} %collective-permute-done.3.qg2), channel_id=1, source_target_pairs={{0,1},{1,0},{2,3},{3,2},{4,5},{5,4},{6,7},{7,6},{8,9},{9,8},{10,11... | collective-permute-start | bytes 786440 | tf_op jit(solution)/shard_map/ppermute | solution.py:442
  11.9 4.9 %collective-permute-start = (bf16[128,256]{1,0:T(8,128)(2,1)S(1)}, bf16[128,256]{1,0:T(8,128)(2,1)S(1)}, u32[]{:S(2)}, u32[]{:S(2)}) collective-permute-start(bf16[128,256]{1,0:T(8,128)(2,1)S(1)} %get-tuple-element.28.kv0), channel_id=1, source_target_pairs={{0,4},{1,5},{2,6},{3,7},{4,8},{5,9},{6,10},{7,11},{8,12},{9,13},{1... | collective-permute-start | bytes 196616 | tf_op jit(solution)/shard_map/ppermute | solution.py:442
  13.1 6.0 %collective-permute-start.1 = (bf16[128,256]{1,0:T(8,128)(2,1)S(1)}, bf16[128,256]{1,0:T(8,128)(2,1)S(1)}, u32[]{:S(2)}, u32[]{:S(2)}) collective-permute-start(bf16[128,256]{1,0:T(8,128)(2,1)S(1)} %get-tuple-element.28.kv0), channel_id=1, source_target_pairs={{0,8},{1,9},{2,10},{3,11},{4,12},{5,13},{6,14},{7,15},{8,0},{9,1},... | collective-permute-start | bytes 196616 | tf_op jit(solution)/shard_map/ppermute | solution.py:442
  21.1 2.2 %collective-permute-start.5 = (f32[4,2048]{1,0:T(4,128)S(1)}, f32[4,2048]{1,0:T(4,128)S(1)}, u32[]{:S(2)}, u32[]{:S(2)}) collective-permute-start(f32[4,2048]{1,0:T(4,128)S(1)} %get-tuple-element.34.st0), channel_id=1, source_target_pairs={{0,1},{1,0},{2,3},{3,2},{4,5},{5,4},{6,7},{7,6},{8,9},{9,8},{10,11... | collective-permute-start | bytes 98312 | tf_op jit(solution)/shard_map/ppermute | solution.py:442
  21.6 2.8 %collective-permute-start.6 = (f32[4,2048]{1,0:T(4,128)S(1)}, f32[4,2048]{1,0:T(4,128)S(1)}, u32[]{:S(2)}, u32[]{:S(2)}) collective-permute-start(f32[4,2048]{1,0:T(4,128)S(1)} %get-tuple-element.34.st0), channel_id=1, source_target_pairs={{0,2},{1,3},{2,0},{3,1},{4,6},{5,7},{6,4},{7,5},{8,10},{9,11},{10,... | collective-permute-start | bytes 98312 | tf_op jit(solution)/shard_map/ppermute | solution.py:442
  23.1 3.4 %collective-permute-start.7 = (f32[4,2048]{1,0:T(4,128)S(1)}, f32[4,2048]{1,0:T(4,128)S(1)}, u32[]{:S(2)}, u32[]{:S(2)}) collective-permute-start(f32[4,2048]{1,0:T(4,128)S(1)} %get-tuple-element.34.st0), channel_id=1, source_target_pairs={{0,3},{1,2},{2,1},{3,0},{4,7},{5,6},{6,5},{7,4},{8,11},{9,10},{10,... | collective-permute-start | bytes 98312 | tf_op jit(solution)/shard_map/ppermute | solution.py:442
  28.1 7.7 %collective-permute-start.10 = (bf16[384,256]{1,0:T(8,128)(2,1)S(1)}, bf16[384,256]{1,0:T(8,128)(2,1)S(1)}, u32[]{:S(2)}, u32[]{:S(2)}) collective-permute-start(bf16[384,256]{1,0:T(8,128)(2,1)S(1)} %get-tuple-element.40), channel_id=1, source_target_pairs={{0,4},{1,5},{2,6},{3,7},{4,8},{5,9},{6,10},{7,11},{8,12},{9,13},{1... | collective-permute-start | bytes 589832 | tf_op jit(solution)/shard_map/ppermute | solution.py:442
  30.2 6.9 %collective-permute-start.12 = (bf16[384,256]{1,0:T(8,128)(2,1)S(1)}, bf16[384,256]{1,0:T(8,128)(2,1)S(1)}, u32[]{:S(2)}, u32[]{:S(2)}) collective-permute-start(bf16[384,256]{1,0:T(8,128)(2,1)S(1)} %get-tuple-element.40), channel_id=1, source_target_pairs={{0,12},{1,13},{2,14},{3,15},{4,0},{5,1},{6,2},{7,3},{8,4},{9,5},{1... | collective-permute-start | bytes 589832 | tf_op jit(solution)/shard_map/ppermute | solution.py:442
  31.2 10.2 %collective-permute-start.14 = (bf16[1024,128]{1,0:T(8,128)(2,1)S(1)}, bf16[1024,128]{1,0:T(8,128)(2,1)S(1)}, u32[]{:S(2)}, u32[]{:S(2)}) collective-permute-start(bf16[1024,128]{1,0:T(8,128)(2,1)S(1)} %get-tuple-element.43), channel_id=1, source_target_pairs={{0,4},{1,5},{2,6},{3,7},{4,8},{5,9},{6,10},{7,11},{8,12},{9,13},{1... | collective-permute-start | bytes 786440 | tf_op jit(solution)/shard_map/ppermute | solution.py:442
  32.1 15.7 %collective-permute-start.15 = (bf16[1024,128]{1,0:T(8,128)(2,1)S(1)}, bf16[1024,128]{1,0:T(8,128)(2,1)S(1)}, u32[]{:S(2)}, u32[]{:S(2)}) collective-permute-start(bf16[1024,128]{1,0:T(8,128)(2,1)S(1)} %get-tuple-element.44), channel_id=1, source_target_pairs={{0,8},{1,9},{2,10},{3,11},{4,12},{5,13},{6,14},{7,15},{8,0},{9,1},... | collective-permute-start | bytes 786440 | tf_op jit(solution)/shard_map/ppermute | solution.py:442
  33.4 14.5 %collective-permute-start.16 = (bf16[1024,128]{1,0:T(8,128)(2,1)S(1)}, bf16[1024,128]{1,0:T(8,128)(2,1)S(1)}, u32[]{:S(2)}, u32[]{:S(2)}) collective-permute-start(bf16[1024,128]{1,0:T(8,128)(2,1)S(1)} %get-tuple-element.45), channel_id=1, source_target_pairs={{0,12},{1,13},{2,14},{3,15},{4,0},{5,1},{6,2},{7,3},{8,4},{9,5},{1... | collective-permute-start | bytes 786440 | tf_op jit(solution)/shard_map/ppermute | solution.py:442
  35.8 13.3 %collective-permute-start.11 = (bf16[384,128]{1,0:T(8,128)(2,1)S(1)}, bf16[384,128]{1,0:T(8,128)(2,1)S(1)}, u32[]{:S(2)}, u32[]{:S(2)}) collective-permute-start(bf16[384,128]{1,0:T(8,128)(2,1)S(1)} %slice.8), channel_id=1, source_target_pairs={{0,4},{1,5},{2,6},{3,7},{4,8},{5,9},{6,10},{7,11},{8,12},{9,13},{1... | collective-permute-start | bytes 294920 | tf_op jit(solution)/shard_map/ppermute | solution.py:442
  37.1 13.0 %collective-permute-start.13 = (bf16[384,128]{1,0:T(8,128)(2,1)S(1)}, bf16[384,128]{1,0:T(8,128)(2,1)S(1)}, u32[]{:S(2)}, u32[]{:S(2)}) collective-permute-start(bf16[384,128]{1,0:T(8,128)(2,1)S(1)} %slice.9), channel_id=1, source_target_pairs={{0,12},{1,13},{2,14},{3,15},{4,0},{5,1},{6,2},{7,3},{8,4},{9,5},{1... | collective-permute-start | bytes 294920 | tf_op jit(solution)/shard_map/ppermute | solution.py:442
  51.4 1.9 %collective-permute-start.17 = (bf16[512,256]{1,0:T(8,128)(2,1)S(1)}, bf16[512,256]{1,0:T(8,128)(2,1)S(1)}, u32[]{:S(2)}, u32[]{:S(2)}) collective-permute-start(bf16[512,256]{1,0:T(8,128)(2,1)S(1)} %get-tuple-element.49), channel_id=1, source_target_pairs={{0,1},{1,0},{2,3},{3,2},{4,5},{5,4},{6,7},{7,6},{8,9},{9,8},{10,11... | collective-permute-start | bytes 786440 | tf_op jit(solution)/shard_map/ppermute | solution.py:442
  54.1 27.0 %all-to-all-start = ((bf16[32,16,256]{2,1,0:T(8,128)(2,1)}), bf16[32,16,256]{2,1,0:T(8,128)(2,1)S(1)}, u32[]{:S(2)}, u32[]{:S(2)}) async-start(bf16[32,16,256]{2,1,0:T(8,128)(2,1)} %bitcast.9), calls=%async_computation | async-start | bytes 524288 | tf_op jit(solution)/shard_map/all_to_all | solution.py:487
  64.8 12.7 %collective-permute-start.8 = (bf16[128,1024]{1,0:T(8,128)(2,1)S(1)}, bf16[128,1024]{1,0:T(8,128)(2,1)S(1)}, u32[]{:S(2)}, u32[]{:S(2)}) collective-permute-start(bf16[128,1024]{1,0:T(8,128)(2,1)S(1)} %get-tuple-element.36), channel_id=1, source_target_pairs={{0,2},{1,3},{2,0},{3,1},{4,6},{5,7},{6,4},{7,5},{8,10},{9,11},{10,... | collective-permute-start | bytes 786440 | tf_op jit(solution)/shard_map/ppermute | solution.py:442
  77.6 2.6 %collective-permute-start.9 = (bf16[128,512]{1,0:T(8,128)(2,1)S(1)}, bf16[128,512]{1,0:T(8,128)(2,1)S(1)}, u32[]{:S(2)}, u32[]{:S(2)}) collective-permute-start(bf16[128,512]{1,0:T(8,128)(2,1)S(1)} %get-tuple-element.38), channel_id=1, source_target_pairs={{0,1},{1,0},{2,3},{3,2},{4,5},{5,4},{6,7},{7,6},{8,9},{9,8},{10,11... | collective-permute-start | bytes 393224 | tf_op jit(solution)/shard_map/ppermute | solution.py:442

commit v2 on v1

--- a/solution.py
+++ b/solution.py
@@ -111,16 +111,19 @@
     slab = where_ref[0] // 4
     for i in range(32):
         turned[i * B : (i + 1) * B, :] = x_ref[:, i * B : (i + 1) * B].T
-    for k, out in enumerate((o0, o1, o2, o3)):
+    plan = ((o0, 0, 0, 16), (o1, 1, 0, 16), (o2, 2, 0, 8), (o3, 3, 0, 16), (o3, 2, 8, 16))
+    for out, k, low, high in plan:
+        base = 1024 - 512 if (k, low) == (2, 8) else 0
         target = (slab + k) % 4
-        for dp in range(16):
-            out[dp * 64 : (dp + 1) * 64, :] = turned[rows(dp * 4 + target, 64), :]
+        for dp in range(low, high):
+            at = base + dp * 64
+            out[at : at + 64, :] = turned[rows(dp * 4 + target, 64), :]
 
 
 def slices(rank, x):
     return pl.pallas_call(
         slices_kernel,
-        out_shape=[shape((1024, B), jnp.bfloat16)] * 4,
+        out_shape=[shape((size, B), jnp.bfloat16) for size in (1024, 1024, 512, 1536)],
         in_specs=[SMEM, VMEM],
         out_specs=[VMEM] * 4,
         scratch_shapes=[pltpu.VMEM((4096, B), jnp.bfloat16)],
@@ -368,16 +371,14 @@
 
 
 def weight_kernel(
-    where_ref, keep_ref, r1, r2k, r2v, r3, tab_ref, x0, x1, x2, x3,
+    where_ref, keep_ref, r1, r2, r3, tab_ref, x0, x1, x2a, x2b, x3,
     key_ref, value_ref, own_ref, send_ref, acc,
 ):
     core = where_ref[0] % 2
 
     def part(source, b, lanes):
         at = slice(b * B, (b + 1) * B)
-        if source == 2:
-            return (r2k, r2v)[lanes][at, :].astype(jnp.float32)
-        ref = (keep_ref, r1, None, r3)[source]
+        ref = (keep_ref, r1, r2, r3)[source]
         return ref[at, lanes * B : (lanes + 1) * B].astype(jnp.float32)
 
     grads = []
@@ -393,7 +394,8 @@
             value_ref[...] = value
         grads.append(jnp.concatenate([key, value], 1))
     total = dot(jnp.concatenate([x0[...], x1[...]], 1), jnp.concatenate(grads[:2], 0), NN)
-    total = total + dot(jnp.concatenate([x2[...], x3[...]], 1), jnp.concatenate(grads[2:], 0), NN)
+    x2 = jnp.concatenate([x2a[...], x2b[...]], 0)
+    total = total + dot(jnp.concatenate([x2, x3[:1024, :]], 1), jnp.concatenate(grads[2:], 0), NN)
     acc[...] = total
     for i in range(32):
         part = slice(i * 16, (i + 1) * 16)
@@ -462,15 +464,15 @@
     qg_cz = swap(qg_z, 1)
 
     xs = slices(where, x)
-    xs = [xs[0]] + [around(xs[k], k) for k in (1, 2, 3)]
+    x1, x2, x3 = (around(xs[k], k) for k in (1, 2, 3))
+    xs = [xs[0], x1, x2, around(x3[1024:], 3), x3]
 
     p, d, q, g, stat = scores(where, lengths, kvs, (qg, qg_c, qg_z, qg_cz))
     stats = [stat] + [swap(stat, bits) for bits in (1, 2, 3)]
     table = tables(where)
     keep, send, dq_keep, dq_send = gradients(where, lengths, kvs, p, d, q, g, stats)
 
-    one, three = around(send, 1), around(send, 3)
-    arrived = [one, around(one[:, :B], 1), around(three[:, B:], 3), three]
+    arrived = [around(send, k) for k in (1, 2, 3)]
     dq_z = swap(dq_send, 2)
     dq_mine, dq_send = query_fold(where, dq_keep, dq_z)
     dq_c = swap(dq_send, 1)

time: 81.9 us -> 82.6 us (level)
  starting transfers between devices: 35.9 us -> 40.4 us
  waiting for transfers between devices: 34.9 us -> 31.1 us
    ppermute x18, starting transfers between devices: 25.3 us -> 29.4 us  [permute(): return lax.ppermute(array, 'ctx', pairs)]
    ppermute x18, waiting for transfers between devices: 34.9 us -> 31.1 us  [permute(): return lax.ppermute(array, 'ctx', pairs)]
  transfers between devices with their start and end apart: 19 -> 19, of which waited for: 14 -> 8; matrix products, arithmetic and copies ran while one was open for 0% -> 0% of each run, Pallas kernels for 3% -> 7%
where the time goes in v2:
time: 82.6 us; the launch traced here: 82.4 us
  starting transfers between devices  40.4 us (49%)
  waiting for transfers between devices  31.1 us (38%)
  Pallas kernels  9.57 us (12%)
    ppermute x18, waiting for transfers between devices, permute(): return lax.ppermute(array, 'ctx', pairs)  31.1 us
    ppermute x18, starting transfers between devices, permute(): return lax.ppermute(array, 'ctx', pairs)  29.4 us
    all_to_all x1, starting transfers between devices, compute(): lax.all_to_all(blocks, ('dp', 'ctx'), split_axis=0, concat_axis=0, tiled=...  11 us
    pallas_call x1, Pallas kernels, scores(): pl.pallas_call(scores_kernel, out_shape=(shape(wide, jnp.float32), shape(...  1.95 us
  transfers between devices with their start and end apart: 19, of which 8 were waited for; matrix products, arithmetic and copies ran while one was open for 0% of the time, Pallas kernels for 7%

profile of v2, /device:TPU:1, one launch (start us, length us, event | category | flops | bytes accessed | tf_op | source)
XLA Modules:
  0.0 82.4 jit_solution(7440072619419630695)
XLA Ops:
  0.6 1.5 %prepare.1 = (bf16[128,256]{1,0:T(8,128)(2,1)S(1)}, bf16[128,1024]{1,0:T(8,128)(2,1)S(1)}, bf16[128,4096]{1,0:T(8,128)(2,1)S(1)}, s32[1,8]{1,0:T(1,128)S(1)}) custom-call(s32[1]{0:T(128)} %bitcast.where_ref, bf16[128,128]{1,0:T(8,128)(2,1)} %bitcast.14, bf16[128,128]{1,0:T(8,128)(2,1)} %bitcast.15, bf16[128,512]{1,0:T(8,128)(2,1)} %bitcast.11, ...), custom_call_target="tpu_custom_call" | custom-call | tf_op jit(solution)/shard_map/prepare/pallas_call | solution.py:90
  2.1 2.5 %collective-permute-start.3 = (bf16[128,1024]{1,0:T(8,128)(2,1)S(1)}, bf16[128,1024]{1,0:T(8,128)(2,1)S(1)}, u32[]{:S(2)}, u32[]{:S(2)}) collective-permute-start(bf16[128,1024]{1,0:T(8,128)(2,1)S(1)} %get-tuple-element.29.qg0), channel_id=1, source_target_pairs={{0,2},{1,3},{2,0},{3,1},{4,6},{5,7},{6,4},{7,5},{8,10},{9,11},{10,... | collective-permute-start | bytes 786440 | tf_op jit(solution)/shard_map/ppermute | solution.py:444
  4.7 1.0 %collective-permute-start.2 = (bf16[128,1024]{1,0:T(8,128)(2,1)S(1)}, bf16[128,1024]{1,0:T(8,128)(2,1)S(1)}, u32[]{:S(2)}, u32[]{:S(2)}) collective-permute-start(bf16[128,1024]{1,0:T(8,128)(2,1)S(1)} %get-tuple-element.29.qg0), channel_id=1, source_target_pairs={{0,1},{1,0},{2,3},{3,2},{4,5},{5,4},{6,7},{7,6},{8,9},{9,8},{10,11... | collective-permute-start | bytes 786440 | tf_op jit(solution)/shard_map/ppermute | solution.py:444
  5.6 4.0 %collective-permute-done.3.qg2 = bf16[128,1024]{1,0:T(8,128)(2,1)S(1)} collective-permute-done((bf16[128,1024]{1,0:T(8,128)(2,1)S(1)}, bf16[128,1024]{1,0:T(8,128)(2,1)S(1)}, u32[]{:S(2)}, u32[]{:S(2)}) %collective-permute-start.3) | collective-permute-done | bytes 262176 | tf_op jit(solution)/shard_map/ppermute | solution.py:444
  9.7 2.3 %collective-permute-start.4 = (bf16[128,1024]{1,0:T(8,128)(2,1)S(1)}, bf16[128,1024]{1,0:T(8,128)(2,1)S(1)}, u32[]{:S(2)}, u32[]{:S(2)}) collective-permute-start(bf16[128,1024]{1,0:T(8,128)(2,1)S(1)} %collective-permute-done.3.qg2), channel_id=1, source_target_pairs={{0,1},{1,0},{2,3},{3,2},{4,5},{5,4},{6,7},{7,6},{8,9},{9,8},{10,11... | collective-permute-start | bytes 786440 | tf_op jit(solution)/shard_map/ppermute | solution.py:444
  11.9 0.4 slices.1
  12.3 2.6 %collective-permute-start.15 = (bf16[1536,128]{1,0:T(8,128)(2,1)S(1)}, bf16[1536,128]{1,0:T(8,128)(2,1)S(1)}, u32[]{:S(2)}, u32[]{:S(2)}) collective-permute-start(bf16[1536,128]{1,0:T(8,128)(2,1)S(1)} %get-tuple-element.45), channel_id=1, source_target_pairs={{0,12},{1,13},{2,14},{3,15},{4,0},{5,1},{6,2},{7,3},{8,4},{9,5},{1... | collective-permute-start | bytes 1179656 | tf_op jit(solution)/shard_map/ppermute | solution.py:444
  14.9 0.0 collective-permute-start
  14.9 1.7 %collective-permute-start.1 = (bf16[128,256]{1,0:T(8,128)(2,1)S(1)}, bf16[128,256]{1,0:T(8,128)(2,1)S(1)}, u32[]{:S(2)}, u32[]{:S(2)}) collective-permute-start(bf16[128,256]{1,0:T(8,128)(2,1)S(1)} %get-tuple-element.28.kv0), channel_id=1, source_target_pairs={{0,8},{1,9},{2,10},{3,11},{4,12},{5,13},{6,14},{7,15},{8,0},{9,1},... | collective-permute-start | bytes 196616 | tf_op jit(solution)/shard_map/ppermute | solution.py:444
  16.6 4.5 %collective-permute-done.kv1 = bf16[128,256]{1,0:T(8,128)(2,1)S(1)} collective-permute-done((bf16[128,256]{1,0:T(8,128)(2,1)S(1)}, bf16[128,256]{1,0:T(8,128)(2,1)S(1)}, u32[]{:S(2)}, u32[]{:S(2)}) %collective-permute-start) | collective-permute-done | bytes 65568 | tf_op jit(solution)/shard_map/ppermute | solution.py:444
  21.1 0.0 collective-permute-done.1.kv2
  21.1 0.0 collective-permute-done.2.qg1
  21.1 0.0 collective-permute-done.4.qg3
  21.1 2.0 %scores.1 = (f32[384,2048]{1,0:T(8,128)S(1)}, f32[384,2048]{1,0:T(8,128)S(1)}, bf16[2048,128]{1,0:T(8,128)(2,1)S(1)}, bf16[2048,128]{1,0:T(8,128)(2,1)S(1)}, f32[4,2048]{1,0:T(4,128)S(1)}) custom-call(s32[1]{0:T(128)} %bitcast.where_ref, s32[1,8]{1,0:T(1,128)S(1)} %get-tuple-element.27.len_ref, bf16[128,256]{1,0:T(8,128)(2,1)S(1)} %get-tuple-element.28.kv0, ...), custom_call_target="tpu_custom_call" | custom-call | flops 400000000 | bytes 8000000 | tf_op jit(solution)/shard_map/scores/pallas_call | solution.py:242
  23.0 0.6 collective-permute-start.5
  23.6 1.5 %collective-permute-start.6 = (f32[4,2048]{1,0:T(4,128)S(1)}, f32[4,2048]{1,0:T(4,128)S(1)}, u32[]{:S(2)}, u32[]{:S(2)}) collective-permute-start(f32[4,2048]{1,0:T(4,128)S(1)} %get-tuple-element.34.st0), channel_id=1, source_target_pairs={{0,2},{1,3},{2,0},{3,1},{4,6},{5,7},{6,4},{7,5},{8,10},{9,11},{10,... | collective-permute-start | bytes 98312 | tf_op jit(solution)/shard_map/ppermute | solution.py:444
  25.1 0.3 collective-permute-start.7
  25.4 6.3 %collective-permute-start.13 = (bf16[1024,128]{1,0:T(8,128)(2,1)S(1)}, bf16[1024,128]{1,0:T(8,128)(2,1)S(1)}, u32[]{:S(2)}, u32[]{:S(2)}) collective-permute-start(bf16[1024,128]{1,0:T(8,128)(2,1)S(1)} %get-tuple-element.43), channel_id=1, source_target_pairs={{0,4},{1,5},{2,6},{3,7},{4,8},{5,9},{6,10},{7,11},{8,12},{9,13},{1... | collective-permute-start | bytes 786440 | tf_op jit(solution)/shard_map/ppermute | solution.py:444
  31.7 0.0 collective-permute-done.5.st1
  31.7 1.0 %collective-permute-start.14 = (bf16[512,128]{1,0:T(8,128)(2,1)S(1)}, bf16[512,128]{1,0:T(8,128)(2,1)S(1)}, u32[]{:S(2)}, u32[]{:S(2)}) collective-permute-start(bf16[512,128]{1,0:T(8,128)(2,1)S(1)} %get-tuple-element.44), channel_id=1, source_target_pairs={{0,8},{1,9},{2,10},{3,11},{4,12},{5,13},{6,14},{7,15},{8,0},{9,1},... | collective-permute-start | bytes 393224 | tf_op jit(solution)/shard_map/ppermute | solution.py:444
  32.7 0.0 collective-permute-done.6.st2
  32.7 0.0 collective-permute-done.7.st3
  32.7 1.6 %gradients.1 = (f32[384,256]{1,0:T(8,128)S(1)}, bf16[384,256]{1,0:T(8,128)(2,1)S(1)}, f32[128,1024]{1,0:T(8,128)S(1)}, bf16[128,1024]{1,0:T(8,128)(2,1)S(1)}) custom-call(s32[1]{0:T(128)} %bitcast.where_ref, s32[1,8]{1,0:T(1,128)S(1)} %get-tuple-element.27.len_ref, bf16[128,256]{1,0:T(8,128)(2,1)S(1)} %get-tuple-element.28.kv0, ...), custom_call_target="tpu_custom_call" | custom-call | flops 600000000 | bytes 8000000 | tf_op jit(solution)/shard_map/gradients/pallas_call | solution.py:309
  34.3 3.2 %collective-permute-start.10 = (bf16[384,256]{1,0:T(8,128)(2,1)S(1)}, bf16[384,256]{1,0:T(8,128)(2,1)S(1)}, u32[]{:S(2)}, u32[]{:S(2)}) collective-permute-start(bf16[384,256]{1,0:T(8,128)(2,1)S(1)} %get-tuple-element.40), channel_id=1, source_target_pairs={{0,4},{1,5},{2,6},{3,7},{4,8},{5,9},{6,10},{7,11},{8,12},{9,13},{1... | collective-permute-start | bytes 589832 | tf_op jit(solution)/shard_map/ppermute | solution.py:444
  37.5 0.7 collective-permute-start.11
  38.2 0.0 collective-permute-done.15.x3
  38.2 1.8 %collective-permute-start.12 = (bf16[384,256]{1,0:T(8,128)(2,1)S(1)}, bf16[384,256]{1,0:T(8,128)(2,1)S(1)}, u32[]{:S(2)}, u32[]{:S(2)}) collective-permute-start(bf16[384,256]{1,0:T(8,128)(2,1)S(1)} %get-tuple-element.40), channel_id=1, source_target_pairs={{0,12},{1,13},{2,14},{3,15},{4,0},{5,1},{6,2},{7,3},{8,4},{9,5},{1... | collective-permute-start | bytes 589832 | tf_op jit(solution)/shard_map/ppermute | solution.py:444
  40.0 1.7 %collective-permute-done.14.x2a = bf16[512,128]{1,0:T(8,128)(2,1)S(1)} collective-permute-done((bf16[512,128]{1,0:T(8,128)(2,1)S(1)}, bf16[512,128]{1,0:T(8,128)(2,1)S(1)}, u32[]{:S(2)}, u32[]{:S(2)}) %collective-permute-start.14) | collective-permute-done | bytes 131104 | tf_op jit(solution)/shard_map/ppermute | solution.py:444
  41.7 0.0 collective-permute-start.16
  41.7 1.0 %tables.1.tab_ref = f32[512,128]{1,0:T(8,128)S(1)} custom-call(s32[1]{0:T(128)} %bitcast.where_ref), custom_call_target="tpu_custom_call" | custom-call | flops 2000000 | bytes 260000 | tf_op jit(solution)/shard_map/tables/pallas_call | solution.py:143
  42.7 0.0 collective-permute-done.13.x1
  42.7 6.5 %collective-permute-done.16.x2b = bf16[512,128]{1,0:T(8,128)(2,1)S(1)} collective-permute-done((bf16[512,128]{1,0:T(8,128)(2,1)S(1)}, bf16[512,128]{1,0:T(8,128)(2,1)S(1)}, u32[]{:S(2)}, u32[]{:S(2)}) %collective-permute-start.16) | collective-permute-done | bytes 131104 | tf_op jit(solution)/shard_map/ppermute | solution.py:444
  49.2 0.0 collective-permute-done.10.r1
  49.2 0.9 %collective-permute-done.11.r2 = bf16[384,256]{1,0:T(8,128)(2,1)S(1)} collective-permute-done((bf16[384,256]{1,0:T(8,128)(2,1)S(1)}, bf16[384,256]{1,0:T(8,128)(2,1)S(1)}, u32[]{:S(2)}, u32[]{:S(2)}) %collective-permute-start.11) | collective-permute-done | bytes 196640 | tf_op jit(solution)/shard_map/ppermute | solution.py:444
  50.1 0.0 collective-permute-done.12.r3
  50.1 1.3 %weight.1 = (bf16[128,128]{1,0:T(8,128)(2,1)}, bf16[128,128]{1,0:T(8,128)(2,1)}, f32[512,256]{1,0:T(8,128)S(1)}, bf16[512,256]{1,0:T(8,128)(2,1)S(1)}) custom-call(s32[1]{0:T(128)} %bitcast.where_ref, f32[384,256]{1,0:T(8,128)S(1)} %get-tuple-element.39.keep_ref, bf16[384,256]{1,0:T(8,128)(2,1)S(1)} %collective-permute-done.10.r1, ...), custom_call_target="tpu_custom_call" | custom-call | flops 268000000 | bytes 3000000 | tf_op jit(solution)/shard_map/weight/pallas_call | solution.py:407
  51.4 1.1 %collective-permute-start.17 = (bf16[512,256]{1,0:T(8,128)(2,1)S(1)}, bf16[512,256]{1,0:T(8,128)(2,1)S(1)}, u32[]{:S(2)}, u32[]{:S(2)}) collective-permute-start(bf16[512,256]{1,0:T(8,128)(2,1)S(1)} %get-tuple-element.49), channel_id=1, source_target_pairs={{0,1},{1,0},{2,3},{3,2},{4,5},{5,4},{6,7},{7,6},{8,9},{9,8},{10,11... | collective-permute-start | bytes 786440 | tf_op jit(solution)/shard_map/ppermute | solution.py:444
  52.5 1.2 %collective-permute-done.17.arrived_ref = bf16[512,256]{1,0:T(8,128)(2,1)S(1)} collective-permute-done((bf16[512,256]{1,0:T(8,128)(2,1)S(1)}, bf16[512,256]{1,0:T(8,128)(2,1)S(1)}, u32[]{:S(2)}, u32[]{:S(2)}) %collective-permute-start.17) | collective-permute-done | bytes 262176 | tf_op jit(solution)/shard_map/ppermute | solution.py:444
  53.7 0.8 weight_fold.1
  54.5 11.0 %all-to-all-start = ((bf16[32,16,256]{2,1,0:T(8,128)(2,1)}), bf16[32,16,256]{2,1,0:T(8,128)(2,1)S(1)}, u32[]{:S(2)}, u32[]{:S(2)}) async-start(bf16[32,16,256]{2,1,0:T(8,128)(2,1)} %bitcast.9), calls=%async_computation | async-start | bytes 524288 | tf_op jit(solution)/shard_map/all_to_all | solution.py:489
  65.4 1.3 %collective-permute-start.8 = (bf16[128,1024]{1,0:T(8,128)(2,1)S(1)}, bf16[128,1024]{1,0:T(8,128)(2,1)S(1)}, u32[]{:S(2)}, u32[]{:S(2)}) collective-permute-start(bf16[128,1024]{1,0:T(8,128)(2,1)S(1)} %get-tuple-element.36), channel_id=1, source_target_pairs={{0,2},{1,3},{2,0},{3,1},{4,6},{5,7},{6,4},{7,5},{8,10},{9,11},{10,... | collective-permute-start | bytes 786440 | tf_op jit(solution)/shard_map/ppermute | solution.py:444
  66.8 11.4 %collective-permute-done.8.arrived_ref = bf16[128,1024]{1,0:T(8,128)(2,1)S(1)} collective-permute-done((bf16[128,1024]{1,0:T(8,128)(2,1)S(1)}, bf16[128,1024]{1,0:T(8,128)(2,1)S(1)}, u32[]{:S(2)}, u32[]{:S(2)}) %collective-permute-start.8) | collective-permute-done | bytes 262176 | tf_op jit(solution)/shard_map/ppermute | solution.py:444
  78.2 0.1 query_fold.1
  78.3 1.6 %collective-permute-start.9 = (bf16[128,512]{1,0:T(8,128)(2,1)S(1)}, bf16[128,512]{1,0:T(8,128)(2,1)S(1)}, u32[]{:S(2)}, u32[]{:S(2)}) collective-permute-start(bf16[128,512]{1,0:T(8,128)(2,1)S(1)} %get-tuple-element.38), channel_id=1, source_target_pairs={{0,1},{1,0},{2,3},{3,2},{4,5},{5,4},{6,7},{7,6},{8,9},{9,8},{10,11... | collective-permute-start | bytes 393224 | tf_op jit(solution)/shard_map/ppermute | solution.py:444
  79.9 1.0 %collective-permute-done.9.arrived_ref = bf16[128,512]{1,0:T(8,128)(2,1)S(1)} collective-permute-done((bf16[128,512]{1,0:T(8,128)(2,1)S(1)}, bf16[128,512]{1,0:T(8,128)(2,1)S(1)}, u32[]{:S(2)}, u32[]{:S(2)}) %collective-permute-start.9) | collective-permute-done | bytes 131104 | tf_op jit(solution)/shard_map/ppermute | solution.py:444
  80.9 0.9 %query_end.1 = bf16[128,512]{1,0:T(8,128)(2,1)} custom-call(f32[128,512]{1,0:T(8,128)S(1)} %get-tuple-element.37.mine_ref, bf16[128,512]{1,0:T(8,128)(2,1)S(1)} %collective-permute-done.9.arrived_ref, f32[512,128]{1,0:T(8,128)S(1)} %tables.1.tab_ref), custom_call_target="tpu_custom_call" | custom-call | flops 300000 | bytes 700000 | tf_op jit(solution)/shard_map/query_end/pallas_call | solution.py:362
  81.8 0.0 all-to-all-done
  81.8 0.7 convert_reduce_fusion
  (1 shorter events, 0.0 us)
Async XLA Ops:
  2.1 7.5 %collective-permute-start.3 = (bf16[128,1024]{1,0:T(8,128)(2,1)S(1)}, bf16[128,1024]{1,0:T(8,128)(2,1)S(1)}, u32[]{:S(2)}, u32[]{:S(2)}) collective-permute-start(bf16[128,1024]{1,0:T(8,128)(2,1)S(1)} %get-tuple-element.29.qg0), channel_id=1, source_target_pairs={{0,2},{1,3},{2,0},{3,1},{4,6},{5,7},{6,4},{7,5},{8,10},{9,11},{10,... | collective-permute-start | bytes 786440 | tf_op jit(solution)/shard_map/ppermute | solution.py:444
  4.7 16.4 %collective-permute-start.2 = (bf16[128,1024]{1,0:T(8,128)(2,1)S(1)}, bf16[128,1024]{1,0:T(8,128)(2,1)S(1)}, u32[]{:S(2)}, u32[]{:S(2)}) collective-permute-start(bf16[128,1024]{1,0:T(8,128)(2,1)S(1)} %get-tuple-element.29.qg0), channel_id=1, source_target_pairs={{0,1},{1,0},{2,3},{3,2},{4,5},{5,4},{6,7},{7,6},{8,9},{9,8},{10,11... | collective-permute-start | bytes 786440 | tf_op jit(solution)/shard_map/ppermute | solution.py:444
  9.7 11.4 %collective-permute-start.4 = (bf16[128,1024]{1,0:T(8,128)(2,1)S(1)}, bf16[128,1024]{1,0:T(8,128)(2,1)S(1)}, u32[]{:S(2)}, u32[]{:S(2)}) collective-permute-start(bf16[128,1024]{1,0:T(8,128)(2,1)S(1)} %collective-permute-done.3.qg2), channel_id=1, source_target_pairs={{0,1},{1,0},{2,3},{3,2},{4,5},{5,4},{6,7},{7,6},{8,9},{9,8},{10,11... | collective-permute-start | bytes 786440 | tf_op jit(solution)/shard_map/ppermute | solution.py:444
  12.3 25.9 %collective-permute-start.15 = (bf16[1536,128]{1,0:T(8,128)(2,1)S(1)}, bf16[1536,128]{1,0:T(8,128)(2,1)S(1)}, u32[]{:S(2)}, u32[]{:S(2)}) collective-permute-start(bf16[1536,128]{1,0:T(8,128)(2,1)S(1)} %get-tuple-element.45), channel_id=1, source_target_pairs={{0,12},{1,13},{2,14},{3,15},{4,0},{5,1},{6,2},{7,3},{8,4},{9,5},{1... | collective-permute-start | bytes 1179656 | tf_op jit(solution)/shard_map/ppermute | solution.py:444
  14.9 6.2 %collective-permute-start = (bf16[128,256]{1,0:T(8,128)(2,1)S(1)}, bf16[128,256]{1,0:T(8,128)(2,1)S(1)}, u32[]{:S(2)}, u32[]{:S(2)}) collective-permute-start(bf16[128,256]{1,0:T(8,128)(2,1)S(1)} %get-tuple-element.28.kv0), channel_id=1, source_target_pairs={{0,4},{1,5},{2,6},{3,7},{4,8},{5,9},{6,10},{7,11},{8,12},{9,13},{1... | collective-permute-start | bytes 196616 | tf_op jit(solution)/shard_map/ppermute | solution.py:444
  14.9 6.2 %collective-permute-start.1 = (bf16[128,256]{1,0:T(8,128)(2,1)S(1)}, bf16[128,256]{1,0:T(8,128)(2,1)S(1)}, u32[]{:S(2)}, u32[]{:S(2)}) collective-permute-start(bf16[128,256]{1,0:T(8,128)(2,1)S(1)} %get-tuple-element.28.kv0), channel_id=1, source_target_pairs={{0,8},{1,9},{2,10},{3,11},{4,12},{5,13},{6,14},{7,15},{8,0},{9,1},... | collective-permute-start | bytes 196616 | tf_op jit(solution)/shard_map/ppermute | solution.py:444
  23.0 8.6 %collective-permute-start.5 = (f32[4,2048]{1,0:T(4,128)S(1)}, f32[4,2048]{1,0:T(4,128)S(1)}, u32[]{:S(2)}, u32[]{:S(2)}) collective-permute-start(f32[4,2048]{1,0:T(4,128)S(1)} %get-tuple-element.34.st0), channel_id=1, source_target_pairs={{0,1},{1,0},{2,3},{3,2},{4,5},{5,4},{6,7},{7,6},{8,9},{9,8},{10,11... | collective-permute-start | bytes 98312 | tf_op jit(solution)/shard_map/ppermute | solution.py:444
  23.6 9.0 %collective-permute-start.6 = (f32[4,2048]{1,0:T(4,128)S(1)}, f32[4,2048]{1,0:T(4,128)S(1)}, u32[]{:S(2)}, u32[]{:S(2)}) collective-permute-start(f32[4,2048]{1,0:T(4,128)S(1)} %get-tuple-element.34.st0), channel_id=1, source_target_pairs={{0,2},{1,3},{2,0},{3,1},{4,6},{5,7},{6,4},{7,5},{8,10},{9,11},{10,... | collective-permute-start | bytes 98312 | tf_op jit(solution)/shard_map/ppermute | solution.py:444
  25.1 7.6 %collective-permute-start.7 = (f32[4,2048]{1,0:T(4,128)S(1)}, f32[4,2048]{1,0:T(4,128)S(1)}, u32[]{:S(2)}, u32[]{:S(2)}) collective-permute-start(f32[4,2048]{1,0:T(4,128)S(1)} %get-tuple-element.34.st0), channel_id=1, source_target_pairs={{0,3},{1,2},{2,1},{3,0},{4,7},{5,6},{6,5},{7,4},{8,11},{9,10},{10,... | collective-permute-start | bytes 98312 | tf_op jit(solution)/shard_map/ppermute | solution.py:444
  25.4 17.4 %collective-permute-start.13 = (bf16[1024,128]{1,0:T(8,128)(2,1)S(1)}, bf16[1024,128]{1,0:T(8,128)(2,1)S(1)}, u32[]{:S(2)}, u32[]{:S(2)}) collective-permute-start(bf16[1024,128]{1,0:T(8,128)(2,1)S(1)} %get-tuple-element.43), channel_id=1, source_target_pairs={{0,4},{1,5},{2,6},{3,7},{4,8},{5,9},{6,10},{7,11},{8,12},{9,13},{1... | collective-permute-start | bytes 786440 | tf_op jit(solution)/shard_map/ppermute | solution.py:444
  31.7 10.0 %collective-permute-start.14 = (bf16[512,128]{1,0:T(8,128)(2,1)S(1)}, bf16[512,128]{1,0:T(8,128)(2,1)S(1)}, u32[]{:S(2)}, u32[]{:S(2)}) collective-permute-start(bf16[512,128]{1,0:T(8,128)(2,1)S(1)} %get-tuple-element.44), channel_id=1, source_target_pairs={{0,8},{1,9},{2,10},{3,11},{4,12},{5,13},{6,14},{7,15},{8,0},{9,1},... | collective-permute-start | bytes 393224 | tf_op jit(solution)/shard_map/ppermute | solution.py:444
  34.3 14.9 %collective-permute-start.10 = (bf16[384,256]{1,0:T(8,128)(2,1)S(1)}, bf16[384,256]{1,0:T(8,128)(2,1)S(1)}, u32[]{:S(2)}, u32[]{:S(2)}) collective-permute-start(bf16[384,256]{1,0:T(8,128)(2,1)S(1)} %get-tuple-element.40), channel_id=1, source_target_pairs={{0,4},{1,5},{2,6},{3,7},{4,8},{5,9},{6,10},{7,11},{8,12},{9,13},{1... | collective-permute-start | bytes 589832 | tf_op jit(solution)/shard_map/ppermute | solution.py:444
  37.5 12.6 %collective-permute-start.11 = (bf16[384,256]{1,0:T(8,128)(2,1)S(1)}, bf16[384,256]{1,0:T(8,128)(2,1)S(1)}, u32[]{:S(2)}, u32[]{:S(2)}) collective-permute-start(bf16[384,256]{1,0:T(8,128)(2,1)S(1)} %get-tuple-element.40), channel_id=1, source_target_pairs={{0,8},{1,9},{2,10},{3,11},{4,12},{5,13},{6,14},{7,15},{8,0},{9,1},... | collective-permute-start | bytes 589832 | tf_op jit(solution)/shard_map/ppermute | solution.py:444
  38.2 11.9 %collective-permute-start.12 = (bf16[384,256]{1,0:T(8,128)(2,1)S(1)}, bf16[384,256]{1,0:T(8,128)(2,1)S(1)}, u32[]{:S(2)}, u32[]{:S(2)}) collective-permute-start(bf16[384,256]{1,0:T(8,128)(2,1)S(1)} %get-tuple-element.40), channel_id=1, source_target_pairs={{0,12},{1,13},{2,14},{3,15},{4,0},{5,1},{6,2},{7,3},{8,4},{9,5},{1... | collective-permute-start | bytes 589832 | tf_op jit(solution)/shard_map/ppermute | solution.py:444
  41.7 7.5 %collective-permute-start.16 = (bf16[512,128]{1,0:T(8,128)(2,1)S(1)}, bf16[512,128]{1,0:T(8,128)(2,1)S(1)}, u32[]{:S(2)}, u32[]{:S(2)}) collective-permute-start(bf16[512,128]{1,0:T(8,128)(2,1)S(1)} %slice.4), channel_id=1, source_target_pairs={{0,12},{1,13},{2,14},{3,15},{4,0},{5,1},{6,2},{7,3},{8,4},{9,5},{1... | collective-permute-start | bytes 393224 | tf_op jit(solution)/shard_map/ppermute | solution.py:444
  51.4 2.3 %collective-permute-start.17 = (bf16[512,256]{1,0:T(8,128)(2,1)S(1)}, bf16[512,256]{1,0:T(8,128)(2,1)S(1)}, u32[]{:S(2)}, u32[]{:S(2)}) collective-permute-start(bf16[512,256]{1,0:T(8,128)(2,1)S(1)} %get-tuple-element.49), channel_id=1, source_target_pairs={{0,1},{1,0},{2,3},{3,2},{4,5},{5,4},{6,7},{7,6},{8,9},{9,8},{10,11... | collective-permute-start | bytes 786440 | tf_op jit(solution)/shard_map/ppermute | solution.py:444
  54.5 27.3 %all-to-all-start = ((bf16[32,16,256]{2,1,0:T(8,128)(2,1)}), bf16[32,16,256]{2,1,0:T(8,128)(2,1)S(1)}, u32[]{:S(2)}, u32[]{:S(2)}) async-start(bf16[32,16,256]{2,1,0:T(8,128)(2,1)} %bitcast.9), calls=%async_computation | async-start | bytes 524288 | tf_op jit(solution)/shard_map/all_to_all | solution.py:489
  65.4 12.7 %collective-permute-start.8 = (bf16[128,1024]{1,0:T(8,128)(2,1)S(1)}, bf16[128,1024]{1,0:T(8,128)(2,1)S(1)}, u32[]{:S(2)}, u32[]{:S(2)}) collective-permute-start(bf16[128,1024]{1,0:T(8,128)(2,1)S(1)} %get-tuple-element.36), channel_id=1, source_target_pairs={{0,2},{1,3},{2,0},{3,1},{4,6},{5,7},{6,4},{7,5},{8,10},{9,11},{10,... | collective-permute-start | bytes 786440 | tf_op jit(solution)/shard_map/ppermute | solution.py:444
  78.3 2.6 %collective-permute-start.9 = (bf16[128,512]{1,0:T(8,128)(2,1)S(1)}, bf16[128,512]{1,0:T(8,128)(2,1)S(1)}, u32[]{:S(2)}, u32[]{:S(2)}) collective-permute-start(bf16[128,512]{1,0:T(8,128)(2,1)S(1)} %get-tuple-element.38), channel_id=1, source_target_pairs={{0,1},{1,0},{2,3},{3,2},{4,5},{5,4},{6,7},{7,6},{8,9},{9,8},{10,11... | collective-permute-start | bytes 393224 | tf_op jit(solution)/shard_map/ppermute | solution.py:444

commit v3 on v1

--- a/solution.py
+++ b/solution.py
@@ -18,6 +18,7 @@
 TN = (((0,), (0,)), ((), ()))
 NN = (((1,), (0,)), ((), ()))
 SCALE = B**-0.5
+LOG2E = 1.4426950408889634
 
 
 VMEM = pl.BlockSpec(memory_space=pltpu.VMEM)
@@ -157,80 +158,48 @@
     return start
 
 
-def unit_needed(rank, b, half, lows):
-    key_first = (rank - 4 * b) * B
-    query_first = (rank // 4 * 4 + 2 * half) * B
-    low = jnp.where(half == 0, lows[0], lows[1])
-    return (key_first <= query_first + 2 * B - 1) & (key_first + B > low)
-
-
-def half_lows(len_ref, rank):
-    return [document_start(len_ref, (rank // 4 * 4 + 2 * half) * B) for half in range(2)]
+def column_keys(kvs):
+    return jnp.concatenate([kv[:, :B] for kv in kvs], 0)
+
+
+def heads_below(ref, first):
+    return jnp.concatenate([ref[:, (first + h) * B : (first + h + 1) * B] for h in range(HEADS)], 0)
 
 
 def scores_kernel(
-    where_ref, len_ref, kv0, kv1, kv2, qg0, qg1, qg2, qg3,
-    p_ref, d_ref, q_ref, g_ref, stat_ref,
-    k_s, v_s, m_s, l_s, w_s, start_s,
+    where_ref, len_ref, kv0, kv1, kv2, qg0, qg1, qg2, qg3, p_ref, d_ref, stat_ref
 ):
     rank = where_ref[0]
     slab, col = rank // 4, rank % 4
-    lows = half_lows(len_ref, rank)
-    for b, ref in enumerate((kv0, kv1, kv2)):
-        k_s[b * B : (b + 1) * B, :] = ref[:, :B]
-        v_s[b * B : (b + 1) * B, :] = ref[:, B:]
+    keys = column_keys((kv0, kv1, kv2))
+    values = jnp.concatenate([kv[:, B:] for kv in (kv0, kv1, kv2)], 0)
+    row = lax.broadcasted_iota(jnp.int32, (B, B), 0)
     for source, ref in enumerate((qg0, qg1, qg2, qg3)):
-        column = col ^ source
-        for h in range(HEADS):
-            at = rows(column // 2 * 8 + h * 2 + column % 2)
-            q_ref[at, :] = ref[:, h * B : (h + 1) * B]
-            g_ref[at, :] = ref[:, (HEADS + h) * B : (HEADS + h + 1) * B]
-    m_s[...] = jnp.full(m_s.shape, NEG, jnp.float32)
-    l_s[...] = jnp.zeros(l_s.shape, jnp.float32)
-    w_s[...] = jnp.zeros(w_s.shape, jnp.float32)
-    start_s[...] = document_start(
-        len_ref, slab * 4 * B + lax.broadcasted_iota(jnp.int32, (1, 4 * B), 1)
-    )
-
-    def first_pass(unit, carry):
-        b, half = unit // 2, unit % 2
-
-        @pl.when(unit_needed(rank, b, half, lows))
-        def _():
-            keys, queries = rows(b), rows(half, HALF)
-            s = dot(k_s[keys, :], q_ref[queries, :], NT) * SCALE
-            d_ref[keys, queries] = dot(v_s[keys, :], g_ref[queries, :], NT)
-            key_pos = (rank - 4 * b) * B + lax.broadcasted_iota(jnp.int32, (B, 2 * B), 0)
-            query_pos = (slab * 4 + 2 * half) * B + lax.broadcasted_iota(jnp.int32, (1, 2 * B), 1)
-            allowed = (key_pos <= query_pos) & (key_pos >= start_s[:, rows(half, 2 * B)])
-            for h in range(HEADS):
-                lanes = rows(half * HEADS + h, 2 * B)
-                part = jnp.where(allowed, s[:, h * 2 * B : (h + 1) * 2 * B], NEG)
-                p_ref[keys, lanes] = part
-                m_s[:, lanes] = jnp.maximum(m_s[:, lanes], jnp.max(part.reshape(16, 8, 2 * B), axis=0))
-
-        return carry
-
-    lax.fori_loop(0, 6, first_pass, 0)
-    top = jnp.max(m_s[...], axis=0, keepdims=True)
-    stat_ref[0:1, :] = top
-
-    def second_pass(unit, carry):
-        b, half = unit // 2, unit % 2
-
-        @pl.when(unit_needed(rank, b, half, lows))
-        def _():
-            keys, queries = rows(b), rows(half, HALF)
-            p = jnp.exp(p_ref[keys, queries] - stat_ref[0:1, queries])
-            p_ref[keys, queries] = p
-            l_s[:, queries] += jnp.sum(p.reshape(16, 8, HALF), axis=0)
-            w_s[:, queries] += jnp.sum((p * d_ref[keys, queries]).reshape(16, 8, HALF), axis=0)
-
-        return carry
-
-    lax.fori_loop(0, 6, second_pass, 0)
-    stat_ref[1:2, :] = jnp.sum(l_s[...], axis=0, keepdims=True)
-    stat_ref[2:3, :] = jnp.sum(w_s[...], axis=0, keepdims=True)
+        position = (slab * 4 + (col ^ source)) * B + lax.broadcasted_iota(jnp.int32, (1, B), 1)
+        start = document_start(len_ref, position)
+        allowed = jnp.concatenate(
+            [
+                (row <= position - (rank - 4 * b) * B) & (row >= start - (rank - 4 * b) * B)
+                for b in range(3)
+            ],
+            0,
+        )
+        queries, grads = heads_below(ref, 0), heads_below(ref, HEADS)
+        for pair in range(2):
+            part = slice(pair * 2 * B, (pair + 1) * 2 * B)
+            s = dot(keys, queries[part], NT)
+            d = dot(values, grads[part], NT)
+            for h in range(2):
+                here = slice(h * B, (h + 1) * B)
+                lanes = slice((source * HEADS + pair * 2 + h) * B, (source * HEADS + pair * 2 + h + 1) * B)
+                masked = jnp.where(allowed, s[:, here], NEG)
+                top = jnp.max(masked, axis=0, keepdims=True)
+                p = jnp.exp2((masked - top) * (SCALE * LOG2E))
+                p_ref[:, lanes] = p
+                d_ref[:, lanes] = d[:, here]
+                stat_ref[0:1, lanes] = top
+                stat_ref[1:2, lanes] = jnp.sum(p, axis=0, keepdims=True)
+                stat_ref[2:3, lanes] = jnp.sum(p * d[:, here], axis=0, keepdims=True)
     stat_ref[3:4, :] = jnp.zeros((1, 2 * HALF), jnp.float32)
 
 
@@ -241,20 +210,10 @@
         out_shape=(
             shape(wide, jnp.float32),
             shape(wide, jnp.float32),
-            shape((2 * HALF, B), jnp.bfloat16),
-            shape((2 * HALF, B), jnp.bfloat16),
             shape((4, 2 * HALF), jnp.float32),
         ),
         in_specs=[SMEM, SMEM] + [VMEM] * 7,
-        out_specs=(VMEM,) * 5,
-        scratch_shapes=[
-            pltpu.VMEM((3 * B, B), jnp.bfloat16),
-            pltpu.VMEM((3 * B, B), jnp.bfloat16),
-            pltpu.VMEM((8, 2 * HALF), jnp.float32),
-            pltpu.VMEM((8, 2 * HALF), jnp.float32),
-            pltpu.VMEM((8, 2 * HALF), jnp.float32),
-            pltpu.VMEM((1, 4 * B), jnp.int32),
-        ],
+        out_specs=(VMEM,) * 3,
         compiler_params=pltpu.CompilerParams(vmem_limit_bytes=20 * MIB),
         cost_estimate=pl.CostEstimate(flops=400_000_000, bytes_accessed=8_000_000, transcendentals=790_000),
         name="scores",
@@ -262,122 +221,87 @@
 
 
 def gradients_kernel(
-    where_ref, len_ref, kv0, kv1, kv2, p_ref, d_ref, q_ref, g_ref, st0, st1, st2, st3,
-    keep_ref, send_ref, dq_keep_ref, dq_send_ref,
-    k_s, dq_s, f_s, delta_s,
+    kv0, kv1, kv2, p_ref, d_ref, qg0, qg1, qg2, qg3, st0, st1, st2, st3,
+    keep_ref, send_ref, dq0, dq1, dq2, dq3,
 ):
-    rank = where_ref[0]
-    lows = half_lows(len_ref, rank)
-    for b, ref in enumerate((kv0, kv1, kv2)):
-        k_s[b * B : (b + 1) * B, :] = ref[:, :B]
-    tops = [st[0:1, :] for st in (st0, st1, st2, st3)]
-    top = jnp.maximum(jnp.maximum(tops[0], tops[1]), jnp.maximum(tops[2], tops[3]))
-    factors = [jnp.exp(t - top) for t in tops]
-    total = sum(st[1:2, :] * f for st, f in zip((st0, st1, st2, st3), factors))
-    weighted = sum(st[2:3, :] * f for st, f in zip((st0, st1, st2, st3), factors))
-    inverse = 1.0 / total
-    f_s[...] = factors[0] * inverse
-    delta_s[...] = weighted * inverse
-    keep_ref[...] = jnp.zeros(keep_ref.shape, jnp.float32)
-    dq_s[...] = jnp.zeros(dq_s.shape, jnp.float32)
-
-    def one_pass(unit, carry):
-        b, half = unit // 2, unit % 2
-
-        @pl.when(unit_needed(rank, b, half, lows))
-        def _():
-            keys, queries = rows(b), rows(half, HALF)
-            p = p_ref[keys, queries] * f_s[:, queries]
-            ds = (p * (d_ref[keys, queries] - delta_s[:, queries])).astype(jnp.bfloat16)
-            keep_ref[keys, B:] += dot(p.astype(jnp.bfloat16), g_ref[queries, :], NN)
-            keep_ref[keys, :B] += dot(ds, q_ref[queries, :], NN) * SCALE
-            dq_s[:, queries] += dot(k_s[keys, :], ds, TN)
-
-        return carry
-
-    lax.fori_loop(0, 6, one_pass, 0)
-    send_ref[...] = keep_ref[...].astype(jnp.bfloat16)
-    z = rank % 4 // 2
-    dq_keep_ref[...] = dq_s[:, rows(z, HALF)]
-    dq_send_ref[...] = dq_s[:, rows(1 - z, HALF)].astype(jnp.bfloat16)
-
-
-def gradients(rank, lengths, kvs, p, d, q, g, stats):
+    keys = column_keys((kv0, kv1, kv2))
+    dk = dv = None
+    for source, (ref, out) in enumerate(zip((qg0, qg1, qg2, qg3), (dq0, dq1, dq2, dq3))):
+        seen = [
+            st[:, (source ^ bits) * HEADS * B : ((source ^ bits) + 1) * HEADS * B]
+            for bits, st in enumerate((st0, st1, st2, st3))
+        ]
+        top = jnp.maximum(
+            jnp.maximum(seen[0][0:1], seen[1][0:1]), jnp.maximum(seen[2][0:1], seen[3][0:1])
+        )
+        factors = [jnp.exp2((st[0:1] - top) * (SCALE * LOG2E)) for st in seen]
+        inverse = 1.0 / sum(st[1:2] * f for st, f in zip(seen, factors))
+        delta = sum(st[2:3] * f for st, f in zip(seen, factors)) * inverse
+        lanes = slice(source * HEADS * B, (source + 1) * HEADS * B)
+        p = p_ref[:, lanes] * (factors[0] * inverse)
+        ds = (p * (d_ref[:, lanes] - delta)).astype(jnp.bfloat16)
+        more_v = dot(p.astype(jnp.bfloat16), heads_below(ref, HEADS), NN)
+        more_k = dot(ds, heads_below(ref, 0), NN)
+        dv = more_v if dv is None else dv + more_v
+        dk = more_k if dk is None else dk + more_k
+        out[...] = dot(keys, ds, TN).astype(out.dtype)
+    dk = dk * SCALE
+    keep_ref[:, :B] = dk
+    keep_ref[:, B:] = dv
+    send_ref[:, :B] = dk.astype(jnp.bfloat16)
+    send_ref[:, B:] = dv.astype(jnp.bfloat16)
+
+
+def gradients(kvs, p, d, qgs, stats):
     return pl.pallas_call(
         gradients_kernel,
         out_shape=(
             shape((3 * B, 2 * B), jnp.float32),
             shape((3 * B, 2 * B), jnp.bfloat16),
-            shape((B, HALF), jnp.float32),
-            shape((B, HALF), jnp.bfloat16),
+            shape((B, HEADS * B), jnp.float32),
+            shape((B, HEADS * B), jnp.bfloat16),
+            shape((B, HEADS * B), jnp.bfloat16),
+            shape((B, HEADS * B), jnp.bfloat16),
         ),
-        in_specs=[SMEM, SMEM] + [VMEM] * 11,
-        out_specs=(VMEM,) * 4,
-        scratch_shapes=[
-            pltpu.VMEM((3 * B, B), jnp.bfloat16),
-            pltpu.VMEM((B, 2 * HALF), jnp.float32),
-            pltpu.VMEM((1, 2 * HALF), jnp.float32),
-            pltpu.VMEM((1, 2 * HALF), jnp.float32),
-        ],
+        in_specs=[VMEM] * 13,
+        out_specs=(VMEM,) * 6,
         compiler_params=pltpu.CompilerParams(vmem_limit_bytes=20 * MIB),
         cost_estimate=pl.CostEstimate(flops=600_000_000, bytes_accessed=8_000_000, transcendentals=8_000),
         name="gradients",
-    )(rank, lengths, *kvs, p, d, q, g, *stats)
-
-
-def query_fold_kernel(where_ref, keep_ref, arrived_ref, mine_ref, send_ref):
-    core = where_ref[0] % 2
-    for h in range(HEADS):
-        part = slice(h * B, (h + 1) * B)
-        mine, other = rows(h * 2 + core), rows(h * 2 + 1 - core)
-        mine_ref[:, part] = keep_ref[:, mine] + arrived_ref[:, mine].astype(jnp.float32)
-        both = keep_ref[:, other] + arrived_ref[:, other].astype(jnp.float32)
-        send_ref[:, part] = both.astype(jnp.bfloat16)
-
-
-def query_fold(rank, keep, arrived):
-    return pl.pallas_call(
-        query_fold_kernel,
-        out_shape=(shape((B, HEADS * B), jnp.float32), shape((B, HEADS * B), jnp.bfloat16)),
-        in_specs=[SMEM, VMEM, VMEM],
-        out_specs=(VMEM, VMEM),
-        compiler_params=pltpu.CompilerParams(vmem_limit_bytes=4 * MIB),
-        cost_estimate=pl.CostEstimate(flops=300_000, bytes_accessed=1_200_000, transcendentals=0),
-        name="query_fold",
-    )(rank, keep, arrived)
-
-
-def query_end_kernel(mine_ref, arrived_ref, tab_ref, out_ref):
+    )(*kvs, p, d, *qgs, *stats)
+
+
+def query_end_kernel(mine_ref, r1, r2, r3, tab_ref, out_ref):
     cosine, sine = split_table(tab_ref[:B, :])
     for h in range(HEADS):
         part = slice(h * B, (h + 1) * B)
-        u = (mine_ref[:, part] + arrived_ref[:, part].astype(jnp.float32)).T * SCALE
-        out_ref[:, part] = rotated(u, cosine, -sine).astype(jnp.bfloat16)
+        u = mine_ref[:, part]
+        for ref in (r1, r2, r3):
+            u = u + ref[:, part].astype(jnp.float32)
+        out_ref[:, part] = rotated(u.T * SCALE, cosine, -sine).astype(jnp.bfloat16)
 
 
 def query_end(mine, arrived, table):
     return pl.pallas_call(
         query_end_kernel,
         out_shape=shape((B, HEADS * B), jnp.bfloat16),
-        in_specs=[VMEM, VMEM, VMEM],
+        in_specs=[VMEM] * 5,
         out_specs=VMEM,
         compiler_params=pltpu.CompilerParams(vmem_limit_bytes=4 * MIB),
-        cost_estimate=pl.CostEstimate(flops=300_000, bytes_accessed=700_000, transcendentals=0),
+        cost_estimate=pl.CostEstimate(flops=300_000, bytes_accessed=900_000, transcendentals=0),
         name="query_end",
-    )(mine, arrived, table)
+    )(mine, *arrived, table)
 
 
 def weight_kernel(
-    where_ref, keep_ref, r1, r2k, r2v, r3, tab_ref, x0, x1, x2, x3,
+    where_ref, keep_ref, r1, r2, r3, tab_ref, x0, x1, x2, x3,
     key_ref, value_ref, own_ref, send_ref, acc,
 ):
     core = where_ref[0] % 2
 
     def part(source, b, lanes):
         at = slice(b * B, (b + 1) * B)
-        if source == 2:
-            return (r2k, r2v)[lanes][at, :].astype(jnp.float32)
-        ref = (keep_ref, r1, None, r3)[source]
+        ref = (keep_ref, r1, r2, r3)[source]
         return ref[at, lanes * B : (lanes + 1) * B].astype(jnp.float32)
 
     grads = []
@@ -410,7 +334,7 @@
             shape((512, 256), jnp.float32),
             shape((512, 256), jnp.bfloat16),
         ),
-        in_specs=[SMEM] + [VMEM] * 10,
+        in_specs=[SMEM] + [VMEM] * 9,
         out_specs=(VMEM,) * 4,
         scratch_shapes=[pltpu.VMEM((1024, 256), jnp.float32)],
         compiler_params=pltpu.CompilerParams(vmem_limit_bytes=12 * MIB),
@@ -464,17 +388,15 @@
     xs = slices(where, x)
     xs = [xs[0]] + [around(xs[k], k) for k in (1, 2, 3)]
 
-    p, d, q, g, stat = scores(where, lengths, kvs, (qg, qg_c, qg_z, qg_cz))
+    qgs = (qg, qg_c, qg_z, qg_cz)
+    p, d, stat = scores(where, lengths, kvs, qgs)
     stats = [stat] + [swap(stat, bits) for bits in (1, 2, 3)]
     table = tables(where)
-    keep, send, dq_keep, dq_send = gradients(where, lengths, kvs, p, d, q, g, stats)
-
-    one, three = around(send, 1), around(send, 3)
-    arrived = [one, around(one[:, :B], 1), around(three[:, B:], 3), three]
-    dq_z = swap(dq_send, 2)
-    dq_mine, dq_send = query_fold(where, dq_keep, dq_z)
-    dq_c = swap(dq_send, 1)
-    query_grad = query_end(dq_mine, dq_c, table)
+    keep, send, mine, *others = gradients(kvs, p, d, qgs, stats)
+
+    arrived = [around(send, k) for k in (1, 2, 3)]
+    query_parts = [swap(part, bits) for bits, part in zip((1, 2, 3), others)]
+    query_grad = query_end(mine, query_parts, table)
 
     key_grad, value_grad, own, send = weight_part(where, keep, arrived, table, xs)
     arrived = swap(send, 1)

time: 81.9 us -> 80.2 us (0.979)
  starting transfers between devices: 35.9 us -> 30 us
  waiting for transfers between devices: 34.9 us -> 39.2 us
    ppermute x18, starting transfers between devices: 25.3 us -> 19 us  [permute(): return lax.ppermute(array, 'ctx', pairs)]
    ppermute x18, waiting for transfers between devices: 34.9 us -> 39.2 us  [permute(): return lax.ppermute(array, 'ctx', pairs)]
  transfers between devices with their start and end apart: 19 -> 19, of which waited for: 14 -> 13; matrix products, arithmetic and copies ran while one was open for 0% -> 0% of each run, Pallas kernels for 3% -> 7%
where the time goes in v3:
time: 80.2 us; the launch traced here: 80.1 us
  waiting for transfers between devices  39.2 us (49%)
  starting transfers between devices  30 us (37%)
  Pallas kernels  9.49 us (12%)
    ppermute x18, waiting for transfers between devices, permute(): return lax.ppermute(array, 'ctx', pairs)  39.2 us
    ppermute x18, starting transfers between devices, permute(): return lax.ppermute(array, 'ctx', pairs)  19 us
    all_to_all x1, starting transfers between devices, compute(): lax.all_to_all(blocks, ('dp', 'ctx'), split_axis=0, concat_axis=0, tiled=...  11 us
    pallas_call x1, Pallas kernels, scores(): pl.pallas_call(scores_kernel, out_shape=(shape(wide, jnp.float32), shape(...  2.23 us
  transfers between devices with their start and end apart: 19, of which 13 were waited for; matrix products, arithmetic and copies ran while one was open for 0% of the time, Pallas kernels for 7%

profile of v3, /device:TPU:1, one launch (start us, length us, event | category | flops | bytes accessed | tf_op | source)
XLA Modules:
  0.0 80.1 jit_solution(1562208276310072731)
XLA Ops:
  0.6 1.5 %prepare.1 = (bf16[128,256]{1,0:T(8,128)(2,1)S(1)}, bf16[128,1024]{1,0:T(8,128)(2,1)S(1)}, bf16[128,4096]{1,0:T(8,128)(2,1)S(1)}, s32[1,8]{1,0:T(1,128)S(1)}) custom-call(s32[1]{0:T(128)} %bitcast.where_ref, bf16[128,128]{1,0:T(8,128)(2,1)} %bitcast.14, bf16[128,128]{1,0:T(8,128)(2,1)} %bitcast.15, bf16[128,512]{1,0:T(8,128)(2,1)} %bitcast.11, ...), custom_call_target="tpu_custom_call" | custom-call | tf_op jit(solution)/shard_map/prepare/pallas_call | solution.py:91
  2.1 2.5 %collective-permute-start.3 = (bf16[128,1024]{1,0:T(8,128)(2,1)S(1)}, bf16[128,1024]{1,0:T(8,128)(2,1)S(1)}, u32[]{:S(2)}, u32[]{:S(2)}) collective-permute-start(bf16[128,1024]{1,0:T(8,128)(2,1)S(1)} %get-tuple-element.27.qg0), channel_id=1, source_target_pairs={{0,2},{1,3},{2,0},{3,1},{4,6},{5,7},{6,4},{7,5},{8,10},{9,11},{10,... | collective-permute-start | bytes 786440 | tf_op jit(solution)/shard_map/ppermute | solution.py:366
  4.7 1.0 %collective-permute-start.2 = (bf16[128,1024]{1,0:T(8,128)(2,1)S(1)}, bf16[128,1024]{1,0:T(8,128)(2,1)S(1)}, u32[]{:S(2)}, u32[]{:S(2)}) collective-permute-start(bf16[128,1024]{1,0:T(8,128)(2,1)S(1)} %get-tuple-element.27.qg0), channel_id=1, source_target_pairs={{0,1},{1,0},{2,3},{3,2},{4,5},{5,4},{6,7},{7,6},{8,9},{9,8},{10,11... | collective-permute-start | bytes 786440 | tf_op jit(solution)/shard_map/ppermute | solution.py:366
  5.6 4.0 %collective-permute-done.3.qg2 = bf16[128,1024]{1,0:T(8,128)(2,1)S(1)} collective-permute-done((bf16[128,1024]{1,0:T(8,128)(2,1)S(1)}, bf16[128,1024]{1,0:T(8,128)(2,1)S(1)}, u32[]{:S(2)}, u32[]{:S(2)}) %collective-permute-start.3) | collective-permute-done | bytes 262176 | tf_op jit(solution)/shard_map/ppermute | solution.py:366
  9.7 2.3 %collective-permute-start.4 = (bf16[128,1024]{1,0:T(8,128)(2,1)S(1)}, bf16[128,1024]{1,0:T(8,128)(2,1)S(1)}, u32[]{:S(2)}, u32[]{:S(2)}) collective-permute-start(bf16[128,1024]{1,0:T(8,128)(2,1)S(1)} %collective-permute-done.3.qg2), channel_id=1, source_target_pairs={{0,1},{1,0},{2,3},{3,2},{4,5},{5,4},{6,7},{7,6},{8,9},{9,8},{10,11... | collective-permute-start | bytes 786440 | tf_op jit(solution)/shard_map/ppermute | solution.py:366
  11.9 0.4 slices.1
  12.3 1.3 %collective-permute-start.14 = (bf16[1024,128]{1,0:T(8,128)(2,1)S(1)}, bf16[1024,128]{1,0:T(8,128)(2,1)S(1)}, u32[]{:S(2)}, u32[]{:S(2)}) collective-permute-start(bf16[1024,128]{1,0:T(8,128)(2,1)S(1)} %get-tuple-element.39), channel_id=1, source_target_pairs={{0,4},{1,5},{2,6},{3,7},{4,8},{5,9},{6,10},{7,11},{8,12},{9,13},{1... | collective-permute-start | bytes 786440 | tf_op jit(solution)/shard_map/ppermute | solution.py:366
  13.6 1.2 %collective-permute-start = (bf16[128,256]{1,0:T(8,128)(2,1)S(1)}, bf16[128,256]{1,0:T(8,128)(2,1)S(1)}, u32[]{:S(2)}, u32[]{:S(2)}) collective-permute-start(bf16[128,256]{1,0:T(8,128)(2,1)S(1)} %get-tuple-element.25.kv0), channel_id=1, source_target_pairs={{0,4},{1,5},{2,6},{3,7},{4,8},{5,9},{6,10},{7,11},{8,12},{9,13},{1... | collective-permute-start | bytes 196616 | tf_op jit(solution)/shard_map/ppermute | solution.py:366
  14.8 1.4 %collective-permute-start.1 = (bf16[128,256]{1,0:T(8,128)(2,1)S(1)}, bf16[128,256]{1,0:T(8,128)(2,1)S(1)}, u32[]{:S(2)}, u32[]{:S(2)}) collective-permute-start(bf16[128,256]{1,0:T(8,128)(2,1)S(1)} %get-tuple-element.25.kv0), channel_id=1, source_target_pairs={{0,8},{1,9},{2,10},{3,11},{4,12},{5,13},{6,14},{7,15},{8,0},{9,1},... | collective-permute-start | bytes 196616 | tf_op jit(solution)/shard_map/ppermute | solution.py:366
  16.3 6.6 %collective-permute-done.kv1 = bf16[128,256]{1,0:T(8,128)(2,1)S(1)} collective-permute-done((bf16[128,256]{1,0:T(8,128)(2,1)S(1)}, bf16[128,256]{1,0:T(8,128)(2,1)S(1)}, u32[]{:S(2)}, u32[]{:S(2)}) %collective-permute-start) | collective-permute-done | bytes 65568 | tf_op jit(solution)/shard_map/ppermute | solution.py:366
  22.9 2.4 %collective-permute-done.1.kv2 = bf16[128,256]{1,0:T(8,128)(2,1)S(1)} collective-permute-done((bf16[128,256]{1,0:T(8,128)(2,1)S(1)}, bf16[128,256]{1,0:T(8,128)(2,1)S(1)}, u32[]{:S(2)}, u32[]{:S(2)}) %collective-permute-start.1) | collective-permute-done | bytes 65568 | tf_op jit(solution)/shard_map/ppermute | solution.py:366
  25.3 0.0 collective-permute-done.2.qg1
  25.3 0.0 collective-permute-done.4.qg3
  25.3 2.2 %scores.1 = (f32[384,2048]{1,0:T(8,128)S(1)}, f32[384,2048]{1,0:T(8,128)S(1)}, f32[4,2048]{1,0:T(4,128)S(1)}) custom-call(s32[1]{0:T(128)} %bitcast.where_ref, s32[1,8]{1,0:T(1,128)S(1)} %get-tuple-element.26.len_ref, bf16[128,256]{1,0:T(8,128)(2,1)S(1)} %get-tuple-element.25.kv0, bf16[128,256]{1,0:T(8,128)(2,1)S(1)} %collective-permute-done.kv1, ...), custom_call_target="tpu_custom_call" | custom-call | flops 400000000 | bytes 8000000 | tf_op jit(solution)/shard_map/scores/pallas_call | solution.py:208
  27.5 0.9 %collective-permute-start.5 = (f32[4,2048]{1,0:T(4,128)S(1)}, f32[4,2048]{1,0:T(4,128)S(1)}, u32[]{:S(2)}, u32[]{:S(2)}) collective-permute-start(f32[4,2048]{1,0:T(4,128)S(1)} %get-tuple-element.30.st0), channel_id=1, source_target_pairs={{0,1},{1,0},{2,3},{3,2},{4,5},{5,4},{6,7},{7,6},{8,9},{9,8},{10,11... | collective-permute-start | bytes 98312 | tf_op jit(solution)/shard_map/ppermute | solution.py:366
  28.5 1.5 %collective-permute-start.6 = (f32[4,2048]{1,0:T(4,128)S(1)}, f32[4,2048]{1,0:T(4,128)S(1)}, u32[]{:S(2)}, u32[]{:S(2)}) collective-permute-start(f32[4,2048]{1,0:T(4,128)S(1)} %get-tuple-element.30.st0), channel_id=1, source_target_pairs={{0,2},{1,3},{2,0},{3,1},{4,6},{5,7},{6,4},{7,5},{8,10},{9,11},{10,... | collective-permute-start | bytes 98312 | tf_op jit(solution)/shard_map/ppermute | solution.py:366
  29.9 0.3 collective-permute-start.7
  30.2 0.5 collective-permute-start.15
  30.7 0.0 collective-permute-done.5.st1
  30.7 0.0 collective-permute-start.16
  30.8 0.5 collective-permute-done.6.st2
  31.2 2.1 %collective-permute-done.7.st3 = f32[4,2048]{1,0:T(4,128)S(1)} collective-permute-done((f32[4,2048]{1,0:T(4,128)S(1)}, f32[4,2048]{1,0:T(4,128)S(1)}, u32[]{:S(2)}, u32[]{:S(2)}) %collective-permute-start.7) | collective-permute-done | bytes 32800 | tf_op jit(solution)/shard_map/ppermute | solution.py:366
  33.3 1.4 %gradients.1 = (f32[384,256]{1,0:T(8,128)S(1)}, bf16[384,256]{1,0:T(8,128)(2,1)S(1)}, f32[128,512]{1,0:T(8,128)S(1)}, bf16[128,512]{1,0:T(8,128)(2,1)S(1)}, bf16...) custom-call(bf16[128,256]{1,0:T(8,128)(2,1)S(1)} %get-tuple-element.25.kv0, ...), custom_call_target="tpu_custom_call" | custom-call | flops 600000000 | bytes 8000000 | tf_op jit(solution)/shard_map/gradients/pallas_call | solution.py:256
  34.7 0.1 collective-permute-start.11
  34.8 1.3 %collective-permute-start.12 = (bf16[384,256]{1,0:T(8,128)(2,1)S(1)}, bf16[384,256]{1,0:T(8,128)(2,1)S(1)}, u32[]{:S(2)}, u32[]{:S(2)}) collective-permute-start(bf16[384,256]{1,0:T(8,128)(2,1)S(1)} %get-tuple-element.36), channel_id=1, source_target_pairs={{0,8},{1,9},{2,10},{3,11},{4,12},{5,13},{6,14},{7,15},{8,0},{9,1},... | collective-permute-start | bytes 589832 | tf_op jit(solution)/shard_map/ppermute | solution.py:366
  36.1 0.0 collective-permute-done.14.x1
  36.1 1.3 %collective-permute-start.13 = (bf16[384,256]{1,0:T(8,128)(2,1)S(1)}, bf16[384,256]{1,0:T(8,128)(2,1)S(1)}, u32[]{:S(2)}, u32[]{:S(2)}) collective-permute-start(bf16[384,256]{1,0:T(8,128)(2,1)S(1)} %get-tuple-element.36), channel_id=1, source_target_pairs={{0,12},{1,13},{2,14},{3,15},{4,0},{5,1},{6,2},{7,3},{8,4},{9,5},{1... | collective-permute-start | bytes 589832 | tf_op jit(solution)/shard_map/ppermute | solution.py:366
  37.5 1.0 %tables.1.tab_ref = f32[512,128]{1,0:T(8,128)S(1)} custom-call(s32[1]{0:T(128)} %bitcast.where_ref), custom_call_target="tpu_custom_call" | custom-call | flops 2000000 | bytes 260000 | tf_op jit(solution)/shard_map/tables/pallas_call | solution.py:141
  38.5 0.9 %collective-permute-done.15.x2 = bf16[1024,128]{1,0:T(8,128)(2,1)S(1)} collective-permute-done((bf16[1024,128]{1,0:T(8,128)(2,1)S(1)}, bf16[1024,128]{1,0:T(8,128)(2,1)S(1)}, u32[]{:S(2)}, u32[]{:S(2)}) %collective-permute-start.15) | collective-permute-done | bytes 262176 | tf_op jit(solution)/shard_map/ppermute | solution.py:366
  39.4 2.6 %collective-permute-done.16.x3 = bf16[1024,128]{1,0:T(8,128)(2,1)S(1)} collective-permute-done((bf16[1024,128]{1,0:T(8,128)(2,1)S(1)}, bf16[1024,128]{1,0:T(8,128)(2,1)S(1)}, u32[]{:S(2)}, u32[]{:S(2)}) %collective-permute-start.16) | collective-permute-done | bytes 262176 | tf_op jit(solution)/shard_map/ppermute | solution.py:366
  42.0 2.6 %collective-permute-done.11.r1 = bf16[384,256]{1,0:T(8,128)(2,1)S(1)} collective-permute-done((bf16[384,256]{1,0:T(8,128)(2,1)S(1)}, bf16[384,256]{1,0:T(8,128)(2,1)S(1)}, u32[]{:S(2)}, u32[]{:S(2)}) %collective-permute-start.11) | collective-permute-done | bytes 196640 | tf_op jit(solution)/shard_map/ppermute | solution.py:366
  44.7 3.2 %collective-permute-done.12.r2 = bf16[384,256]{1,0:T(8,128)(2,1)S(1)} collective-permute-done((bf16[384,256]{1,0:T(8,128)(2,1)S(1)}, bf16[384,256]{1,0:T(8,128)(2,1)S(1)}, u32[]{:S(2)}, u32[]{:S(2)}) %collective-permute-start.12) | collective-permute-done | bytes 196640 | tf_op jit(solution)/shard_map/ppermute | solution.py:366
  47.9 2.7 %collective-permute-done.13.r3 = bf16[384,256]{1,0:T(8,128)(2,1)S(1)} collective-permute-done((bf16[384,256]{1,0:T(8,128)(2,1)S(1)}, bf16[384,256]{1,0:T(8,128)(2,1)S(1)}, u32[]{:S(2)}, u32[]{:S(2)}) %collective-permute-start.13) | collective-permute-done | bytes 196640 | tf_op jit(solution)/shard_map/ppermute | solution.py:366
  50.5 1.3 %weight.1 = (bf16[128,128]{1,0:T(8,128)(2,1)}, bf16[128,128]{1,0:T(8,128)(2,1)}, f32[512,256]{1,0:T(8,128)S(1)}, bf16[512,256]{1,0:T(8,128)(2,1)S(1)}) custom-call(s32[1]{0:T(128)} %bitcast.where_ref, f32[384,256]{1,0:T(8,128)S(1)} %get-tuple-element.35.keep_ref, bf16[384,256]{1,0:T(8,128)(2,1)S(1)} %collective-permute-done.11.r1, ...), custom_call_target="tpu_custom_call" | custom-call | flops 268000000 | bytes 3000000 | tf_op jit(solution)/shard_map/weight/pallas_call | solution.py:329
  51.8 1.0 %collective-permute-start.17 = (bf16[512,256]{1,0:T(8,128)(2,1)S(1)}, bf16[512,256]{1,0:T(8,128)(2,1)S(1)}, u32[]{:S(2)}, u32[]{:S(2)}) collective-permute-start(bf16[512,256]{1,0:T(8,128)(2,1)S(1)} %get-tuple-element.45), channel_id=1, source_target_pairs={{0,1},{1,0},{2,3},{3,2},{4,5},{5,4},{6,7},{7,6},{8,9},{9,8},{10,11... | collective-permute-start | bytes 786440 | tf_op jit(solution)/shard_map/ppermute | solution.py:366
  52.8 1.2 %collective-permute-done.17.arrived_ref = bf16[512,256]{1,0:T(8,128)(2,1)S(1)} collective-permute-done((bf16[512,256]{1,0:T(8,128)(2,1)S(1)}, bf16[512,256]{1,0:T(8,128)(2,1)S(1)}, u32[]{:S(2)}, u32[]{:S(2)}) %collective-permute-start.17) | collective-permute-done | bytes 262176 | tf_op jit(solution)/shard_map/ppermute | solution.py:366
  54.0 0.8 weight_fold.1
  54.8 11.0 %all-to-all-start = ((bf16[32,16,256]{2,1,0:T(8,128)(2,1)}), bf16[32,16,256]{2,1,0:T(8,128)(2,1)S(1)}, u32[]{:S(2)}, u32[]{:S(2)}) async-start(bf16[32,16,256]{2,1,0:T(8,128)(2,1)} %bitcast.9), calls=%async_computation | async-start | bytes 524288 | tf_op jit(solution)/shard_map/all_to_all | solution.py:409
  65.8 2.1 %collective-permute-start.10 = (bf16[128,512]{1,0:T(8,128)(2,1)S(1)}, bf16[128,512]{1,0:T(8,128)(2,1)S(1)}, u32[]{:S(2)}, u32[]{:S(2)}) collective-permute-start(bf16[128,512]{1,0:T(8,128)(2,1)S(1)} %get-tuple-element.34), channel_id=1, source_target_pairs={{0,3},{1,2},{2,1},{3,0},{4,7},{5,6},{6,5},{7,4},{8,11},{9,10},{10,... | collective-permute-start | bytes 393224 | tf_op jit(solution)/shard_map/ppermute | solution.py:366
  67.9 0.0 collective-permute-start.8
  67.9 0.2 collective-permute-start.9
  68.1 9.7 %collective-permute-done.10.r3 = bf16[128,512]{1,0:T(8,128)(2,1)S(1)} collective-permute-done((bf16[128,512]{1,0:T(8,128)(2,1)S(1)}, bf16[128,512]{1,0:T(8,128)(2,1)S(1)}, u32[]{:S(2)}, u32[]{:S(2)}) %collective-permute-start.10) | collective-permute-done | bytes 131104 | tf_op jit(solution)/shard_map/ppermute | solution.py:366
  77.9 0.0 collective-permute-done.8.r1
  77.9 0.6 collective-permute-done.9.r2
  78.5 0.9 %query_end.1 = bf16[128,512]{1,0:T(8,128)(2,1)} custom-call(f32[128,512]{1,0:T(8,128)S(1)} %get-tuple-element.31.mine_ref, bf16[128,512]{1,0:T(8,128)(2,1)S(1)} %collective-permute-done.8.r1, bf16[128,512]{1,0:T(8,128)(2,1)S(1)} %collective-permute-done.9.r2, bf16[128,512]{1,0:T(8,128)(2,1)S(1)} %collective-permute-done.10.r3, f32[512,128]{1,0:T(8,128)S(1)} %tables.1.tab_ref), custom_call_target="tpu_custom_call" | custom-call | flops 300000 | bytes 900000 | tf_op jit(solution)/shard_map/query_end/pallas_call | solution.py:285
  79.4 0.0 all-to-all-done
  79.4 0.7 convert_reduce_fusion
Async XLA Ops:
  2.1 7.5 %collective-permute-start.3 = (bf16[128,1024]{1,0:T(8,128)(2,1)S(1)}, bf16[128,1024]{1,0:T(8,128)(2,1)S(1)}, u32[]{:S(2)}, u32[]{:S(2)}) collective-permute-start(bf16[128,1024]{1,0:T(8,128)(2,1)S(1)} %get-tuple-element.27.qg0), channel_id=1, source_target_pairs={{0,2},{1,3},{2,0},{3,1},{4,6},{5,7},{6,4},{7,5},{8,10},{9,11},{10,... | collective-permute-start | bytes 786440 | tf_op jit(solution)/shard_map/ppermute | solution.py:366
  4.7 20.6 %collective-permute-start.2 = (bf16[128,1024]{1,0:T(8,128)(2,1)S(1)}, bf16[128,1024]{1,0:T(8,128)(2,1)S(1)}, u32[]{:S(2)}, u32[]{:S(2)}) collective-permute-start(bf16[128,1024]{1,0:T(8,128)(2,1)S(1)} %get-tuple-element.27.qg0), channel_id=1, source_target_pairs={{0,1},{1,0},{2,3},{3,2},{4,5},{5,4},{6,7},{7,6},{8,9},{9,8},{10,11... | collective-permute-start | bytes 786440 | tf_op jit(solution)/shard_map/ppermute | solution.py:366
  9.7 15.6 %collective-permute-start.4 = (bf16[128,1024]{1,0:T(8,128)(2,1)S(1)}, bf16[128,1024]{1,0:T(8,128)(2,1)S(1)}, u32[]{:S(2)}, u32[]{:S(2)}) collective-permute-start(bf16[128,1024]{1,0:T(8,128)(2,1)S(1)} %collective-permute-done.3.qg2), channel_id=1, source_target_pairs={{0,1},{1,0},{2,3},{3,2},{4,5},{5,4},{6,7},{7,6},{8,9},{9,8},{10,11... | collective-permute-start | bytes 786440 | tf_op jit(solution)/shard_map/ppermute | solution.py:366
  12.3 23.8 %collective-permute-start.14 = (bf16[1024,128]{1,0:T(8,128)(2,1)S(1)}, bf16[1024,128]{1,0:T(8,128)(2,1)S(1)}, u32[]{:S(2)}, u32[]{:S(2)}) collective-permute-start(bf16[1024,128]{1,0:T(8,128)(2,1)S(1)} %get-tuple-element.39), channel_id=1, source_target_pairs={{0,4},{1,5},{2,6},{3,7},{4,8},{5,9},{6,10},{7,11},{8,12},{9,13},{1... | collective-permute-start | bytes 786440 | tf_op jit(solution)/shard_map/ppermute | solution.py:366
  13.6 9.3 %collective-permute-start = (bf16[128,256]{1,0:T(8,128)(2,1)S(1)}, bf16[128,256]{1,0:T(8,128)(2,1)S(1)}, u32[]{:S(2)}, u32[]{:S(2)}) collective-permute-start(bf16[128,256]{1,0:T(8,128)(2,1)S(1)} %get-tuple-element.25.kv0), channel_id=1, source_target_pairs={{0,4},{1,5},{2,6},{3,7},{4,8},{5,9},{6,10},{7,11},{8,12},{9,13},{1... | collective-permute-start | bytes 196616 | tf_op jit(solution)/shard_map/ppermute | solution.py:366
  14.8 10.4 %collective-permute-start.1 = (bf16[128,256]{1,0:T(8,128)(2,1)S(1)}, bf16[128,256]{1,0:T(8,128)(2,1)S(1)}, u32[]{:S(2)}, u32[]{:S(2)}) collective-permute-start(bf16[128,256]{1,0:T(8,128)(2,1)S(1)} %get-tuple-element.25.kv0), channel_id=1, source_target_pairs={{0,8},{1,9},{2,10},{3,11},{4,12},{5,13},{6,14},{7,15},{8,0},{9,1},... | collective-permute-start | bytes 196616 | tf_op jit(solution)/shard_map/ppermute | solution.py:366
  27.5 3.2 %collective-permute-start.5 = (f32[4,2048]{1,0:T(4,128)S(1)}, f32[4,2048]{1,0:T(4,128)S(1)}, u32[]{:S(2)}, u32[]{:S(2)}) collective-permute-start(f32[4,2048]{1,0:T(4,128)S(1)} %get-tuple-element.30.st0), channel_id=1, source_target_pairs={{0,1},{1,0},{2,3},{3,2},{4,5},{5,4},{6,7},{7,6},{8,9},{9,8},{10,11... | collective-permute-start | bytes 98312 | tf_op jit(solution)/shard_map/ppermute | solution.py:366
  28.5 2.8 %collective-permute-start.6 = (f32[4,2048]{1,0:T(4,128)S(1)}, f32[4,2048]{1,0:T(4,128)S(1)}, u32[]{:S(2)}, u32[]{:S(2)}) collective-permute-start(f32[4,2048]{1,0:T(4,128)S(1)} %get-tuple-element.30.st0), channel_id=1, source_target_pairs={{0,2},{1,3},{2,0},{3,1},{4,6},{5,7},{6,4},{7,5},{8,10},{9,11},{10,... | collective-permute-start | bytes 98312 | tf_op jit(solution)/shard_map/ppermute | solution.py:366
  29.9 3.4 %collective-permute-start.7 = (f32[4,2048]{1,0:T(4,128)S(1)}, f32[4,2048]{1,0:T(4,128)S(1)}, u32[]{:S(2)}, u32[]{:S(2)}) collective-permute-start(f32[4,2048]{1,0:T(4,128)S(1)} %get-tuple-element.30.st0), channel_id=1, source_target_pairs={{0,3},{1,2},{2,1},{3,0},{4,7},{5,6},{6,5},{7,4},{8,11},{9,10},{10,... | collective-permute-start | bytes 98312 | tf_op jit(solution)/shard_map/ppermute | solution.py:366
  30.2 9.2 %collective-permute-start.15 = (bf16[1024,128]{1,0:T(8,128)(2,1)S(1)}, bf16[1024,128]{1,0:T(8,128)(2,1)S(1)}, u32[]{:S(2)}, u32[]{:S(2)}) collective-permute-start(bf16[1024,128]{1,0:T(8,128)(2,1)S(1)} %get-tuple-element.40), channel_id=1, source_target_pairs={{0,8},{1,9},{2,10},{3,11},{4,12},{5,13},{6,14},{7,15},{8,0},{9,1},... | collective-permute-start | bytes 786440 | tf_op jit(solution)/shard_map/ppermute | solution.py:366
  30.7 11.3 %collective-permute-start.16 = (bf16[1024,128]{1,0:T(8,128)(2,1)S(1)}, bf16[1024,128]{1,0:T(8,128)(2,1)S(1)}, u32[]{:S(2)}, u32[]{:S(2)}) collective-permute-start(bf16[1024,128]{1,0:T(8,128)(2,1)S(1)} %get-tuple-element.41), channel_id=1, source_target_pairs={{0,12},{1,13},{2,14},{3,15},{4,0},{5,1},{6,2},{7,3},{8,4},{9,5},{1... | collective-permute-start | bytes 786440 | tf_op jit(solution)/shard_map/ppermute | solution.py:366
  34.7 10.0 %collective-permute-start.11 = (bf16[384,256]{1,0:T(8,128)(2,1)S(1)}, bf16[384,256]{1,0:T(8,128)(2,1)S(1)}, u32[]{:S(2)}, u32[]{:S(2)}) collective-permute-start(bf16[384,256]{1,0:T(8,128)(2,1)S(1)} %get-tuple-element.36), channel_id=1, source_target_pairs={{0,4},{1,5},{2,6},{3,7},{4,8},{5,9},{6,10},{7,11},{8,12},{9,13},{1... | collective-permute-start | bytes 589832 | tf_op jit(solution)/shard_map/ppermute | solution.py:366
  34.8 13.1 %collective-permute-start.12 = (bf16[384,256]{1,0:T(8,128)(2,1)S(1)}, bf16[384,256]{1,0:T(8,128)(2,1)S(1)}, u32[]{:S(2)}, u32[]{:S(2)}) collective-permute-start(bf16[384,256]{1,0:T(8,128)(2,1)S(1)} %get-tuple-element.36), channel_id=1, source_target_pairs={{0,8},{1,9},{2,10},{3,11},{4,12},{5,13},{6,14},{7,15},{8,0},{9,1},... | collective-permute-start | bytes 589832 | tf_op jit(solution)/shard_map/ppermute | solution.py:366
  36.1 14.4 %collective-permute-start.13 = (bf16[384,256]{1,0:T(8,128)(2,1)S(1)}, bf16[384,256]{1,0:T(8,128)(2,1)S(1)}, u32[]{:S(2)}, u32[]{:S(2)}) collective-permute-start(bf16[384,256]{1,0:T(8,128)(2,1)S(1)} %get-tuple-element.36), channel_id=1, source_target_pairs={{0,12},{1,13},{2,14},{3,15},{4,0},{5,1},{6,2},{7,3},{8,4},{9,5},{1... | collective-permute-start | bytes 589832 | tf_op jit(solution)/shard_map/ppermute | solution.py:366
  51.8 2.1 %collective-permute-start.17 = (bf16[512,256]{1,0:T(8,128)(2,1)S(1)}, bf16[512,256]{1,0:T(8,128)(2,1)S(1)}, u32[]{:S(2)}, u32[]{:S(2)}) collective-permute-start(bf16[512,256]{1,0:T(8,128)(2,1)S(1)} %get-tuple-element.45), channel_id=1, source_target_pairs={{0,1},{1,0},{2,3},{3,2},{4,5},{5,4},{6,7},{7,6},{8,9},{9,8},{10,11... | collective-permute-start | bytes 786440 | tf_op jit(solution)/shard_map/ppermute | solution.py:366
  54.8 24.6 %all-to-all-start = ((bf16[32,16,256]{2,1,0:T(8,128)(2,1)}), bf16[32,16,256]{2,1,0:T(8,128)(2,1)S(1)}, u32[]{:S(2)}, u32[]{:S(2)}) async-start(bf16[32,16,256]{2,1,0:T(8,128)(2,1)} %bitcast.9), calls=%async_computation | async-start | bytes 524288 | tf_op jit(solution)/shard_map/all_to_all | solution.py:409
  65.8 12.1 %collective-permute-start.10 = (bf16[128,512]{1,0:T(8,128)(2,1)S(1)}, bf16[128,512]{1,0:T(8,128)(2,1)S(1)}, u32[]{:S(2)}, u32[]{:S(2)}) collective-permute-start(bf16[128,512]{1,0:T(8,128)(2,1)S(1)} %get-tuple-element.34), channel_id=1, source_target_pairs={{0,3},{1,2},{2,1},{3,0},{4,7},{5,6},{6,5},{7,4},{8,11},{9,10},{10,... | collective-permute-start | bytes 393224 | tf_op jit(solution)/shard_map/ppermute | solution.py:366
  67.9 9.9 %collective-permute-start.8 = (bf16[128,512]{1,0:T(8,128)(2,1)S(1)}, bf16[128,512]{1,0:T(8,128)(2,1)S(1)}, u32[]{:S(2)}, u32[]{:S(2)}) collective-permute-start(bf16[128,512]{1,0:T(8,128)(2,1)S(1)} %get-tuple-element.32), channel_id=1, source_target_pairs={{0,1},{1,0},{2,3},{3,2},{4,5},{5,4},{6,7},{7,6},{8,9},{9,8},{10,11... | collective-permute-start | bytes 393224 | tf_op jit(solution)/shard_map/ppermute | solution.py:366
  67.9 10.6 %collective-permute-start.9 = (bf16[128,512]{1,0:T(8,128)(2,1)S(1)}, bf16[128,512]{1,0:T(8,128)(2,1)S(1)}, u32[]{:S(2)}, u32[]{:S(2)}) collective-permute-start(bf16[128,512]{1,0:T(8,128)(2,1)S(1)} %get-tuple-element.33), channel_id=1, source_target_pairs={{0,2},{1,3},{2,0},{3,1},{4,6},{5,7},{6,4},{7,5},{8,10},{9,11},{10,... | collective-permute-start | bytes 393224 | tf_op jit(solution)/shard_map/ppermute | solution.py:366

commit v4 on v3

--- a/solution.py
+++ b/solution.py
@@ -111,11 +111,13 @@
 def slices_kernel(where_ref, x_ref, o0, o1, o2, o3, turned):
     slab = where_ref[0] // 4
     for i in range(32):
-        turned[i * B : (i + 1) * B, :] = x_ref[:, i * B : (i + 1) * B].T
+        tile = x_ref[:, i * B : (i + 1) * B].T
+        for j in range(8):
+            to, z, core = i % 2 * 2 + j // 4, j // 2 % 2, j % 2
+            at = ((to * 2 + core) * 32 + i // 2 * 2 + z) * 16
+            turned[at : at + 16, :] = tile[j * 16 : (j + 1) * 16, :]
     for k, out in enumerate((o0, o1, o2, o3)):
-        target = (slab + k) % 4
-        for dp in range(16):
-            out[dp * 64 : (dp + 1) * 64, :] = turned[rows(dp * 4 + target, 64), :]
+        out[...] = turned[rows((slab + k) % 4, 1024), :]
 
 
 def slices(rank, x):
@@ -134,13 +136,15 @@
 def tables_kernel(where_ref, tab_ref):
     rank = where_ref[0]
     for k in range(4):
-        tab_ref[k * B : (k + 1) * B, :] = rope_table(((rank // 4 - k + 4) % 4 * 4 + rank % 4) * B)
+        cosine, sine = split_table(rope_table(((rank // 4 - k + 4) % 4 * 4 + rank % 4) * B))
+        tab_ref[k * B : (k + 1) * B, :B] = cosine
+        tab_ref[k * B : (k + 1) * B, B:] = sine
 
 
 def tables(rank):
     return pl.pallas_call(
         tables_kernel,
-        out_shape=shape((4 * B, B), jnp.float32),
+        out_shape=shape((4 * B, 2 * B), jnp.float32),
         in_specs=[SMEM],
         out_specs=VMEM,
         compiler_params=pltpu.CompilerParams(vmem_limit_bytes=4 * MIB),
@@ -272,7 +276,7 @@
 
 
 def query_end_kernel(mine_ref, r1, r2, r3, tab_ref, out_ref):
-    cosine, sine = split_table(tab_ref[:B, :])
+    cosine, sine = tab_ref[:B, :B], tab_ref[:B, B:]
     for h in range(HEADS):
         part = slice(h * B, (h + 1) * B)
         u = mine_ref[:, part]
@@ -295,7 +299,7 @@
 
 def weight_kernel(
     where_ref, keep_ref, r1, r2, r3, tab_ref, x0, x1, x2, x3,
-    key_ref, value_ref, own_ref, send_ref, acc,
+    key_ref, value_ref, send_ref, g01_ref, g23_ref,
 ):
     core = where_ref[0] % 2
 
@@ -309,20 +313,40 @@
         key, value = (
             part(k, 0, lanes) + part((k - 1) % 4, 1, lanes) + part((k - 2) % 4, 2, lanes) for lanes in (0, 1)
         )
-        cosine, sine = split_table(tab_ref[k * B : (k + 1) * B, :])
+        cosine, sine = tab_ref[k * B : (k + 1) * B, :B], tab_ref[k * B : (k + 1) * B, B:]
         key = rotated(key, cosine, -sine).astype(jnp.bfloat16)
         value = value.astype(jnp.bfloat16)
         if k == 0:
             key_ref[...] = key
             value_ref[...] = value
         grads.append(jnp.concatenate([key, value], 1))
-    total = dot(jnp.concatenate([x0[...], x1[...]], 1), jnp.concatenate(grads[:2], 0), NN)
-    total = total + dot(jnp.concatenate([x2[...], x3[...]], 1), jnp.concatenate(grads[2:], 0), NN)
-    acc[...] = total
-    for i in range(32):
-        part = slice(i * 16, (i + 1) * 16)
-        own_ref[part, :] = acc[rows(i * 2 + core, 16), :]
-        send_ref[part, :] = acc[rows(i * 2 + 1 - core, 16), :].astype(jnp.bfloat16)
+    low, high = jnp.concatenate(grads[:2], 0), jnp.concatenate(grads[2:], 0)
+    g01_ref[...] = low
+    g23_ref[...] = high
+    send_ref[...] = half_of_weight(1 - core, (x0, x1, x2, x3), low, high).astype(jnp.bfloat16)
+
+
+def half_of_weight(core, xs, low, high):
+    at = rows(core, 512)
+    total = dot(jnp.concatenate([xs[0][at, :], xs[1][at, :]], 1), low, NN)
+    return total + dot(jnp.concatenate([xs[2][at, :], xs[3][at, :]], 1), high, NN)
+
+
+def own_half_kernel(where_ref, g01_ref, g23_ref, x0, x1, x2, x3, own_ref):
+    core = where_ref[0] % 2
+    own_ref[...] = half_of_weight(core, (x0, x1, x2, x3), g01_ref[...], g23_ref[...])
+
+
+def own_half(rank, low, high, xs):
+    return pl.pallas_call(
+        own_half_kernel,
+        out_shape=shape((512, 256), jnp.float32),
+        in_specs=[SMEM] + [VMEM] * 6,
+        out_specs=VMEM,
+        compiler_params=pltpu.CompilerParams(vmem_limit_bytes=12 * MIB),
+        cost_estimate=pl.CostEstimate(flops=134_000_000, bytes_accessed=1_800_000, transcendentals=0),
+        name="own_half",
+    )(rank, low, high, *xs)
 
 
 def weight_part(rank, keep, arrived, table, xs):
@@ -331,14 +355,14 @@
         out_shape=(
             shape((B, B), jnp.bfloat16),
             shape((B, B), jnp.bfloat16),
-            shape((512, 256), jnp.float32),
             shape((512, 256), jnp.bfloat16),
+            shape((256, 256), jnp.bfloat16),
+            shape((256, 256), jnp.bfloat16),
         ),
         in_specs=[SMEM] + [VMEM] * 9,
-        out_specs=(VMEM,) * 4,
-        scratch_shapes=[pltpu.VMEM((1024, 256), jnp.float32)],
+        out_specs=(VMEM,) * 5,
         compiler_params=pltpu.CompilerParams(vmem_limit_bytes=12 * MIB),
-        cost_estimate=pl.CostEstimate(flops=268_000_000, bytes_accessed=3_000_000, transcendentals=0),
+        cost_estimate=pl.CostEstimate(flops=134_000_000, bytes_accessed=3_000_000, transcendentals=0),
         name="weight",
     )(rank, keep, *arrived, table, *xs)
 
@@ -398,8 +422,9 @@
     query_parts = [swap(part, bits) for bits, part in zip((1, 2, 3), others)]
     query_grad = query_end(mine, query_parts, table)
 
-    key_grad, value_grad, own, send = weight_part(where, keep, arrived, table, xs)
+    key_grad, value_grad, send, low, high = weight_part(where, keep, arrived, table, xs)
     arrived = swap(send, 1)
+    own = own_half(where, low, high, xs)
     blocks = weight_fold(own, arrived).reshape(32, 16, 256)
     groups = [
         [dp * 16 + slab * 4 + z * 2 + core for dp in range(16) for z in range(2)]

time: 80.2 us -> 79.7 us (level)
  transfers between devices with their start and end apart: 19 -> 19, of which waited for: 13 -> 13; matrix products, arithmetic and copies ran while one was open for 0% -> 0% of each run, Pallas kernels for 7% -> 8%
where the time goes in v4:
time: 79.7 us; the launch traced here: 79.5 us
  waiting for transfers between devices  38.8 us (49%)
  starting transfers between devices  30 us (38%)
  Pallas kernels  9.31 us (12%)
    ppermute x18, waiting for transfers between devices, permute(): return lax.ppermute(array, 'ctx', pairs)  38.8 us
    ppermute x18, starting transfers between devices, permute(): return lax.ppermute(array, 'ctx', pairs)  19 us
    all_to_all x1, starting transfers between devices, compute(): lax.all_to_all(blocks, ('dp', 'ctx'), split_axis=0, concat_axis=0, tiled=...  11 us
    pallas_call x1, Pallas kernels, scores(): pl.pallas_call(scores_kernel, out_shape=(shape(wide, jnp.float32), shape(...  2.23 us
  transfers between devices with their start and end apart: 19, of which 13 were waited for; matrix products, arithmetic and copies ran while one was open for 0% of the time, Pallas kernels for 8%

profile of v4, /device:TPU:1, one launch (start us, length us, event | category | flops | bytes accessed | tf_op | source)
XLA Modules:
  0.0 79.5 jit_solution(3529785613703376842)
XLA Ops:
  0.6 1.5 %prepare.1 = (bf16[128,256]{1,0:T(8,128)(2,1)S(1)}, bf16[128,1024]{1,0:T(8,128)(2,1)S(1)}, bf16[128,4096]{1,0:T(8,128)(2,1)S(1)}, s32[1,8]{1,0:T(1,128)S(1)}) custom-call(s32[1]{0:T(128)} %bitcast.where_ref, bf16[128,128]{1,0:T(8,128)(2,1)} %bitcast.14, bf16[128,128]{1,0:T(8,128)(2,1)} %bitcast.15, bf16[128,512]{1,0:T(8,128)(2,1)} %bitcast.11, ...), custom_call_target="tpu_custom_call" | custom-call | tf_op jit(solution)/shard_map/prepare/pallas_call | solution.py:91
  2.1 2.5 %collective-permute-start.3 = (bf16[128,1024]{1,0:T(8,128)(2,1)S(1)}, bf16[128,1024]{1,0:T(8,128)(2,1)S(1)}, u32[]{:S(2)}, u32[]{:S(2)}) collective-permute-start(bf16[128,1024]{1,0:T(8,128)(2,1)S(1)} %get-tuple-element.28.qg0), channel_id=1, source_target_pairs={{0,2},{1,3},{2,0},{3,1},{4,6},{5,7},{6,4},{7,5},{8,10},{9,11},{10,... | collective-permute-start | bytes 786440 | tf_op jit(solution)/shard_map/ppermute | solution.py:390
  4.7 1.0 %collective-permute-start.2 = (bf16[128,1024]{1,0:T(8,128)(2,1)S(1)}, bf16[128,1024]{1,0:T(8,128)(2,1)S(1)}, u32[]{:S(2)}, u32[]{:S(2)}) collective-permute-start(bf16[128,1024]{1,0:T(8,128)(2,1)S(1)} %get-tuple-element.28.qg0), channel_id=1, source_target_pairs={{0,1},{1,0},{2,3},{3,2},{4,5},{5,4},{6,7},{7,6},{8,9},{9,8},{10,11... | collective-permute-start | bytes 786440 | tf_op jit(solution)/shard_map/ppermute | solution.py:390
  5.6 4.0 %collective-permute-done.3.qg2 = bf16[128,1024]{1,0:T(8,128)(2,1)S(1)} collective-permute-done((bf16[128,1024]{1,0:T(8,128)(2,1)S(1)}, bf16[128,1024]{1,0:T(8,128)(2,1)S(1)}, u32[]{:S(2)}, u32[]{:S(2)}) %collective-permute-start.3) | collective-permute-done | bytes 262176 | tf_op jit(solution)/shard_map/ppermute | solution.py:390
  9.7 2.3 %collective-permute-start.4 = (bf16[128,1024]{1,0:T(8,128)(2,1)S(1)}, bf16[128,1024]{1,0:T(8,128)(2,1)S(1)}, u32[]{:S(2)}, u32[]{:S(2)}) collective-permute-start(bf16[128,1024]{1,0:T(8,128)(2,1)S(1)} %collective-permute-done.3.qg2), channel_id=1, source_target_pairs={{0,1},{1,0},{2,3},{3,2},{4,5},{5,4},{6,7},{7,6},{8,9},{9,8},{10,11... | collective-permute-start | bytes 786440 | tf_op jit(solution)/shard_map/ppermute | solution.py:390
  11.9 0.4 slices.1
  12.3 1.3 %collective-permute-start.14 = (bf16[1024,128]{1,0:T(8,128)(2,1)S(1)}, bf16[1024,128]{1,0:T(8,128)(2,1)S(1)}, u32[]{:S(2)}, u32[]{:S(2)}) collective-permute-start(bf16[1024,128]{1,0:T(8,128)(2,1)S(1)} %get-tuple-element.40), channel_id=1, source_target_pairs={{0,4},{1,5},{2,6},{3,7},{4,8},{5,9},{6,10},{7,11},{8,12},{9,13},{1... | collective-permute-start | bytes 786440 | tf_op jit(solution)/shard_map/ppermute | solution.py:390
  13.6 1.2 %collective-permute-start = (bf16[128,256]{1,0:T(8,128)(2,1)S(1)}, bf16[128,256]{1,0:T(8,128)(2,1)S(1)}, u32[]{:S(2)}, u32[]{:S(2)}) collective-permute-start(bf16[128,256]{1,0:T(8,128)(2,1)S(1)} %get-tuple-element.26.kv0), channel_id=1, source_target_pairs={{0,4},{1,5},{2,6},{3,7},{4,8},{5,9},{6,10},{7,11},{8,12},{9,13},{1... | collective-permute-start | bytes 196616 | tf_op jit(solution)/shard_map/ppermute | solution.py:390
  14.8 1.4 %collective-permute-start.1 = (bf16[128,256]{1,0:T(8,128)(2,1)S(1)}, bf16[128,256]{1,0:T(8,128)(2,1)S(1)}, u32[]{:S(2)}, u32[]{:S(2)}) collective-permute-start(bf16[128,256]{1,0:T(8,128)(2,1)S(1)} %get-tuple-element.26.kv0), channel_id=1, source_target_pairs={{0,8},{1,9},{2,10},{3,11},{4,12},{5,13},{6,14},{7,15},{8,0},{9,1},... | collective-permute-start | bytes 196616 | tf_op jit(solution)/shard_map/ppermute | solution.py:390
  16.3 6.6 %collective-permute-done.kv1 = bf16[128,256]{1,0:T(8,128)(2,1)S(1)} collective-permute-done((bf16[128,256]{1,0:T(8,128)(2,1)S(1)}, bf16[128,256]{1,0:T(8,128)(2,1)S(1)}, u32[]{:S(2)}, u32[]{:S(2)}) %collective-permute-start) | collective-permute-done | bytes 65568 | tf_op jit(solution)/shard_map/ppermute | solution.py:390
  22.9 2.4 %collective-permute-done.1.kv2 = bf16[128,256]{1,0:T(8,128)(2,1)S(1)} collective-permute-done((bf16[128,256]{1,0:T(8,128)(2,1)S(1)}, bf16[128,256]{1,0:T(8,128)(2,1)S(1)}, u32[]{:S(2)}, u32[]{:S(2)}) %collective-permute-start.1) | collective-permute-done | bytes 65568 | tf_op jit(solution)/shard_map/ppermute | solution.py:390
  25.3 0.0 collective-permute-done.2.qg1
  25.3 0.0 collective-permute-done.4.qg3
  25.3 2.2 %scores.1 = (f32[384,2048]{1,0:T(8,128)S(1)}, f32[384,2048]{1,0:T(8,128)S(1)}, f32[4,2048]{1,0:T(4,128)S(1)}) custom-call(s32[1]{0:T(128)} %bitcast.where_ref, s32[1,8]{1,0:T(1,128)S(1)} %get-tuple-element.27.len_ref, bf16[128,256]{1,0:T(8,128)(2,1)S(1)} %get-tuple-element.26.kv0, bf16[128,256]{1,0:T(8,128)(2,1)S(1)} %collective-permute-done.kv1, ...), custom_call_target="tpu_custom_call" | custom-call | flops 400000000 | bytes 8000000 | tf_op jit(solution)/shard_map/scores/pallas_call | solution.py:212
  27.5 0.9 %collective-permute-start.5 = (f32[4,2048]{1,0:T(4,128)S(1)}, f32[4,2048]{1,0:T(4,128)S(1)}, u32[]{:S(2)}, u32[]{:S(2)}) collective-permute-start(f32[4,2048]{1,0:T(4,128)S(1)} %get-tuple-element.31.st0), channel_id=1, source_target_pairs={{0,1},{1,0},{2,3},{3,2},{4,5},{5,4},{6,7},{7,6},{8,9},{9,8},{10,11... | collective-permute-start | bytes 98312 | tf_op jit(solution)/shard_map/ppermute | solution.py:390
  28.5 1.5 %collective-permute-start.6 = (f32[4,2048]{1,0:T(4,128)S(1)}, f32[4,2048]{1,0:T(4,128)S(1)}, u32[]{:S(2)}, u32[]{:S(2)}) collective-permute-start(f32[4,2048]{1,0:T(4,128)S(1)} %get-tuple-element.31.st0), channel_id=1, source_target_pairs={{0,2},{1,3},{2,0},{3,1},{4,6},{5,7},{6,4},{7,5},{8,10},{9,11},{10,... | collective-permute-start | bytes 98312 | tf_op jit(solution)/shard_map/ppermute | solution.py:390
  29.9 0.3 collective-permute-start.7
  30.2 0.6 collective-permute-start.15
  30.7 0.0 collective-permute-done.5.st1
  30.7 0.0 collective-permute-start.16
  30.7 0.5 collective-permute-done.6.st2
  31.2 2.1 %collective-permute-done.7.st3 = f32[4,2048]{1,0:T(4,128)S(1)} collective-permute-done((f32[4,2048]{1,0:T(4,128)S(1)}, f32[4,2048]{1,0:T(4,128)S(1)}, u32[]{:S(2)}, u32[]{:S(2)}) %collective-permute-start.7) | collective-permute-done | bytes 32800 | tf_op jit(solution)/shard_map/ppermute | solution.py:390
  33.3 1.4 %gradients.1 = (f32[384,256]{1,0:T(8,128)S(1)}, bf16[384,256]{1,0:T(8,128)(2,1)S(1)}, f32[128,512]{1,0:T(8,128)S(1)}, bf16[128,512]{1,0:T(8,128)(2,1)S(1)}, bf16...) custom-call(bf16[128,256]{1,0:T(8,128)(2,1)S(1)} %get-tuple-element.26.kv0, ...), custom_call_target="tpu_custom_call" | custom-call | flops 600000000 | bytes 8000000 | tf_op jit(solution)/shard_map/gradients/pallas_call | solution.py:260
  34.7 0.1 collective-permute-start.11
  34.8 1.3 %collective-permute-start.12 = (bf16[384,256]{1,0:T(8,128)(2,1)S(1)}, bf16[384,256]{1,0:T(8,128)(2,1)S(1)}, u32[]{:S(2)}, u32[]{:S(2)}) collective-permute-start(bf16[384,256]{1,0:T(8,128)(2,1)S(1)} %get-tuple-element.37), channel_id=1, source_target_pairs={{0,8},{1,9},{2,10},{3,11},{4,12},{5,13},{6,14},{7,15},{8,0},{9,1},... | collective-permute-start | bytes 589832 | tf_op jit(solution)/shard_map/ppermute | solution.py:390
  36.1 0.0 collective-permute-done.14.x1
  36.1 1.3 %collective-permute-start.13 = (bf16[384,256]{1,0:T(8,128)(2,1)S(1)}, bf16[384,256]{1,0:T(8,128)(2,1)S(1)}, u32[]{:S(2)}, u32[]{:S(2)}) collective-permute-start(bf16[384,256]{1,0:T(8,128)(2,1)S(1)} %get-tuple-element.37), channel_id=1, source_target_pairs={{0,12},{1,13},{2,14},{3,15},{4,0},{5,1},{6,2},{7,3},{8,4},{9,5},{1... | collective-permute-start | bytes 589832 | tf_op jit(solution)/shard_map/ppermute | solution.py:390
  37.4 1.1 %tables.1.tab_ref = f32[512,256]{1,0:T(8,128)S(1)} custom-call(s32[1]{0:T(128)} %bitcast.where_ref), custom_call_target="tpu_custom_call" | custom-call | flops 2000000 | bytes 260000 | tf_op jit(solution)/shard_map/tables/pallas_call | solution.py:145
  38.6 0.9 %collective-permute-done.15.x2 = bf16[1024,128]{1,0:T(8,128)(2,1)S(1)} collective-permute-done((bf16[1024,128]{1,0:T(8,128)(2,1)S(1)}, bf16[1024,128]{1,0:T(8,128)(2,1)S(1)}, u32[]{:S(2)}, u32[]{:S(2)}) %collective-permute-start.15) | collective-permute-done | bytes 262176 | tf_op jit(solution)/shard_map/ppermute | solution.py:390
  39.4 2.6 %collective-permute-done.16.x3 = bf16[1024,128]{1,0:T(8,128)(2,1)S(1)} collective-permute-done((bf16[1024,128]{1,0:T(8,128)(2,1)S(1)}, bf16[1024,128]{1,0:T(8,128)(2,1)S(1)}, u32[]{:S(2)}, u32[]{:S(2)}) %collective-permute-start.16) | collective-permute-done | bytes 262176 | tf_op jit(solution)/shard_map/ppermute | solution.py:390
  42.0 2.6 %collective-permute-done.11.r1 = bf16[384,256]{1,0:T(8,128)(2,1)S(1)} collective-permute-done((bf16[384,256]{1,0:T(8,128)(2,1)S(1)}, bf16[384,256]{1,0:T(8,128)(2,1)S(1)}, u32[]{:S(2)}, u32[]{:S(2)}) %collective-permute-start.11) | collective-permute-done | bytes 196640 | tf_op jit(solution)/shard_map/ppermute | solution.py:390
  44.7 3.2 %collective-permute-done.12.r2 = bf16[384,256]{1,0:T(8,128)(2,1)S(1)} collective-permute-done((bf16[384,256]{1,0:T(8,128)(2,1)S(1)}, bf16[384,256]{1,0:T(8,128)(2,1)S(1)}, u32[]{:S(2)}, u32[]{:S(2)}) %collective-permute-start.12) | collective-permute-done | bytes 196640 | tf_op jit(solution)/shard_map/ppermute | solution.py:390
  47.9 2.7 %collective-permute-done.13.r3 = bf16[384,256]{1,0:T(8,128)(2,1)S(1)} collective-permute-done((bf16[384,256]{1,0:T(8,128)(2,1)S(1)}, bf16[384,256]{1,0:T(8,128)(2,1)S(1)}, u32[]{:S(2)}, u32[]{:S(2)}) %collective-permute-start.13) | collective-permute-done | bytes 196640 | tf_op jit(solution)/shard_map/ppermute | solution.py:390
  50.5 0.8 weight.1
  51.3 1.0 %collective-permute-start.17 = (bf16[512,256]{1,0:T(8,128)(2,1)S(1)}, bf16[512,256]{1,0:T(8,128)(2,1)S(1)}, u32[]{:S(2)}, u32[]{:S(2)}) collective-permute-start(bf16[512,256]{1,0:T(8,128)(2,1)S(1)} %get-tuple-element.47), channel_id=1, source_target_pairs={{0,1},{1,0},{2,3},{3,2},{4,5},{5,4},{6,7},{7,6},{8,9},{9,8},{10,11... | collective-permute-start | bytes 786440 | tf_op jit(solution)/shard_map/ppermute | solution.py:390
  52.3 0.3 own_half.1.own_ref
  52.6 0.9 %collective-permute-done.17.arrived_ref = bf16[512,256]{1,0:T(8,128)(2,1)S(1)} collective-permute-done((bf16[512,256]{1,0:T(8,128)(2,1)S(1)}, bf16[512,256]{1,0:T(8,128)(2,1)S(1)}, u32[]{:S(2)}, u32[]{:S(2)}) %collective-permute-start.17) | collective-permute-done | bytes 262176 | tf_op jit(solution)/shard_map/ppermute | solution.py:390
  53.4 0.7 weight_fold.1
  54.2 11.0 %all-to-all-start = ((bf16[32,16,256]{2,1,0:T(8,128)(2,1)}), bf16[32,16,256]{2,1,0:T(8,128)(2,1)S(1)}, u32[]{:S(2)}, u32[]{:S(2)}) async-start(bf16[32,16,256]{2,1,0:T(8,128)(2,1)} %bitcast.9), calls=%async_computation | async-start | bytes 524288 | tf_op jit(solution)/shard_map/all_to_all | solution.py:434
  65.2 2.1 %collective-permute-start.10 = (bf16[128,512]{1,0:T(8,128)(2,1)S(1)}, bf16[128,512]{1,0:T(8,128)(2,1)S(1)}, u32[]{:S(2)}, u32[]{:S(2)}) collective-permute-start(bf16[128,512]{1,0:T(8,128)(2,1)S(1)} %get-tuple-element.35), channel_id=1, source_target_pairs={{0,3},{1,2},{2,1},{3,0},{4,7},{5,6},{6,5},{7,4},{8,11},{9,10},{10,... | collective-permute-start | bytes 393224 | tf_op jit(solution)/shard_map/ppermute | solution.py:390
  67.4 0.0 collective-permute-start.8
  67.4 0.2 collective-permute-start.9
  67.6 9.7 %collective-permute-done.10.r3 = bf16[128,512]{1,0:T(8,128)(2,1)S(1)} collective-permute-done((bf16[128,512]{1,0:T(8,128)(2,1)S(1)}, bf16[128,512]{1,0:T(8,128)(2,1)S(1)}, u32[]{:S(2)}, u32[]{:S(2)}) %collective-permute-start.10) | collective-permute-done | bytes 131104 | tf_op jit(solution)/shard_map/ppermute | solution.py:390
  77.3 0.0 collective-permute-done.8.r1
  77.3 0.6 collective-permute-done.9.r2
  77.9 0.9 %query_end.1 = bf16[128,512]{1,0:T(8,128)(2,1)} custom-call(f32[128,512]{1,0:T(8,128)S(1)} %get-tuple-element.32.mine_ref, bf16[128,512]{1,0:T(8,128)(2,1)S(1)} %collective-permute-done.8.r1, bf16[128,512]{1,0:T(8,128)(2,1)S(1)} %collective-permute-done.9.r2, bf16[128,512]{1,0:T(8,128)(2,1)S(1)} %collective-permute-done.10.r3, f32[512,256]{1,0:T(8,128)S(1)} %tables.1.tab_ref), custom_call_target="tpu_custom_call" | custom-call | flops 300000 | bytes 900000 | tf_op jit(solution)/shard_map/query_end/pallas_call | solution.py:289
  78.9 0.0 all-to-all-done
  78.9 0.7 convert_reduce_fusion
Async XLA Ops:
  2.1 7.5 %collective-permute-start.3 = (bf16[128,1024]{1,0:T(8,128)(2,1)S(1)}, bf16[128,1024]{1,0:T(8,128)(2,1)S(1)}, u32[]{:S(2)}, u32[]{:S(2)}) collective-permute-start(bf16[128,1024]{1,0:T(8,128)(2,1)S(1)} %get-tuple-element.28.qg0), channel_id=1, source_target_pairs={{0,2},{1,3},{2,0},{3,1},{4,6},{5,7},{6,4},{7,5},{8,10},{9,11},{10,... | collective-permute-start | bytes 786440 | tf_op jit(solution)/shard_map/ppermute | solution.py:390
  4.7 20.6 %collective-permute-start.2 = (bf16[128,1024]{1,0:T(8,128)(2,1)S(1)}, bf16[128,1024]{1,0:T(8,128)(2,1)S(1)}, u32[]{:S(2)}, u32[]{:S(2)}) collective-permute-start(bf16[128,1024]{1,0:T(8,128)(2,1)S(1)} %get-tuple-element.28.qg0), channel_id=1, source_target_pairs={{0,1},{1,0},{2,3},{3,2},{4,5},{5,4},{6,7},{7,6},{8,9},{9,8},{10,11... | collective-permute-start | bytes 786440 | tf_op jit(solution)/shard_map/ppermute | solution.py:390
  9.7 15.6 %collective-permute-start.4 = (bf16[128,1024]{1,0:T(8,128)(2,1)S(1)}, bf16[128,1024]{1,0:T(8,128)(2,1)S(1)}, u32[]{:S(2)}, u32[]{:S(2)}) collective-permute-start(bf16[128,1024]{1,0:T(8,128)(2,1)S(1)} %collective-permute-done.3.qg2), channel_id=1, source_target_pairs={{0,1},{1,0},{2,3},{3,2},{4,5},{5,4},{6,7},{7,6},{8,9},{9,8},{10,11... | collective-permute-start | bytes 786440 | tf_op jit(solution)/shard_map/ppermute | solution.py:390
  12.3 23.8 %collective-permute-start.14 = (bf16[1024,128]{1,0:T(8,128)(2,1)S(1)}, bf16[1024,128]{1,0:T(8,128)(2,1)S(1)}, u32[]{:S(2)}, u32[]{:S(2)}) collective-permute-start(bf16[1024,128]{1,0:T(8,128)(2,1)S(1)} %get-tuple-element.40), channel_id=1, source_target_pairs={{0,4},{1,5},{2,6},{3,7},{4,8},{5,9},{6,10},{7,11},{8,12},{9,13},{1... | collective-permute-start | bytes 786440 | tf_op jit(solution)/shard_map/ppermute | solution.py:390
  13.6 9.3 %collective-permute-start = (bf16[128,256]{1,0:T(8,128)(2,1)S(1)}, bf16[128,256]{1,0:T(8,128)(2,1)S(1)}, u32[]{:S(2)}, u32[]{:S(2)}) collective-permute-start(bf16[128,256]{1,0:T(8,128)(2,1)S(1)} %get-tuple-element.26.kv0), channel_id=1, source_target_pairs={{0,4},{1,5},{2,6},{3,7},{4,8},{5,9},{6,10},{7,11},{8,12},{9,13},{1... | collective-permute-start | bytes 196616 | tf_op jit(solution)/shard_map/ppermute | solution.py:390
  14.8 10.4 %collective-permute-start.1 = (bf16[128,256]{1,0:T(8,128)(2,1)S(1)}, bf16[128,256]{1,0:T(8,128)(2,1)S(1)}, u32[]{:S(2)}, u32[]{:S(2)}) collective-permute-start(bf16[128,256]{1,0:T(8,128)(2,1)S(1)} %get-tuple-element.26.kv0), channel_id=1, source_target_pairs={{0,8},{1,9},{2,10},{3,11},{4,12},{5,13},{6,14},{7,15},{8,0},{9,1},... | collective-permute-start | bytes 196616 | tf_op jit(solution)/shard_map/ppermute | solution.py:390
  27.5 3.2 %collective-permute-start.5 = (f32[4,2048]{1,0:T(4,128)S(1)}, f32[4,2048]{1,0:T(4,128)S(1)}, u32[]{:S(2)}, u32[]{:S(2)}) collective-permute-start(f32[4,2048]{1,0:T(4,128)S(1)} %get-tuple-element.31.st0), channel_id=1, source_target_pairs={{0,1},{1,0},{2,3},{3,2},{4,5},{5,4},{6,7},{7,6},{8,9},{9,8},{10,11... | collective-permute-start | bytes 98312 | tf_op jit(solution)/shard_map/ppermute | solution.py:390
  28.5 2.8 %collective-permute-start.6 = (f32[4,2048]{1,0:T(4,128)S(1)}, f32[4,2048]{1,0:T(4,128)S(1)}, u32[]{:S(2)}, u32[]{:S(2)}) collective-permute-start(f32[4,2048]{1,0:T(4,128)S(1)} %get-tuple-element.31.st0), channel_id=1, source_target_pairs={{0,2},{1,3},{2,0},{3,1},{4,6},{5,7},{6,4},{7,5},{8,10},{9,11},{10,... | collective-permute-start | bytes 98312 | tf_op jit(solution)/shard_map/ppermute | solution.py:390
  29.9 3.4 %collective-permute-start.7 = (f32[4,2048]{1,0:T(4,128)S(1)}, f32[4,2048]{1,0:T(4,128)S(1)}, u32[]{:S(2)}, u32[]{:S(2)}) collective-permute-start(f32[4,2048]{1,0:T(4,128)S(1)} %get-tuple-element.31.st0), channel_id=1, source_target_pairs={{0,3},{1,2},{2,1},{3,0},{4,7},{5,6},{6,5},{7,4},{8,11},{9,10},{10,... | collective-permute-start | bytes 98312 | tf_op jit(solution)/shard_map/ppermute | solution.py:390
  30.2 9.2 %collective-permute-start.15 = (bf16[1024,128]{1,0:T(8,128)(2,1)S(1)}, bf16[1024,128]{1,0:T(8,128)(2,1)S(1)}, u32[]{:S(2)}, u32[]{:S(2)}) collective-permute-start(bf16[1024,128]{1,0:T(8,128)(2,1)S(1)} %get-tuple-element.41), channel_id=1, source_target_pairs={{0,8},{1,9},{2,10},{3,11},{4,12},{5,13},{6,14},{7,15},{8,0},{9,1},... | collective-permute-start | bytes 786440 | tf_op jit(solution)/shard_map/ppermute | solution.py:390
  30.7 11.3 %collective-permute-start.16 = (bf16[1024,128]{1,0:T(8,128)(2,1)S(1)}, bf16[1024,128]{1,0:T(8,128)(2,1)S(1)}, u32[]{:S(2)}, u32[]{:S(2)}) collective-permute-start(bf16[1024,128]{1,0:T(8,128)(2,1)S(1)} %get-tuple-element.42), channel_id=1, source_target_pairs={{0,12},{1,13},{2,14},{3,15},{4,0},{5,1},{6,2},{7,3},{8,4},{9,5},{1... | collective-permute-start | bytes 786440 | tf_op jit(solution)/shard_map/ppermute | solution.py:390
  34.7 10.0 %collective-permute-start.11 = (bf16[384,256]{1,0:T(8,128)(2,1)S(1)}, bf16[384,256]{1,0:T(8,128)(2,1)S(1)}, u32[]{:S(2)}, u32[]{:S(2)}) collective-permute-start(bf16[384,256]{1,0:T(8,128)(2,1)S(1)} %get-tuple-element.37), channel_id=1, source_target_pairs={{0,4},{1,5},{2,6},{3,7},{4,8},{5,9},{6,10},{7,11},{8,12},{9,13},{1... | collective-permute-start | bytes 589832 | tf_op jit(solution)/shard_map/ppermute | solution.py:390
  34.8 13.1 %collective-permute-start.12 = (bf16[384,256]{1,0:T(8,128)(2,1)S(1)}, bf16[384,256]{1,0:T(8,128)(2,1)S(1)}, u32[]{:S(2)}, u32[]{:S(2)}) collective-permute-start(bf16[384,256]{1,0:T(8,128)(2,1)S(1)} %get-tuple-element.37), channel_id=1, source_target_pairs={{0,8},{1,9},{2,10},{3,11},{4,12},{5,13},{6,14},{7,15},{8,0},{9,1},... | collective-permute-start | bytes 589832 | tf_op jit(solution)/shard_map/ppermute | solution.py:390
  36.1 14.4 %collective-permute-start.13 = (bf16[384,256]{1,0:T(8,128)(2,1)S(1)}, bf16[384,256]{1,0:T(8,128)(2,1)S(1)}, u32[]{:S(2)}, u32[]{:S(2)}) collective-permute-start(bf16[384,256]{1,0:T(8,128)(2,1)S(1)} %get-tuple-element.37), channel_id=1, source_target_pairs={{0,12},{1,13},{2,14},{3,15},{4,0},{5,1},{6,2},{7,3},{8,4},{9,5},{1... | collective-permute-start | bytes 589832 | tf_op jit(solution)/shard_map/ppermute | solution.py:390
  51.3 2.1 %collective-permute-start.17 = (bf16[512,256]{1,0:T(8,128)(2,1)S(1)}, bf16[512,256]{1,0:T(8,128)(2,1)S(1)}, u32[]{:S(2)}, u32[]{:S(2)}) collective-permute-start(bf16[512,256]{1,0:T(8,128)(2,1)S(1)} %get-tuple-element.47), channel_id=1, source_target_pairs={{0,1},{1,0},{2,3},{3,2},{4,5},{5,4},{6,7},{7,6},{8,9},{9,8},{10,11... | collective-permute-start | bytes 786440 | tf_op jit(solution)/shard_map/ppermute | solution.py:390
  54.2 24.7 %all-to-all-start = ((bf16[32,16,256]{2,1,0:T(8,128)(2,1)}), bf16[32,16,256]{2,1,0:T(8,128)(2,1)S(1)}, u32[]{:S(2)}, u32[]{:S(2)}) async-start(bf16[32,16,256]{2,1,0:T(8,128)(2,1)} %bitcast.9), calls=%async_computation | async-start | bytes 524288 | tf_op jit(solution)/shard_map/all_to_all | solution.py:434
  65.2 12.1 %collective-permute-start.10 = (bf16[128,512]{1,0:T(8,128)(2,1)S(1)}, bf16[128,512]{1,0:T(8,128)(2,1)S(1)}, u32[]{:S(2)}, u32[]{:S(2)}) collective-permute-start(bf16[128,512]{1,0:T(8,128)(2,1)S(1)} %get-tuple-element.35), channel_id=1, source_target_pairs={{0,3},{1,2},{2,1},{3,0},{4,7},{5,6},{6,5},{7,4},{8,11},{9,10},{10,... | collective-permute-start | bytes 393224 | tf_op jit(solution)/shard_map/ppermute | solution.py:390
  67.4 9.9 %collective-permute-start.8 = (bf16[128,512]{1,0:T(8,128)(2,1)S(1)}, bf16[128,512]{1,0:T(8,128)(2,1)S(1)}, u32[]{:S(2)}, u32[]{:S(2)}) collective-permute-start(bf16[128,512]{1,0:T(8,128)(2,1)S(1)} %get-tuple-element.33), channel_id=1, source_target_pairs={{0,1},{1,0},{2,3},{3,2},{4,5},{5,4},{6,7},{7,6},{8,9},{9,8},{10,11... | collective-permute-start | bytes 393224 | tf_op jit(solution)/shard_map/ppermute | solution.py:390
  67.4 10.6 %collective-permute-start.9 = (bf16[128,512]{1,0:T(8,128)(2,1)S(1)}, bf16[128,512]{1,0:T(8,128)(2,1)S(1)}, u32[]{:S(2)}, u32[]{:S(2)}) collective-permute-start(bf16[128,512]{1,0:T(8,128)(2,1)S(1)} %get-tuple-element.34), channel_id=1, source_target_pairs={{0,2},{1,3},{2,0},{3,1},{4,6},{5,7},{6,4},{7,5},{8,10},{9,11},{10,... | collective-permute-start | bytes 393224 | tf_op jit(solution)/shard_map/ppermute | solution.py:390
